TPU v7x, 32 devices: a whole 2x2x4 slice. The times are simulated.
32 devices in a mesh: row: 2 (over core), col: 4 (over z), kk: 4 (over y, x).
Axes of the slice: x: 2, y: 2, z: 4, core: 2. Of those that a mesh axis runs over, the one named last changes fastest.
Arguments:
- contribution: float32 [32, 256, 16, 512], P('kk', 'row', None, 'col'), may hold values from -6 to 6
- left_panel: float32 [32, 256, 4, 768], P(None, 'row', 'kk', 'col'), may hold values from -6 to 6
- right_panel: float32 [4, 768, 16, 512], P('kk', 'row', None, 'col'), may hold values from -0.109375 to 0.109375
Outputs:
- updated: float32 [32, 256, 16, 512], P('kk', 'row', None, 'col')
All inputs are finite; a program needn't handle non-finite values.
Results may differ from a plain program's by a relative error of at most 0.00005.
Values sent between devices are 32-bit elements; how exact they have to be, the bound alone decides.
No kernel may reach another device: no remote copies, remote signals or barrier semaphores. Data moves between devices by JAX's collectives and lax.ppermute only.
A program may use at most 128 MiB of HBM per device.

v0:
```python
import jax
import jax.numpy as jnp
from jax import lax
from jax.sharding import PartitionSpec as P


def local(contribution, left_panel, right_panel):
    right_rows = lax.all_gather(right_panel, "row", axis=1, tiled=True)
    col_width = contribution.shape[2] * contribution.shape[3]
    exchanged = lax.all_to_all(left_panel, "kk", split_axis=0, concat_axis=2, tiled=True)
    left_full = lax.all_gather(exchanged, "col", axis=3, tiled=True)
    right_full = lax.all_gather(right_rows, "kk", axis=0, tiled=True)
    row_total = left_full.shape[0] * left_full.shape[1]
    left_flat = left_full.reshape(row_total, -1)
    right_flat = right_full.reshape(-1, col_width)
    product = jnp.dot(
        left_flat, right_flat, precision=lax.Precision.HIGHEST, preferred_element_type=jnp.float32
    )
    product = product.reshape(contribution.shape)
    return contribution - product


def solution(mesh):
    placed = (P("kk", "row", None, "col"), P(None, "row", "kk", "col"), P("kk", "row", None, "col"))
    return jax.shard_map(
        local, mesh=mesh, in_specs=placed, out_specs=P("kk", "row", None, "col"), check_vma=False
    )
```

profile of v0, /device:TPU:0, one launch (start us, length us, event | category | flops | bytes accessed | tf_op | source)
XLA Modules:
  0.0 655.1 jit_solution(10757515280889346965)
XLA Ops:
  6.5 0.0 all-gather.5.cloned.1.call-start
  6.5 0.7 all-gather.5.cloned.1.call-update
  7.3 0.0 all-gather.9.cloned.1.call-start
  7.3 41.9 %all_to_all.18 = f32[32,128,1,192]{1,3,2,0:T(8,128)S(1)} all-to-all(f32[32,128,1,192]{1,3,2,0:T(8,128)} %param.4), channel_id=1, replica_groups=mesh['row'=2,'col'=4,'kk'=4] {'kk'}, dimensions={0} | all-to-all | bytes 6291456 | tf_op jit(solution)/shard_map/all_to_all | solution.py:10
  49.2 3.5 copy.21
  52.6 0.0 all-gather.9.cloned.1.call-update
  52.7 0.0 all-gather.7.cloned.1.call-start
  52.7 0.0 all-gather.5.cloned.1.call-done
  52.7 0.7 all-gather.7.cloned.1.call-update
  53.4 217.5 %all-gather.9.cloned.1.call-done = f32[8,128,4,1,768]{1,0,3,2,4:T(8,128)} async-done(((f32[8,128,4,1,192]{1,0,3,2,4:T(8,128)}), f32[8,128,4,1,768]{1,0,3,2,4:T(8,128)}) %all-gather.9.cloned.1.call-update) | async-done | bytes 12582928 | tf_op jit(solution)/shard_map/all_gather | solution.py:11
  270.9 14.2 %copy.9 = f32[8,128,4,1,768]{4,2,1,0,3:T(4,128)} copy(f32[8,128,4,1,768]{1,0,3,2,4:T(8,128)} %all-gather.9.cloned.1.call-done) | data formatting | bytes 25165824 | tf_op jit(solution)/shard_map/all_gather | solution.py:11
  285.1 16.0 %reshape.11 = f32[8,128,3072,1]{2,1,0,3:T(8,128)} reshape(f32[8,128,4,1,768]{4,2,1,0,3:T(4,128)} %copy.9) | data formatting | bytes 25165824 | tf_op jit(solution)/shard_map/dot_general | solution.py:16
  301.1 197.5 %all-gather.7.cloned.1.call-done = f32[4,768,16,128]{3,2,1,0:T(8,128)} async-done(((f32[1,768,16,128]{3,2,1,0:T(8,128)}), f32[4,768,16,128]{3,2,1,0:T(8,128)}) %all-gather.7.cloned.1.call-update) | async-done | bytes 25165840 | tf_op jit(solution)/shard_map/all_gather | solution.py:12
  498.6 22.8 %copy.20 = f32[384,8,16,128]{3,1,2,0:T(8,128)} copy(f32[384,8,16,128]{3,2,1,0:T(8,128)} %bitcast.26) | data formatting | bytes 50331648
  521.4 24.8 %copy.12 = f32[3072,2048]{0,1:T(8,128)} copy(f32[3072,2048]{1,0:T(8,128)} %bitcast.25) | data formatting | bytes 50331648 | tf_op jit(solution)/shard_map/reshape | solution.py:15
  546.2 90.9 %copy_subtract_fusion = f32[8,128,16,128]{3,1,2,0:T(8,128)} fusion(f32[8,128,16,128]{3,2,1,0:T(8,128)} %param.3, f32[16,128,3072,1]{2,1,0,3:T(8,128)} %bitcast.27, f32[8,128,3072,1]{2,1,0,3:T(8,128)} %reshape.11), kind=kOutput, calls=%fused_computation.3 | convolution fusion | flops 77311508480 | bytes 54525952 | tf_op jit(solution)/shard_map/dot_general | solution.py:16
  637.0 11.5 %copy.14 = f32[8,128,16,128]{3,2,1,0:T(8,128)} copy(f32[8,128,16,128]{3,1,2,0:T(8,128)} %copy_subtract_fusion) | data formatting | bytes 16777216 | tf_op jit(solution)/shard_map/sub | solution.py:20
Async XLA Ops:
  6.5 46.2 %all-gather.5.cloned.1.call-start = ((), (), s32[]{:S(2)}) async-start(), calls=%async_computation.1 | async-start | bytes 9437184 | tf_op jit(solution)/shard_map/all_gather | solution.py:8
  7.3 263.7 %all-gather.9.cloned.1.call-start = ((), (), s32[]{:S(2)}) async-start(), calls=%async_computation.3 | async-start | bytes 15728640 | tf_op jit(solution)/shard_map/all_gather | solution.py:11
  52.7 445.9 %all-gather.7.cloned.1.call-start = ((), (), s32[]{:S(2)}) async-start(), calls=%async_computation.2 | async-start | bytes 31457280 | tf_op jit(solution)/shard_map/all_gather | solution.py:12
Sparse Core Ops, SparseCore 0:
  8.9 19.4 all-gather.4
  52.8 218.0 all-gather.8
  272.8 225.7 all-gather.6
where the time goes:
time: 656 us; the launch traced here: 655 us
  waiting for transfers between devices  416 us (63%)
  local copies, waits for them, and re-layouts  92.8 us (14%)
  matrix products  90.9 us (14%)
  blocking collectives  41.9 us (6%)
  between operations  13.1 us (2%)
    all_gather x1, waiting for transfers between devices, local(): left_full = lax.all_gather(exchanged, 'col', axis=3, tiled=True)  218 us
    all_gather x1, waiting for transfers between devices, local(): right_full = lax.all_gather(right_rows, 'kk', axis=0, tiled=True)  197 us
    dot_general x1, matrix products, local(): jnp.dot(left_flat, right_flat, precision=lax.Precision.HIGHEST, preferred...  90.9 us
    all_to_all x1, blocking collectives, local(): lax.all_to_all(left_panel, 'kk', split_axis=0, concat_axis=2, tiled=True)  41.9 us
    reshape x1, local copies, waits for them, and re-layouts, local(): right_flat = right_full.reshape(-1, col_width)  24.8 us
    unnamed x1, local copies, waits for them, and re-layouts  22.8 us
    dot_general x1, local copies, waits for them, and re-layouts, local(): jnp.dot(left_flat, right_flat, precision=lax.Precision.HIGHEST, preferred...  16 us
    all_gather x1, local copies, waits for them, and re-layouts, local(): left_full = lax.all_gather(exchanged, 'col', axis=3, tiled=True)  14.2 us
  transfers between devices with their start and end apart: 3, of which 2 were waited for; matrix products, arithmetic and copies ran while one was open for 5% of the time, Pallas kernels for 0%

commit v1 on v0

v1 whole, which is shorter than its diff:
```python
import functools

import jax
import jax.numpy as jnp
from jax import lax
from jax.experimental import pallas as pl
from jax.experimental.pallas import tpu as pltpu
from jax.sharding import PartitionSpec as P


LANES = 128
VMEM_LIMIT = 16 * 1024 * 1024


def split(value):
    high = value.astype(jnp.bfloat16)
    return high, (value - high.astype(jnp.float32)).astype(jnp.bfloat16)


def product(left_high, left_low, right_high, right_low):
    dot = functools.partial(jnp.dot, preferred_element_type=jnp.float32)
    return dot(left_high, right_high) + (dot(left_high, right_low) + dot(left_low, right_high))


def fetch(slot, flag, first, buffer, sem):
    count = buffer.shape[0]
    copies = []
    for ref, skip in zip(slot, first):
        copies.append(pltpu.make_async_copy(ref.at[pl.ds(skip, count)], buffer, sem))
    if len(copies) == 1:
        copies[0].start()
    else:
        pl.when(flag != 0)(copies[0].start)
        pl.when(flag == 0)(copies[1].start)
    return copies[0]


def add_kernel(counts, pieces, keep, scalars, acc_ref, *refs):
    right, refs = refs[:pieces], refs[pieces:]
    slots = []
    for count in counts:
        slots.append(refs[:count])
        refs = refs[count:]
    out_ref, right_high, right_low, buffers, sems, turned, left_high, left_low = refs
    width, rows = slots[0][0].shape[1:]
    row_blocks = buffers.shape[1]
    cut = right[0].shape[1]
    step = pl.program_id(0)
    lanes = pl.ds(pl.multiple_of(step * cut, cut), cut)
    mine = lanes if keep else slice(None)

    def copies(start):
        for index, slot in enumerate(slots):
            if start:
                fetch(slot, scalars[2 * index + 1], (0, 0), buffers.at[index], sems.at[index])
            else:
                pltpu.make_async_copy(slot[0].at[pl.ds(0, row_blocks)], buffers.at[index], sems.at[index]).wait()

    @pl.when(step == 0)
    def _():
        copies(True)
        turned[...] = jnp.zeros_like(turned)

    at = 0
    for piece in right:
        high, low = split(piece[...])
        right_high[at : at + piece.shape[0], mine] = high
        right_low[at : at + piece.shape[0], mine] = low
        at += piece.shape[0]

    @pl.when(step == 0)
    def _():
        copies(False)

        def one(block, carry):
            for index in range(len(slots)):
                at = pl.multiple_of(scalars[2 * index] * width, width)
                turned[pl.ds(at, width), :] = buffers[index, block]
            high, low = split(turned[...].T)
            at = pl.multiple_of(block * rows, rows)
            left_high[pl.ds(at, rows), :] = high
            left_low[pl.ds(at, rows), :] = low
            return carry

        lax.fori_loop(0, row_blocks, one, 0)

    out_ref[:, lanes] = acc_ref[:, lanes] - product(
        left_high[...], left_low[...], right_high[:, mine], right_low[:, mine]
    )


def add(acc, slots, scalars, right, keep):
    rows, cols = acc.shape
    depth = sum(piece.shape[0] for piece in right)
    flat = [array for slot in slots for array in slot]
    cut = min(cols, 2 * LANES)
    resident = pl.BlockSpec(memory_space=pltpu.VMEM)
    used = len(slots) * flat[0].shape[1]
    shape = jax.ShapeDtypeStruct((depth, cols), jnp.bfloat16)
    terms = [pltpu.VMEM((depth, cut), jnp.bfloat16)] * 2
    return pl.pallas_call(
        functools.partial(add_kernel, [len(slot) for slot in slots], len(right), keep),
        out_shape=[jax.ShapeDtypeStruct(acc.shape, acc.dtype)] + [shape, shape] * keep,
        grid_spec=pltpu.PrefetchScalarGridSpec(
            num_scalar_prefetch=1,
            grid=(cols // cut,),
            in_specs=[resident]
            + [pl.BlockSpec((piece.shape[0], cut), lambda i, s: (0, i)) for piece in right]
            + [pl.BlockSpec(memory_space=pl.ANY)] * len(flat),
            out_specs=[resident] + [resident] * (2 * keep),
            scratch_shapes=terms * (not keep)
            + [
                pltpu.VMEM((len(slots),) + flat[0].shape, jnp.float32),
                pltpu.SemaphoreType.DMA((len(slots),)),
                pltpu.VMEM((depth, flat[0].shape[2]), jnp.float32),
                pltpu.VMEM((rows, depth), jnp.bfloat16),
                pltpu.VMEM((rows, depth), jnp.bfloat16),
            ],
        ),
        input_output_aliases={1: 0},
        compiler_params=pltpu.CompilerParams(vmem_limit_bytes=VMEM_LIMIT),
        cost_estimate=pl.CostEstimate(
            flops=6 * rows * used * cols, bytes_accessed=4 * depth * cols, transcendentals=0
        ),
        name="add",
    )(scalars, acc, *right, *flat)


def fold_kernel(blocks, x_ref, acc_ref):
    rows = x_ref.shape[0] // blocks
    mine = pl.ds(pl.multiple_of(pl.program_id(0) * rows, rows), rows)
    for block in range(blocks):
        acc_ref[mine, block * LANES : (block + 1) * LANES] = x_ref[pl.ds(block, rows, stride=blocks), :]


def fold(front):
    row_blocks, height, blocks, lanes = front.shape
    rows, cols = row_blocks * height, blocks * lanes
    return pl.pallas_call(
        functools.partial(fold_kernel, blocks),
        out_shape=jax.ShapeDtypeStruct((rows, cols), front.dtype),
        grid=(row_blocks,),
        in_specs=[pl.BlockSpec((height * blocks, lanes), lambda i: (i, 0))],
        out_specs=pl.BlockSpec(memory_space=pltpu.VMEM),
        compiler_params=pltpu.CompilerParams(vmem_limit_bytes=VMEM_LIMIT),
        cost_estimate=pl.CostEstimate(flops=0, bytes_accessed=4 * front.size, transcendentals=0),
        name="fold",
    )(front.reshape(rows * blocks, lanes))


def one_kernel(count, scalars, acc_ref, high_ref, low_ref, *refs):
    slot = refs[:count]
    out_ref, buffer, sem, left_high, left_low = refs[count:]
    row_blocks, width, height = buffer.shape
    cut = acc_ref.shape[1] // pl.num_programs(0)
    step = pl.program_id(0)

    @pl.when(step == 0)
    def _():
        fetch(slot, scalars[1], (0, 0), buffer, sem).wait()
        for block in range(row_blocks):
            high, low = split(buffer[block].T)
            left_high[block * height : (block + 1) * height, :] = high
            left_low[block * height : (block + 1) * height, :] = low

    pivots = pl.ds(pl.multiple_of(scalars[0] * width, width), width)
    lanes = pl.ds(pl.multiple_of(step * cut, cut), cut)
    out_ref[:, lanes] = acc_ref[:, lanes] - product(
        left_high[...], left_low[...], high_ref[pivots, lanes], low_ref[pivots, lanes]
    )


def one(acc, slot, scalars, right):
    rows, cols = acc.shape
    width = slot[0].shape[1]
    cut = min(cols, 2 * LANES)
    resident = pl.BlockSpec(memory_space=pltpu.VMEM)
    return pl.pallas_call(
        functools.partial(one_kernel, len(slot)),
        out_shape=jax.ShapeDtypeStruct(acc.shape, acc.dtype),
        grid_spec=pltpu.PrefetchScalarGridSpec(
            num_scalar_prefetch=1,
            grid=(cols // cut,),
            in_specs=[resident] * 3 + [pl.BlockSpec(memory_space=pl.ANY)] * len(slot),
            out_specs=resident,
            scratch_shapes=[
                pltpu.VMEM(slot[0].shape, jnp.float32),
                pltpu.SemaphoreType.DMA,
                pltpu.VMEM((rows, width), jnp.bfloat16),
                pltpu.VMEM((rows, width), jnp.bfloat16),
            ],
        ),
        input_output_aliases={1: 0},
        compiler_params=pltpu.CompilerParams(vmem_limit_bytes=VMEM_LIMIT),
        cost_estimate=pl.CostEstimate(flops=6 * rows * width * cols, bytes_accessed=4 * slot[0].size, transcendentals=0),
        name="one",
    )(scalars, acc, right[0], right[1], *slot)


def last_kernel(blocks, count, first, base, scalars, acc_ref, high_ref, low_ref, *refs):
    slot = refs[:count]
    out_ref, _, buffer, sem = refs[-4:]
    _, width, height = buffer.shape
    rows = out_ref.shape[0] // blocks
    row_blocks = rows // height
    step = pl.program_id(0)

    @pl.when(step == 0)
    def _():
        fetch(slot, scalars[1], first, buffer, sem).wait()

    parts = [split(buffer[step * row_blocks + block].T) for block in range(row_blocks)]
    left_high = jnp.concatenate([part[0] for part in parts], axis=0)
    left_low = jnp.concatenate([part[1] for part in parts], axis=0)
    pivots = pl.ds(pl.multiple_of(scalars[0] * width, width), width)
    mine = pl.ds(pl.multiple_of(base + step * rows, rows), rows)
    pair = min(blocks, 2)
    for block in range(0, blocks, pair):
        lanes = pl.ds(block * LANES, pair * LANES)
        value = acc_ref[mine, lanes] - product(left_high, left_low, high_ref[pivots, lanes], low_ref[pivots, lanes])
        for one in range(pair):
            out_ref[pl.ds(block + one, rows, stride=blocks), :] = value[:, one * LANES : (one + 1) * LANES]


def last(acc, slot, first, scalars, right, blocks, first_block, row_blocks, buffer):
    rows, cols = acc.shape
    width, height = slot[0].shape[1:]
    step = 2 if row_blocks % 2 == 0 else 1
    base = first_block // step
    buffers = () if buffer is None else (buffer,)
    resident = pl.BlockSpec(memory_space=pltpu.VMEM)
    return pl.pallas_call(
        functools.partial(last_kernel, blocks, len(slot), first, first_block * height),
        out_shape=[
            jax.ShapeDtypeStruct((rows * blocks, LANES), acc.dtype),
            jax.ShapeDtypeStruct(acc.shape, acc.dtype),
        ],
        grid_spec=pltpu.PrefetchScalarGridSpec(
            num_scalar_prefetch=1,
            grid=(row_blocks // step,),
            in_specs=[resident] * 3 + [pl.BlockSpec(memory_space=pl.ANY)] * (len(slot) + len(buffers)),
            out_specs=[pl.BlockSpec((step * height * blocks, LANES), lambda i, s: (base + i, 0)), resident],
            scratch_shapes=[
                pltpu.VMEM((row_blocks, width, height), jnp.float32),
                pltpu.SemaphoreType.DMA,
            ],
        ),
        input_output_aliases={1: 1, 4 + len(slot): 0} if buffers else {1: 1},
        compiler_params=pltpu.CompilerParams(vmem_limit_bytes=VMEM_LIMIT),
        cost_estimate=pl.CostEstimate(
            flops=6 * row_blocks * height * width * cols, bytes_accessed=4 * row_blocks * height * cols, transcendentals=0
        ),
        name="last",
    )(scalars, acc, right[0], right[1], *slot, *buffers)


def moves(count):
    power = count & (count - 1) == 0
    pairs = lambda m: [(i, i ^ m if power else (i + m) % count) for i in range(count)]
    source = lambda me, m: me ^ m if power else lax.rem(me + count - m, count)
    target = lambda me, m: me ^ m if power else lax.rem(me + m, count)
    return power, pairs, source, target


def line(piece, axis, count, tails):
    mate = lambda i, odd: i + 1 if i % 2 == odd else i - 1
    reach = lambda i, odd: count - 1 - i if i % 2 == odd else i
    streams = {0: [], 1: []}
    for step in range(1, count):
        new = {}
        for odd in (0, 1):
            pairs = [(mate(i, odd), i) for i in range(count) if reach(i, odd) >= step]
            if pairs:
                what = piece if step == 1 else streams[1 - odd][step - 2]
                if tails > 1 and odd == 0 and step == count - 1:
                    cut = what.shape[0] // tails
                    new[odd] = [lax.ppermute(what[n * cut : (n + 1) * cut], axis, pairs) for n in range(tails)]
                else:
                    new[odd] = lax.ppermute(what, axis, pairs)
        for odd, value in new.items():
            streams[odd].append(value)
    return streams


def local(sizes, contribution, left_panel, right_panel):
    n_row, n_col, n_kk = sizes["row"], sizes["col"], sizes["kk"]
    row, col, kk = lax.axis_index("row"), lax.axis_index("col"), lax.axis_index("kk")
    row_blocks, height, blocks, lanes = contribution.shape
    cols = blocks * lanes
    width = left_panel.shape[3]
    depth = right_panel.shape[1]
    quarter = depth * n_row
    order = sorted(range(n_kk), key=lambda m: (bin(m).count("1"), m))

    power, pairs, _, target = moves(n_kk)
    left = left_panel.transpose(0, 2, 3, 1).reshape(n_kk, row_blocks, width, height)
    group = lambda index: lax.dynamic_index_in_dim(left, index, 0, keepdims=False)
    pieces = [group(kk) if m == 0 else lax.ppermute(group(target(kk, m)), "kk", pairs(m)) for m in order]

    tails = 2 if row_blocks % 2 == 0 and n_col > 2 else 1
    streams = [line(piece, "col", n_col, tails if i == n_kk - 1 else 0) for i, piece in enumerate(pieces)]
    even = col % 2 == 0
    length = jnp.where(even, n_col - 1 - col, col)
    lengths = sorted({n_col - 1 - i if i % 2 == 0 else i for i in range(n_col)})

    def slot_of(piece, stream, index):
        if index == 0:
            return (piece,)
        near, far = stream[0], stream[1]
        options = [(reach, far[index - 1 - reach]) for reach in lengths if index > reach]
        if not options:
            return (near[index - 1],)
        value = options[-1][1]
        for reach, other in options[:-1]:
            value = jnp.where(length == reach, other, value)
        return (near[index - 1], value) if index <= lengths[-1] else (value,)

    def scalars_of(index):
        if index == 0:
            return [col, jnp.int32(1)]
        past = index - length
        by_near = jnp.where(even, col + index, col - index)
        by_far = jnp.where(even, col - past, col + past)
        is_near = index <= length
        return [jnp.where(is_near, by_near, by_far), is_near.astype(jnp.int32)]

    own = right_panel.reshape(depth, cols)
    parts = {0: [own]}
    for m in order:
        bits = [1 << b for b in range(n_kk.bit_length()) if m >> b & 1]
        if m == 0:
            continue
        if not power or len(bits) == 1:
            parts[m] = [lax.ppermute(own, "kk", pairs(m))]
        else:
            half = depth // 2
            whole = lambda piece: piece[0] if len(piece) == 1 else jnp.concatenate(piece, axis=0)
            first = lax.ppermute(whole(parts[m ^ bits[0]])[:half], "kk", pairs(bits[0]))
            second = lax.ppermute(whole(parts[m ^ bits[-1]])[half:], "kk", pairs(bits[-1]))
            parts[m] = [first, second]

    row_power, row_pairs, row_source, _ = moves(n_row)
    rights = []
    for i, m in enumerate(order):
        rights.append(list(parts[m]))
        for j in range(1, n_row):
            rights[i] += [lax.ppermute(part, "row", row_pairs(j)) for part in parts[m]]
    if depth % width == 0:
        per = depth // width

        def place(shard):
            rank = shard // per
            return (rank ^ row if row_power else lax.rem(row - rank + n_row, n_row)) * per + lax.rem(shard, per)

    else:
        place = lambda shard: shard
        for i, right in enumerate(rights):
            count = len(right) // n_row
            total = jnp.zeros((quarter, cols), jnp.float32)
            for j in range(n_row):
                piece = jnp.concatenate(right[j * count : (j + 1) * count], axis=0)
                rank = row if j == 0 else row_source(row, j)
                total = lax.dynamic_update_slice_in_dim(total, piece, rank * depth, 0)
            rights[i] = [total]

    scalars = []
    for index in range(n_col):
        shard, flag = scalars_of(index)
        scalars += [place(shard), flag]
    scalars = jnp.stack(scalars).astype(jnp.int32)

    acc = fold(contribution)
    final = n_kk - 1
    early = max(n_col - 2, 1)
    for i in [*range(final - 1), final, final - 1]:
        slots = [slot_of(pieces[i], streams[i], index) for index in range(early if i == final else n_col)]
        acc, *terms = add(acc, slots, scalars, rights[i], i == final)
        if terms:
            kept = terms
    for index in range(early, n_col - 1):
        slot = slot_of(pieces[final], streams[final], index)
        acc = one(acc, slot, scalars[2 * index : 2 * index + 2], kept)

    cut = row_blocks // tails
    out = None
    for part in range(tails):
        stream = {0: list(streams[final][0]), 1: streams[final][1]}
        stream[0][-1] = stream[0][-1][part] if isinstance(stream[0][-1], list) else stream[0][-1]
        options = slot_of(pieces[final], stream, n_col - 1)
        first = [0 if option.shape[0] == cut else part * cut for option in options]
        out, acc = last(acc, options, first, scalars[-2:], kept, blocks, part * cut, cut, out)
    return out.reshape(contribution.shape)


def solution(mesh):
    placed = (P("kk", "row", None, "col"), P(None, "row", "kk", "col"), P("kk", "row", None, "col"))

    def body(*args):
        return local(dict(mesh.shape), *args)

    return jax.shard_map(
        body, mesh=mesh, in_specs=placed, out_specs=P("kk", "row", None, "col"), check_vma=False
    )
```

time: 656 us -> 283 us (0.43)
  waiting for transfers between devices: 416 us -> 127 us
  matrix products: 90.9 us -> 0 us
  Pallas kernels: 0 us -> 83.4 us
  local copies, waits for them, and re-layouts: 92.8 us -> 33.1 us
  blocking collectives: 41.9 us -> 0 us
  starting transfers between devices: 0.08 us -> 37.4 us
  between operations: 13.1 us -> 0.83 us
    all_gather x3 -> x0, waiting for transfers between devices: 415 us -> none  [the longest x1 218 us: local(): left_full = lax.all_gather(exchanged, 'col', axis=3, tiled=True)]
    ppermute x0 -> x33, waiting for transfers between devices: none -> 127 us  [the longest x19 84.5 us: line(): new[odd] = lax.ppermute(what, axis, pairs)]
    dot_general x1 -> x0, matrix products: 90.9 us -> none  [local(): jnp.dot(left_flat, right_flat, precision=lax.Precision.HIGHEST, preferred...]
    pallas_call x0 -> x8, Pallas kernels: none -> 83.4 us  [the longest x4 64.7 us: add(): pl.pallas_call(functools.partial(add_kernel, [len(slot) for slot in slots...]
    all_to_all x1 -> x0, blocking collectives: 41.9 us -> none  [local(): lax.all_to_all(left_panel, 'kk', split_axis=0, concat_axis=2, tiled=True)]
    ppermute x0 -> x33, starting transfers between devices: none -> 37.4 us  [the longest x19 25.6 us: line(): new[odd] = lax.ppermute(what, axis, pairs)]
    reshape x1 -> x0, local copies, waits for them, and re-layouts: 24.8 us -> none  [local(): right_flat = right_full.reshape(-1, col_width)]
    dot_general x1 -> x0, local copies, waits for them, and re-layouts: 16 us -> none  [local(): jnp.dot(left_flat, right_flat, precision=lax.Precision.HIGHEST, preferred...]
  transfers between devices with their start and end apart: 3 -> 33, of which waited for: 2 -> 13; matrix products, arithmetic and copies ran while one was open for 5% -> 3% of each run, Pallas kernels for 0% -> 28%
where the time goes in v1:
time: 283 us; the launch traced here: 282 us
  waiting for transfers between devices  127 us (45%)
  Pallas kernels  83.4 us (29%)
  starting transfers between devices  37.4 us (13%)
  local copies, waits for them, and re-layouts  33.1 us (12%)
    ppermute x19, waiting for transfers between devices, line(): new[odd] = lax.ppermute(what, axis, pairs)  84.5 us
    pallas_call x4, Pallas kernels, add(): pl.pallas_call(functools.partial(add_kernel, [len(slot) for slot in slots...  64.7 us
    ppermute x19, starting transfers between devices, line(): new[odd] = lax.ppermute(what, axis, pairs)  25.6 us
    unnamed x69, local copies, waits for them, and re-layouts  25.3 us
    ppermute x1, waiting for transfers between devices, local(): first = lax.ppermute(whole(parts[m ^ bits[0]])[:half], 'kk', pairs(bits[0]))  20.9 us
    ppermute x3, waiting for transfers between devices, local(): lax.ppermute(group(target(kk, m)), 'kk', pairs(m))  14.6 us
    pallas_call x2, Pallas kernels, last(): pl.pallas_call(functools.partial(last_kernel, blocks, len(slot), first, f...  10.1 us
    pallas_call x1, Pallas kernels, one(): pl.pallas_call(functools.partial(one_kernel, len(slot)), out_shape=jax.Sh...  5.76 us
  transfers between devices with their start and end apart: 33, of which 13 were waited for; matrix products, arithmetic and copies ran while one was open for 3% of the time, Pallas kernels for 28%

profile of v1, /device:TPU:0, one launch (start us, length us, event | category | flops | bytes accessed | tf_op | source)
XLA Modules:
  0.0 281.6 jit_solution(2128842003301396355)
XLA Ops:
  0.0 2.2 dynamic-slice_bitcast_fusion
  2.2 3.1 %collective-permute-start.1 = (f32[8,192,128]{2,1,0:T(8,128)S(1)}, f32[8,192,128]{2,1,0:T(8,128)S(1)}, u32[]{:S(2)}, u32[]{:S(2)}) collective-permute-start(f32[8,192,128]{2,1,0:T(8,128)S(1)} %get-tuple-element.20.refs_2_), channel_id=1, source_target_pairs={{4,0},{0,4},{12,8},{8,12},{5,1},{1,5},{13,9},{9,13},{6,2},{2,6},{1... | collective-permute-start | bytes 2359304 | tf_op jit(solution)/shard_map/ppermute | solution.py:279
  6.1 1.6 collective-permute-start.8
  7.6 1.5 collective-permute-start.19
  9.6 13.3 %collective-permute-done.1.refs_3_ = f32[8,192,128]{2,1,0:T(8,128)S(1)} collective-permute-done((f32[8,192,128]{2,1,0:T(8,128)S(1)}, f32[8,192,128]{2,1,0:T(8,128)S(1)}, u32[]{:S(2)}, u32[]{:S(2)}) %collective-permute-start.1) | collective-permute-done | bytes 786464 | tf_op jit(solution)/shard_map/ppermute | solution.py:279
  22.9 0.7 collective-permute-start.4
  23.6 1.3 collective-permute-start.3
  24.9 3.1 %copy.14 = f32[48,8,16,128]{3,1,2,0:T(8,128)} copy(f32[48,8,16,128]{3,2,1,0:T(8,128)S(1)} %bitcast.27) | data formatting | bytes 6291456
  28.1 1.7 collective-permute-start.6
  29.8 14.6 %collective-permute-done.19.refs_4_ = f32[8,192,128]{2,1,0:T(8,128)S(1)} collective-permute-done((f32[8,192,128]{2,1,0:T(8,128)S(1)}, f32[8,192,128]{2,1,0:T(8,128)S(1)}, u32[]{:S(2)}, u32[]{:S(2)}) %collective-permute-start.19) | collective-permute-done | bytes 786464 | tf_op jit(solution)/shard_map/ppermute | solution.py:298
  44.9 4.4 %collective-permute-start.9 = (f32[8,192,128]{2,1,0:T(8,128)S(1)}, f32[8,192,128]{2,1,0:T(8,128)S(1)}, u32[]{:S(2)}, u32[]{:S(2)}) collective-permute-start(f32[8,192,128]{2,1,0:T(8,128)S(1)} %collective-permute-done.8.refs_2_), channel_id=1, source_target_pairs={{4,0},{0,4},{12,8},{8,12},{5,1},{1,5},{13,9},{9,13},{6,2},{2,6},{1... | collective-permute-start | bytes 2359304 | tf_op jit(solution)/shard_map/ppermute | solution.py:279
  49.3 0.7 collective-permute-start.10
  50.0 0.9 copy-done.5
  50.9 0.9 copy-done.19
  51.8 1.2 collective-permute-start.20
  53.0 14.6 %collective-permute-done.9.refs_3_ = f32[8,192,128]{2,1,0:T(8,128)S(1)} collective-permute-done((f32[8,192,128]{2,1,0:T(8,128)S(1)}, f32[8,192,128]{2,1,0:T(8,128)S(1)}, u32[]{:S(2)}, u32[]{:S(2)}) %collective-permute-start.9) | collective-permute-done | bytes 786464 | tf_op jit(solution)/shard_map/ppermute | solution.py:279
  67.6 2.0 collective-permute-start.23
  69.7 0.7 collective-permute-start.24
  70.4 14.1 %collective-permute-done.20.refs_5_ = f32[8,192,128]{2,1,0:T(8,128)S(1)} collective-permute-done((f32[8,192,128]{2,1,0:T(8,128)S(1)}, f32[8,192,128]{2,1,0:T(8,128)S(1)}, u32[]{:S(2)}, u32[]{:S(2)}) %collective-permute-start.20) | collective-permute-done | bytes 786464 | tf_op jit(solution)/shard_map/ppermute | solution.py:279
  84.5 0.7 collective-permute-start.28
  85.2 11.9 %collective-permute-done.23.refs_3_ = f32[8,192,128]{2,1,0:T(8,128)S(1)} collective-permute-done((f32[8,192,128]{2,1,0:T(8,128)S(1)}, f32[8,192,128]{2,1,0:T(8,128)S(1)}, u32[]{:S(2)}, u32[]{:S(2)}) %collective-permute-start.23) | collective-permute-done | bytes 786464 | tf_op jit(solution)/shard_map/ppermute | solution.py:279
  97.1 1.3 collective-permute-start.5
  98.4 0.9 copy-done.17
  99.3 0.7 collective-permute-start.12
  100.0 0.9 copy-done.21
  100.9 18.0 %collective-permute-done.5.refs_6_ = f32[8,192,128]{2,1,0:T(8,128)S(1)} collective-permute-done((f32[8,192,128]{2,1,0:T(8,128)S(1)}, f32[8,192,128]{2,1,0:T(8,128)S(1)}, u32[]{:S(2)}, u32[]{:S(2)}) %collective-permute-start.5) | collective-permute-done | bytes 786464 | tf_op jit(solution)/shard_map/ppermute | solution.py:279
  119.0 0.9 copy-done.31
  119.8 1.3 collective-permute-start.11
  121.1 0.9 copy-done.23
  122.0 0.7 collective-permute-start.26
  122.8 0.7 collective-permute-start.30
  123.6 2.7 slice.22
  126.3 2.8 slice.21
  129.1 11.7 %collective-permute-done.11.refs_4_ = f32[8,192,128]{2,1,0:T(8,128)S(1)} collective-permute-done((f32[8,192,128]{2,1,0:T(8,128)S(1)}, f32[8,192,128]{2,1,0:T(8,128)S(1)}, u32[]{:S(2)}, u32[]{:S(2)}) %collective-permute-start.11) | collective-permute-done | bytes 786464 | tf_op jit(solution)/shard_map/ppermute | solution.py:279
  140.8 0.9 copy-done.29
  141.7 1.5 collective-permute-start.15
  143.2 1.5 collective-permute-start.16
  144.9 3.4 %copy-done.2 = f32[8,128,16,128]{3,2,1,0:T(8,128)S(1)} copy-done((f32[8,128,16,128]{3,2,1,0:T(8,128)S(1)}, f32[8,128,16,128]{3,2,1,0:T(8,128)}, u32[]{:S(2)}) %copy-start.2) | copy-done | bytes 8388632
  148.3 2.8 fold.1.acc_ref
  151.1 3.4 %copy-done = f32[1024,2048]{1,0:T(8,128)} copy-done((f32[1024,2048]{1,0:T(8,128)}, f32[1024,2048]{1,0:T(8,128)S(1)}, u32[]{:S(2)}) %copy-start) | copy-done | bytes 8388632
  154.8 1.4 collective-permute-start.13
  156.2 20.9 %collective-permute-done.15.refs_0_ = f32[192,2048]{1,0:T(8,128)} collective-permute-done((f32[192,2048]{1,0:T(8,128)}, f32[192,2048]{1,0:T(8,128)}, u32[]{:S(2)}, u32[]{:S(2)}) %collective-permute-start.15) | collective-permute-done | bytes 1572896 | tf_op jit(solution)/shard_map/ppermute | solution.py:338
  177.1 1.2 collective-permute-done.16.refs_1_
  178.3 3.4 %copy-done.1 = f32[1024,2048]{1,0:T(8,128)S(1)} copy-done((f32[1024,2048]{1,0:T(8,128)S(1)}, f32[1024,2048]{1,0:T(8,128)}, u32[]{:S(2)}) %copy-start.1) | copy-done | bytes 8388632
  181.7 1.1 copy-done.8
  182.8 1.1 copy-done.10
  184.0 1.1 copy-done.18
  185.1 1.1 copy-done.20
  186.3 1.1 copy-done.32
  187.4 16.4 %add.77.acc_ref = f32[1024,2048]{1,0:T(8,128)S(1)} custom-call(s32[8]{0:T(128)S(1)} %stack.49.scalars, f32[1024,2048]{1,0:T(8,128)S(1)} %copy-done.1, f32[384,2048]{1,0:T(8,128)} %bitcast.24.refs_0_, f32[384,2048]{1,0:T(8,128)} %collective-permute-done.refs_1_, f32[8,192,128]{2,1,0:T(8,128)S(1)} %get-tuple-element.20.refs_2_, ...), custom_call_target="tpu_custom_call", output_to_operand_aliasing={{}: (1, {})} | custom-call | flops 9663676416 | bytes 6291456 | tf_op jit(solution)/shard_map/add/pallas_call | solution.py:101
  203.8 1.4 collective-permute-start.25
  205.3 1.3 collective-permute-start.27
  206.6 16.1 %add.78.acc_ref = f32[1024,2048]{1,0:T(8,128)S(1)} custom-call(s32[8]{0:T(128)S(1)} %stack.49.scalars, f32[1024,2048]{1,0:T(8,128)S(1)} %add.77.acc_ref, f32[384,2048]{1,0:T(8,128)} %collective-permute-done.6.refs_0_, f32[384,2048]{1,0:T(8,128)} %collective-permute-done.7.refs_1_, f32[8,192,128]{2,1,0:T(8,128)S(1)} %copy-done.6, ...), custom_call_target="tpu_custom_call", output_to_operand_aliasing={{}: (1, {})} | custom-call | flops 9663676416 | bytes 6291456 | tf_op jit(solution)/shard_map/add/pallas_call | solution.py:101
  222.8 1.3 collective-permute-start.29
  224.1 1.4 collective-permute-start.31
  225.6 16.0 %add.79 = (f32[1024,2048]{1,0:T(8,128)S(1)}, bf16[768,2048]{1,0:T(8,128)(2,1)S(1)}, bf16[768,2048]{1,0:T(8,128)(2,1)S(1)}) custom-call(s32[8]{0:T(128)S(1)} %stack.49.scalars, f32[1024,2048]{1,0:T(8,128)S(1)} %add.78.acc_ref, f32[192,2048]{1,0:T(8,128)} %collective-permute-done.15.refs_0_, ...), custom_call_target="tpu_custom_call", output_to_operand_aliasing={{0}: (1, {})} | custom-call | flops 4831838208 | bytes 6291456 | tf_op jit(solution)/shard_map/add/pallas_call | solution.py:101
  241.6 1.5 collective-permute-start.32
  243.1 16.1 %add.80.acc_ref = f32[1024,2048]{1,0:T(8,128)S(1)} custom-call(s32[8]{0:T(128)S(1)} %stack.49.scalars, f32[1024,2048]{1,0:T(8,128)S(1)} %get-tuple-element.11.acc_ref, f32[384,2048]{1,0:T(8,128)} %collective-permute-done.14.refs_0_, f32[384,2048]{1,0:T(8,128)} %collective-permute-done.21.refs_1_, ...), custom_call_target="tpu_custom_call", output_to_operand_aliasing={{}: (1, {})} | custom-call | flops 9663676416 | bytes 6291456 | tf_op jit(solution)/shard_map/add/pallas_call | solution.py:101
  259.3 0.7 collective-permute-done.29.refs_0_
  260.0 5.8 %one.1.acc_ref = f32[1024,2048]{1,0:T(8,128)S(1)} custom-call(s32[2]{0:T(128)S(1)} %pad_add_fusion.1.scalars, f32[1024,2048]{1,0:T(8,128)S(1)} %add.80.acc_ref, bf16[768,2048]{1,0:T(8,128)(2,1)S(1)} %get-tuple-element.12.high_ref, bf16[768,2048]{1,0:T(8,128)(2,1)S(1)} %get-tuple-element.13.low_ref, ...), custom_call_target="tpu_custom_call", output_to_operand_aliasing={{}: (1, {})} | custom-call | flops 2415919104 | bytes 786432 | tf_op jit(solution)/shard_map/one/pallas_call | solution.py:178
  265.8 2.7 collective-permute-done.31.refs_0_
  268.4 5.1 %last.2 = (f32[16384,128]{1,0:T(8,128)}, f32[1024,2048]{1,0:T(8,128)S(1)}) custom-call(s32[2]{0:T(128)S(1)} %pad_add_fusion.scalars, f32[1024,2048]{1,0:T(8,128)S(1)} %one.1.acc_ref, bf16[768,2048]{1,0:T(8,128)(2,1)S(1)} %get-tuple-element.12.high_ref, bf16[768,2048]{1,0:T(8,128)(2,1)S(1)} %get-tuple-element.13.low_ref, ...), custom_call_target="tpu_custom_call", output_to_operand_aliasing={{1}: (1, {})} | custom-call | flops 1207959552 | bytes 4194304 | tf_op jit(solution)/shard_map/last/pallas_call | solution.py:232
  273.5 2.9 %collective-permute-done.32.refs_0_ = f32[4,192,128]{2,1,0:T(8,128)S(1)} collective-permute-done((f32[4,192,128]{2,1,0:T(8,128)S(1)}, f32[4,192,128]{2,1,0:T(8,128)S(1)}, u32[]{:S(2)}, u32[]{:S(2)}) %collective-permute-start.32) | collective-permute-done | bytes 393248 | tf_op jit(solution)/shard_map/ppermute | solution.py:277
  276.4 5.1 %last.3 = (f32[16384,128]{1,0:T(8,128)}, f32[1024,2048]{1,0:T(8,128)S(1)}) custom-call(s32[2]{0:T(128)S(1)} %pad_add_fusion.scalars, f32[1024,2048]{1,0:T(8,128)S(1)} %get-tuple-element.14.acc_ref, bf16[768,2048]{1,0:T(8,128)(2,1)S(1)} %get-tuple-element.12.high_ref, ...), custom_call_target="tpu_custom_call", output_to_operand_aliasing={{1}: (1, {}), {0}: (6, {})} | custom-call | flops 1207959552 | bytes 4194304 | tf_op jit(solution)/shard_map/last/pallas_call | solution.py:232
  (86 shorter events, 2.3 us)
Async XLA Ops:
  0.0 24.9 %copy-start.33 = (f32[1,384,16,128]{3,2,1,0:T(8,128)S(1)}, f32[1,384,16,128]{3,2,1,0:T(8,128)}, u32[]{:S(2)}) copy-start(f32[1,384,16,128]{3,2,1,0:T(8,128)} %param.5) | copy-start | bytes 9437188
  2.2 20.7 %collective-permute-start.1 = (f32[8,192,128]{2,1,0:T(8,128)S(1)}, f32[8,192,128]{2,1,0:T(8,128)S(1)}, u32[]{:S(2)}, u32[]{:S(2)}) collective-permute-start(f32[8,192,128]{2,1,0:T(8,128)S(1)} %get-tuple-element.20.refs_2_), channel_id=1, source_target_pairs={{4,0},{0,4},{12,8},{8,12},{5,1},{1,5},{13,9},{9,13},{6,2},{2,6},{1... | collective-permute-start | bytes 2359304 | tf_op jit(solution)/shard_map/ppermute | solution.py:279
  5.3 18.3 %collective-permute-start.2 = (f32[8,192,128]{2,1,0:T(8,128)S(1)}, f32[8,192,128]{2,1,0:T(8,128)S(1)}, u32[]{:S(2)}, u32[]{:S(2)}) collective-permute-start(f32[8,192,128]{2,1,0:T(8,128)S(1)} %get-tuple-element.20.refs_2_), channel_id=1, source_target_pairs={{8,4},{4,8},{9,5},{5,9},{10,6},{6,10},{11,7},{7,11},{24,20},{20,24... | collective-permute-start | bytes 2359304 | tf_op jit(solution)/shard_map/ppermute | solution.py:279
  6.1 22.0 %collective-permute-start.8 = (f32[8,192,128]{2,1,0:T(8,128)S(1)}, f32[8,192,128]{2,1,0:T(8,128)S(1)}, u32[]{:S(2)}, u32[]{:S(2)}) collective-permute-start(f32[8,192,128]{2,1,0:T(8,128)S(1)} %get-tuple-element.19), channel_id=1, source_target_pairs={{0,1},{1,0},{2,3},{3,2},{4,5},{5,4},{6,7},{7,6},{8,9},{9,8},{10,11... | collective-permute-start | bytes 2359304 | tf_op jit(solution)/shard_map/ppermute | solution.py:298
  7.6 36.8 %collective-permute-start.19 = (f32[8,192,128]{2,1,0:T(8,128)S(1)}, f32[8,192,128]{2,1,0:T(8,128)S(1)}, u32[]{:S(2)}, u32[]{:S(2)}) collective-permute-start(f32[8,192,128]{2,1,0:T(8,128)S(1)} %get-tuple-element.18), channel_id=1, source_target_pairs={{0,3},{1,2},{2,1},{3,0},{4,7},{5,6},{6,5},{7,4},{8,11},{9,10},{10,... | collective-permute-start | bytes 2359304 | tf_op jit(solution)/shard_map/ppermute | solution.py:298
  9.1 35.8 %collective-permute-start.22 = (f32[8,192,128]{2,1,0:T(8,128)S(1)}, f32[8,192,128]{2,1,0:T(8,128)S(1)}, u32[]{:S(2)}, u32[]{:S(2)}) collective-permute-start(f32[8,192,128]{2,1,0:T(8,128)S(1)} %get-tuple-element.17), channel_id=1, source_target_pairs={{0,2},{1,3},{2,0},{3,1},{4,6},{5,7},{6,4},{7,5},{8,10},{9,11},{10,... | collective-permute-start | bytes 2359304 | tf_op jit(solution)/shard_map/ppermute | solution.py:298
  22.9 5.2 %copy-start.7 = (f32[8,192,128]{2,1,0:T(8,128)}, f32[8,192,128]{2,1,0:T(8,128)S(1)}, u32[]{:S(2)}) copy-start(f32[8,192,128]{2,1,0:T(8,128)S(1)} %collective-permute-done.1.refs_3_) | copy-start | bytes 2359300
  22.9 26.4 %collective-permute-start.4 = (f32[8,192,128]{2,1,0:T(8,128)S(1)}, f32[8,192,128]{2,1,0:T(8,128)S(1)}, u32[]{:S(2)}, u32[]{:S(2)}) collective-permute-start(f32[8,192,128]{2,1,0:T(8,128)S(1)} %collective-permute-done.1.refs_3_), channel_id=1, source_target_pairs={{8,4},{4,8},{9,5},{5,9},{10,6},{6,10},{11,7},{7,11},{24,20},{20,24... | collective-permute-start | bytes 2359304 | tf_op jit(solution)/shard_map/ppermute | solution.py:279
  23.6 4.4 %copy-start.9 = (f32[8,192,128]{2,1,0:T(8,128)}, f32[8,192,128]{2,1,0:T(8,128)S(1)}, u32[]{:S(2)}) copy-start(f32[8,192,128]{2,1,0:T(8,128)S(1)} %collective-permute-done.2.refs_5_) | copy-start | bytes 2359300
  23.6 27.3 %collective-permute-start.3 = (f32[8,192,128]{2,1,0:T(8,128)S(1)}, f32[8,192,128]{2,1,0:T(8,128)S(1)}, u32[]{:S(2)}, u32[]{:S(2)}) collective-permute-start(f32[8,192,128]{2,1,0:T(8,128)S(1)} %collective-permute-done.2.refs_5_), channel_id=1, source_target_pairs={{4,0},{8,12},{5,1},{9,13},{6,2},{10,14},{7,3},{11,15},{20,16},{24,... | collective-permute-start | bytes 2359304 | tf_op jit(solution)/shard_map/ppermute | solution.py:279
  28.1 94.7 %collective-permute-start.6 = (f32[384,2048]{1,0:T(8,128)}, f32[384,2048]{1,0:T(8,128)}, u32[]{:S(2)}, u32[]{:S(2)}) collective-permute-start(f32[384,2048]{1,0:T(8,128)} %bitcast.24.refs_0_), channel_id=1, source_target_pairs={{0,1},{1,0},{2,3},{3,2},{4,5},{5,4},{6,7},{7,6},{8,9},{9,8},{10,11... | collective-permute-start | bytes 9437192 | tf_op jit(solution)/shard_map/ppermute | solution.py:334
  44.4 84.7 %copy-start.3 = (f32[8,192,128]{2,1,0:T(8,128)}, f32[8,192,128]{2,1,0:T(8,128)S(1)}, u32[]{:S(2)}) copy-start(f32[8,192,128]{2,1,0:T(8,128)S(1)} %collective-permute-done.19.refs_4_) | copy-start | bytes 2359300
  44.4 78.5 %collective-permute-start.14 = (f32[384,2048]{1,0:T(8,128)}, f32[384,2048]{1,0:T(8,128)}, u32[]{:S(2)}, u32[]{:S(2)}) collective-permute-start(f32[384,2048]{1,0:T(8,128)} %bitcast.24.refs_0_), channel_id=1, source_target_pairs={{0,2},{1,3},{2,0},{3,1},{4,6},{5,7},{6,4},{7,5},{8,10},{9,11},{10,... | collective-permute-start | bytes 9437192 | tf_op jit(solution)/shard_map/ppermute | solution.py:334
  44.9 22.7 %collective-permute-start.9 = (f32[8,192,128]{2,1,0:T(8,128)S(1)}, f32[8,192,128]{2,1,0:T(8,128)S(1)}, u32[]{:S(2)}, u32[]{:S(2)}) collective-permute-start(f32[8,192,128]{2,1,0:T(8,128)S(1)} %collective-permute-done.8.refs_2_), channel_id=1, source_target_pairs={{4,0},{0,4},{12,8},{8,12},{5,1},{1,5},{13,9},{9,13},{6,2},{2,6},{1... | collective-permute-start | bytes 2359304 | tf_op jit(solution)/shard_map/ppermute | solution.py:279
  49.3 20.4 %collective-permute-start.10 = (f32[8,192,128]{2,1,0:T(8,128)S(1)}, f32[8,192,128]{2,1,0:T(8,128)S(1)}, u32[]{:S(2)}, u32[]{:S(2)}) collective-permute-start(f32[8,192,128]{2,1,0:T(8,128)S(1)} %collective-permute-done.8.refs_2_), channel_id=1, source_target_pairs={{8,4},{4,8},{9,5},{5,9},{10,6},{6,10},{11,7},{7,11},{24,20},{20,24... | collective-permute-start | bytes 2359304 | tf_op jit(solution)/shard_map/ppermute | solution.py:279
  50.9 0.9 copy-start.19
  51.8 32.7 %collective-permute-start.20 = (f32[8,192,128]{2,1,0:T(8,128)S(1)}, f32[8,192,128]{2,1,0:T(8,128)S(1)}, u32[]{:S(2)}, u32[]{:S(2)}) collective-permute-start(f32[8,192,128]{2,1,0:T(8,128)S(1)} %collective-permute-done.19.refs_4_), channel_id=1, source_target_pairs={{4,0},{0,4},{12,8},{8,12},{5,1},{1,5},{13,9},{9,13},{6,2},{2,6},{1... | collective-permute-start | bytes 2359304 | tf_op jit(solution)/shard_map/ppermute | solution.py:279
  67.6 29.5 %collective-permute-start.23 = (f32[8,192,128]{2,1,0:T(8,128)S(1)}, f32[8,192,128]{2,1,0:T(8,128)S(1)}, u32[]{:S(2)}, u32[]{:S(2)}) collective-permute-start(f32[8,192,128]{2,1,0:T(8,128)S(1)} %collective-permute-done.22.refs_2_), channel_id=1, source_target_pairs={{4,0},{0,4},{12,8},{8,12},{5,1},{1,5},{13,9},{9,13},{6,2},{2,6},{1... | collective-permute-start | bytes 2359304 | tf_op jit(solution)/shard_map/ppermute | solution.py:279
  69.7 27.4 %collective-permute-start.24 = (f32[8,192,128]{2,1,0:T(8,128)S(1)}, f32[8,192,128]{2,1,0:T(8,128)S(1)}, u32[]{:S(2)}, u32[]{:S(2)}) collective-permute-start(f32[8,192,128]{2,1,0:T(8,128)S(1)} %collective-permute-done.22.refs_2_), channel_id=1, source_target_pairs={{8,4},{4,8},{9,5},{5,9},{10,6},{6,10},{11,7},{7,11},{24,20},{20,24... | collective-permute-start | bytes 2359304 | tf_op jit(solution)/shard_map/ppermute | solution.py:279
  84.5 44.6 %copy-start.15 = (f32[8,192,128]{2,1,0:T(8,128)}, f32[8,192,128]{2,1,0:T(8,128)S(1)}, u32[]{:S(2)}) copy-start(f32[8,192,128]{2,1,0:T(8,128)S(1)} %collective-permute-done.20.refs_5_) | copy-start | bytes 2359300
  84.5 14.8 %collective-permute-start.28 = (f32[8,192,128]{2,1,0:T(8,128)S(1)}, f32[8,192,128]{2,1,0:T(8,128)S(1)}, u32[]{:S(2)}, u32[]{:S(2)}) collective-permute-start(f32[8,192,128]{2,1,0:T(8,128)S(1)} %collective-permute-done.19.refs_4_), channel_id=1, source_target_pairs={{8,4},{4,8},{9,5},{5,9},{10,6},{6,10},{11,7},{7,11},{24,20},{20,24... | collective-permute-start | bytes 2359304 | tf_op jit(solution)/shard_map/ppermute | solution.py:279
  97.1 32.0 %copy-start.11 = (f32[8,192,128]{2,1,0:T(8,128)}, f32[8,192,128]{2,1,0:T(8,128)S(1)}, u32[]{:S(2)}) copy-start(f32[8,192,128]{2,1,0:T(8,128)S(1)} %collective-permute-done.23.refs_3_) | copy-start | bytes 2359300
  97.1 57.7 %collective-permute-start = (f32[384,2048]{1,0:T(8,128)}, f32[384,2048]{1,0:T(8,128)}, u32[]{:S(2)}, u32[]{:S(2)}) collective-permute-start(f32[384,2048]{1,0:T(8,128)} %bitcast.24.refs_0_), channel_id=1, source_target_pairs={{0,16},{16,0},{1,17},{17,1},{2,18},{18,2},{3,19},{19,3},{4,20},{20... | collective-permute-start | bytes 9437192 | tf_op jit(solution)/shard_map/ppermute | solution.py:347
  97.1 32.0 %copy-start.13 = (f32[8,192,128]{2,1,0:T(8,128)}, f32[8,192,128]{2,1,0:T(8,128)S(1)}, u32[]{:S(2)}) copy-start(f32[8,192,128]{2,1,0:T(8,128)S(1)} %collective-permute-done.24.refs_5_) | copy-start | bytes 2359300
  97.1 21.8 %collective-permute-start.5 = (f32[8,192,128]{2,1,0:T(8,128)S(1)}, f32[8,192,128]{2,1,0:T(8,128)S(1)}, u32[]{:S(2)}, u32[]{:S(2)}) collective-permute-start(f32[8,192,128]{2,1,0:T(8,128)S(1)} %collective-permute-done.4.refs_7_), channel_id=1, source_target_pairs={{4,0},{8,12},{5,1},{9,13},{6,2},{10,14},{7,3},{11,15},{20,16},{24,... | collective-permute-start | bytes 2359304 | tf_op jit(solution)/shard_map/ppermute | solution.py:279
  99.3 22.7 %collective-permute-start.12 = (f32[8,192,128]{2,1,0:T(8,128)S(1)}, f32[8,192,128]{2,1,0:T(8,128)S(1)}, u32[]{:S(2)}, u32[]{:S(2)}) collective-permute-start(f32[8,192,128]{2,1,0:T(8,128)S(1)} %collective-permute-done.9.refs_3_), channel_id=1, source_target_pairs={{8,4},{4,8},{9,5},{5,9},{10,6},{6,10},{11,7},{7,11},{24,20},{20,24... | collective-permute-start | bytes 2359304 | tf_op jit(solution)/shard_map/ppermute | solution.py:279
  100.0 0.9 copy-start.21
  119.8 21.0 %collective-permute-start.11 = (f32[8,192,128]{2,1,0:T(8,128)S(1)}, f32[8,192,128]{2,1,0:T(8,128)S(1)}, u32[]{:S(2)}, u32[]{:S(2)}) collective-permute-start(f32[8,192,128]{2,1,0:T(8,128)S(1)} %collective-permute-done.10.refs_5_), channel_id=1, source_target_pairs={{4,0},{8,12},{5,1},{9,13},{6,2},{10,14},{7,3},{11,15},{20,16},{24,... | collective-permute-start | bytes 2359304 | tf_op jit(solution)/shard_map/ppermute | solution.py:279
  121.1 0.9 copy-start.23
  122.0 7.0 %copy-start.27 = (f32[8,192,128]{2,1,0:T(8,128)}, f32[8,192,128]{2,1,0:T(8,128)S(1)}, u32[]{:S(2)}) copy-start(f32[8,192,128]{2,1,0:T(8,128)S(1)} %collective-permute-done.12.refs_7_) | copy-start | bytes 2359300
  122.0 21.2 %collective-permute-start.26 = (f32[8,192,128]{2,1,0:T(8,128)S(1)}, f32[8,192,128]{2,1,0:T(8,128)S(1)}, u32[]{:S(2)}, u32[]{:S(2)}) collective-permute-start(f32[8,192,128]{2,1,0:T(8,128)S(1)} %collective-permute-done.23.refs_3_), channel_id=1, source_target_pairs={{8,4},{4,8},{9,5},{5,9},{10,6},{6,10},{11,7},{7,11},{24,20},{20,24... | collective-permute-start | bytes 2359304 | tf_op jit(solution)/shard_map/ppermute | solution.py:279
  122.8 82.5 %collective-permute-start.7 = (f32[384,2048]{1,0:T(8,128)}, f32[384,2048]{1,0:T(8,128)}, u32[]{:S(2)}, u32[]{:S(2)}) collective-permute-start(f32[384,2048]{1,0:T(8,128)} %collective-permute-done.6.refs_0_), channel_id=1, source_target_pairs={{0,16},{16,0},{1,17},{17,1},{2,18},{18,2},{3,19},{19,3},{4,20},{20... | collective-permute-start | bytes 9437192 | tf_op jit(solution)/shard_map/ppermute | solution.py:347
  122.8 21.9 %collective-permute-start.30 = (f32[8,192,128]{2,1,0:T(8,128)S(1)}, f32[8,192,128]{2,1,0:T(8,128)S(1)}, u32[]{:S(2)}, u32[]{:S(2)}) collective-permute-start(f32[8,192,128]{2,1,0:T(8,128)S(1)} %collective-permute-done.20.refs_5_), channel_id=1, source_target_pairs={{8,4},{4,8},{9,5},{5,9},{10,6},{6,10},{11,7},{7,11},{24,20},{20,24... | collective-permute-start | bytes 2359304 | tf_op jit(solution)/shard_map/ppermute | solution.py:279
  140.8 0.9 copy-start.29
  141.7 35.4 %collective-permute-start.15 = (f32[192,2048]{1,0:T(8,128)}, f32[192,2048]{1,0:T(8,128)}, u32[]{:S(2)}, u32[]{:S(2)}) collective-permute-start(f32[192,2048]{1,0:T(8,128)} %slice.21), channel_id=1, source_target_pairs={{0,1},{1,0},{2,3},{3,2},{4,5},{5,4},{6,7},{7,6},{8,9},{9,8},{10,11... | collective-permute-start | bytes 4718600 | tf_op jit(solution)/shard_map/ppermute | solution.py:338
  143.2 1.5 copy-start.25
  143.2 35.1 %collective-permute-start.16 = (f32[192,2048]{1,0:T(8,128)}, f32[192,2048]{1,0:T(8,128)}, u32[]{:S(2)}, u32[]{:S(2)}) collective-permute-start(f32[192,2048]{1,0:T(8,128)} %slice.22), channel_id=1, source_target_pairs={{0,2},{1,3},{2,0},{3,1},{4,6},{5,7},{6,4},{7,5},{8,10},{9,11},{10,... | collective-permute-start | bytes 4718600 | tf_op jit(solution)/shard_map/ppermute | solution.py:339
  144.7 98.4 %collective-permute-start.21 = (f32[384,2048]{1,0:T(8,128)}, f32[384,2048]{1,0:T(8,128)}, u32[]{:S(2)}, u32[]{:S(2)}) collective-permute-start(f32[384,2048]{1,0:T(8,128)} %collective-permute-done.14.refs_0_), channel_id=1, source_target_pairs={{0,16},{16,0},{1,17},{17,1},{2,18},{18,2},{3,19},{19,3},{4,20},{20... | collective-permute-start | bytes 9437192 | tf_op jit(solution)/shard_map/ppermute | solution.py:347
  144.9 3.4 %copy-start.2 = (f32[8,128,16,128]{3,2,1,0:T(8,128)S(1)}, f32[8,128,16,128]{3,2,1,0:T(8,128)}, u32[]{:S(2)}) copy-start(f32[8,128,16,128]{3,2,1,0:T(8,128)} %param.3) | copy-start | bytes 25165828
  151.1 3.4 %copy-start = (f32[1024,2048]{1,0:T(8,128)}, f32[1024,2048]{1,0:T(8,128)S(1)}, u32[]{:S(2)}) copy-start(f32[1024,2048]{1,0:T(8,128)S(1)} %fold.1.acc_ref) | copy-start | bytes 25165828
  154.7 49.1 %copy-start.14 = (f32[8,192,128]{2,1,0:T(8,128)S(1)}, f32[8,192,128]{2,1,0:T(8,128)}, u32[]{:S(2)}) copy-start(f32[8,192,128]{2,1,0:T(8,128)} %copy-done.13) | copy-start | bytes 2359300
  154.7 51.9 %copy-start.6 = (f32[8,192,128]{2,1,0:T(8,128)S(1)}, f32[8,192,128]{2,1,0:T(8,128)}, u32[]{:S(2)}) copy-start(f32[8,192,128]{2,1,0:T(8,128)} %copy-done.5) | copy-start | bytes 2359300
  154.8 49.0 %collective-permute-start.13 = (f32[8,192,128]{2,1,0:T(8,128)}, f32[8,192,128]{2,1,0:T(8,128)S(1)}, u32[]{:S(2)}, u32[]{:S(2)}) collective-permute-start(f32[8,192,128]{2,1,0:T(8,128)} %copy-done.27), channel_id=1, source_target_pairs={{4,0},{8,12},{5,1},{9,13},{6,2},{10,14},{7,3},{11,15},{20,16},{24,... | collective-permute-start | bytes 2359304 | tf_op jit(solution)/shard_map/ppermute | solution.py:279
  177.1 45.7 %collective-permute-start.17 = (f32[192,2048]{1,0:T(8,128)}, f32[192,2048]{1,0:T(8,128)S(1)}, u32[]{:S(2)}, u32[]{:S(2)}) collective-permute-start(f32[192,2048]{1,0:T(8,128)} %collective-permute-done.15.refs_0_), channel_id=1, source_target_pairs={{0,16},{16,0},{1,17},{17,1},{2,18},{18,2},{3,19},{19,3},{4,20},{20... | collective-permute-start | bytes 4718600 | tf_op jit(solution)/shard_map/ppermute | solution.py:347
  178.3 45.8 %collective-permute-start.18 = (f32[192,2048]{1,0:T(8,128)}, f32[192,2048]{1,0:T(8,128)S(1)}, u32[]{:S(2)}, u32[]{:S(2)}) collective-permute-start(f32[192,2048]{1,0:T(8,128)} %collective-permute-done.16.refs_1_), channel_id=1, source_target_pairs={{0,16},{16,0},{1,17},{17,1},{2,18},{18,2},{3,19},{19,3},{4,20},{20... | collective-permute-start | bytes 4718600 | tf_op jit(solution)/shard_map/ppermute | solution.py:347
  178.3 3.4 %copy-start.1 = (f32[1024,2048]{1,0:T(8,128)S(1)}, f32[1024,2048]{1,0:T(8,128)}, u32[]{:S(2)}) copy-start(f32[1024,2048]{1,0:T(8,128)} %copy-done) | copy-start | bytes 25165828
  181.7 1.1 copy-start.8
  182.8 1.1 copy-start.10
  184.0 1.1 copy-start.18
  185.1 1.1 copy-start.20
  186.2 1.1 copy-start.32
  187.4 17.9 %copy-start.26 = (f32[8,192,128]{2,1,0:T(8,128)S(1)}, f32[8,192,128]{2,1,0:T(8,128)}, u32[]{:S(2)}) copy-start(f32[8,192,128]{2,1,0:T(8,128)} %copy-done.25) | copy-start | bytes 2359300
  187.4 19.2 %copy-start.22 = (f32[8,192,128]{2,1,0:T(8,128)S(1)}, f32[8,192,128]{2,1,0:T(8,128)}, u32[]{:S(2)}) copy-start(f32[8,192,128]{2,1,0:T(8,128)} %copy-done.21) | copy-start | bytes 2359300
  187.4 19.2 %copy-start.24 = (f32[8,192,128]{2,1,0:T(8,128)S(1)}, f32[8,192,128]{2,1,0:T(8,128)}, u32[]{:S(2)}) copy-start(f32[8,192,128]{2,1,0:T(8,128)} %copy-done.23) | copy-start | bytes 2359300
  187.4 19.2 %copy-start.28 = (f32[8,192,128]{2,1,0:T(8,128)S(1)}, f32[8,192,128]{2,1,0:T(8,128)}, u32[]{:S(2)}) copy-start(f32[8,192,128]{2,1,0:T(8,128)} %copy-done.27) | copy-start | bytes 2359300
  187.4 19.2 %copy-start.30 = (f32[8,192,128]{2,1,0:T(8,128)S(1)}, f32[8,192,128]{2,1,0:T(8,128)}, u32[]{:S(2)}) copy-start(f32[8,192,128]{2,1,0:T(8,128)} %copy-done.29) | copy-start | bytes 2359300
  203.8 21.7 %copy-start.4 = (f32[8,192,128]{2,1,0:T(8,128)S(1)}, f32[8,192,128]{2,1,0:T(8,128)}, u32[]{:S(2)}) copy-start(f32[8,192,128]{2,1,0:T(8,128)} %copy-done.3) | copy-start | bytes 2359300
  203.8 21.7 %copy-start.16 = (f32[8,192,128]{2,1,0:T(8,128)S(1)}, f32[8,192,128]{2,1,0:T(8,128)}, u32[]{:S(2)}) copy-start(f32[8,192,128]{2,1,0:T(8,128)} %copy-done.15) | copy-start | bytes 2359300
  203.8 37.7 %collective-permute-start.25 = (f32[8,192,128]{2,1,0:T(8,128)S(1)}, f32[8,192,128]{2,1,0:T(8,128)S(1)}, u32[]{:S(2)}, u32[]{:S(2)}) collective-permute-start(f32[8,192,128]{2,1,0:T(8,128)S(1)} %copy-done.14), channel_id=1, source_target_pairs={{4,0},{8,12},{5,1},{9,13},{6,2},{10,14},{7,3},{11,15},{20,16},{24,... | collective-permute-start | bytes 2359304 | tf_op jit(solution)/shard_map/ppermute | solution.py:279
  205.3 37.8 %collective-permute-start.27 = (f32[8,192,128]{2,1,0:T(8,128)S(1)}, f32[8,192,128]{2,1,0:T(8,128)S(1)}, u32[]{:S(2)}, u32[]{:S(2)}) collective-permute-start(f32[8,192,128]{2,1,0:T(8,128)S(1)} %copy-done.26), channel_id=1, source_target_pairs={{4,0},{8,12},{5,1},{9,13},{6,2},{10,14},{7,3},{11,15},{20,16},{24,... | collective-permute-start | bytes 2359304 | tf_op jit(solution)/shard_map/ppermute | solution.py:279
  222.8 37.2 %collective-permute-start.29 = (f32[8,192,128]{2,1,0:T(8,128)S(1)}, f32[8,192,128]{2,1,0:T(8,128)S(1)}, u32[]{:S(2)}, u32[]{:S(2)}) collective-permute-start(f32[8,192,128]{2,1,0:T(8,128)S(1)} %collective-permute-done.28.refs_1_), channel_id=1, source_target_pairs={{4,0},{8,12},{5,1},{9,13},{6,2},{10,14},{7,3},{11,15},{20,16},{24,... | collective-permute-start | bytes 2359304 | tf_op jit(solution)/shard_map/ppermute | solution.py:279
  224.1 19.1 %copy-start.12 = (f32[8,192,128]{2,1,0:T(8,128)S(1)}, f32[8,192,128]{2,1,0:T(8,128)}, u32[]{:S(2)}) copy-start(f32[8,192,128]{2,1,0:T(8,128)} %copy-done.11) | copy-start | bytes 2359300
  224.1 44.3 %collective-permute-start.31 = (f32[4,192,128]{2,1,0:T(8,128)S(1)}, f32[4,192,128]{2,1,0:T(8,128)S(1)}, u32[]{:S(2)}, u32[]{:S(2)}) collective-permute-start(f32[4,192,128]{2,1,0:T(8,128)S(1)} %get-tuple-element.22), channel_id=1, source_target_pairs={{4,0},{8,12},{5,1},{9,13},{6,2},{10,14},{7,3},{11,15},{20,16},{24,... | collective-permute-start | bytes 1179656 | tf_op jit(solution)/shard_map/ppermute | solution.py:277
  241.6 34.8 %collective-permute-start.32 = (f32[4,192,128]{2,1,0:T(8,128)S(1)}, f32[4,192,128]{2,1,0:T(8,128)S(1)}, u32[]{:S(2)}, u32[]{:S(2)}) collective-permute-start(f32[4,192,128]{2,1,0:T(8,128)S(1)} %get-tuple-element.21), channel_id=1, source_target_pairs={{4,0},{8,12},{5,1},{9,13},{6,2},{10,14},{7,3},{11,15},{20,16},{24,... | collective-permute-start | bytes 1179656 | tf_op jit(solution)/shard_map/ppermute | solution.py:277
  (3 other events, 2.7 us)

commit v2 on v1

--- a/solution.py
+++ b/solution.py
@@ -225,7 +225,7 @@
 def last(acc, slot, first, scalars, right, blocks, first_block, row_blocks, buffer):
     rows, cols = acc.shape
     width, height = slot[0].shape[1:]
-    step = 2 if row_blocks % 2 == 0 else 1
+    step = 2 if row_blocks % 4 == 0 else 1
     base = first_block // step
     buffers = () if buffer is None else (buffer,)
     resident = pl.BlockSpec(memory_space=pltpu.VMEM)
@@ -272,9 +272,9 @@
             pairs = [(mate(i, odd), i) for i in range(count) if reach(i, odd) >= step]
             if pairs:
                 what = piece if step == 1 else streams[1 - odd][step - 2]
-                if tails > 1 and odd == 0 and step == count - 1:
-                    cut = what.shape[0] // tails
-                    new[odd] = [lax.ppermute(what[n * cut : (n + 1) * cut], axis, pairs) for n in range(tails)]
+                if len(tails) > 1 and odd == 0 and step == count - 1:
+                    parts = [what[sum(tails[:n]) : sum(tails[: n + 1])] for n in range(len(tails))]
+                    new[odd] = [lax.ppermute(part, axis, pairs) for part in parts]
                 else:
                     new[odd] = lax.ppermute(what, axis, pairs)
         for odd, value in new.items():
@@ -295,10 +295,13 @@
     power, pairs, _, target = moves(n_kk)
     left = left_panel.transpose(0, 2, 3, 1).reshape(n_kk, row_blocks, width, height)
     group = lambda index: lax.dynamic_index_in_dim(left, index, 0, keepdims=False)
-    pieces = [group(kk) if m == 0 else lax.ppermute(group(target(kk, m)), "kk", pairs(m)) for m in order]
-
-    tails = 2 if row_blocks % 2 == 0 and n_col > 2 else 1
-    streams = [line(piece, "col", n_col, tails if i == n_kk - 1 else 0) for i, piece in enumerate(pieces)]
+    groups = [group(kk)] + [group(target(kk, m)) for m in order[1:2]]
+    *groups, left = lax.optimization_barrier((*groups, left))
+    groups += [group(target(kk, m)) for m in order[2:]]
+    pieces = [groups[0] if m == 0 else lax.ppermute(groups[i], "kk", pairs(m)) for i, m in enumerate(order)]
+
+    tails = [row_blocks // n for n in (2, 4, 4)] if row_blocks % 4 == 0 and n_col > 2 else [row_blocks]
+    streams = [line(piece, "col", n_col, tails if i == n_kk - 1 else ()) for i, piece in enumerate(pieces)]
     even = col % 2 == 0
     length = jnp.where(even, n_col - 1 - col, col)
     lengths = sorted({n_col - 1 - i if i % 2 == 0 else i for i in range(n_col)})
@@ -381,14 +384,15 @@
         slot = slot_of(pieces[final], streams[final], index)
         acc = one(acc, slot, scalars[2 * index : 2 * index + 2], kept)
 
-    cut = row_blocks // tails
-    out = None
-    for part in range(tails):
+    out, start = None, 0
+    for part, count in enumerate(tails):
         stream = {0: list(streams[final][0]), 1: streams[final][1]}
-        stream[0][-1] = stream[0][-1][part] if isinstance(stream[0][-1], list) else stream[0][-1]
+        if len(tails) > 1:
+            stream[0][-1] = stream[0][-1][part]
         options = slot_of(pieces[final], stream, n_col - 1)
-        first = [0 if option.shape[0] == cut else part * cut for option in options]
-        out, acc = last(acc, options, first, scalars[-2:], kept, blocks, part * cut, cut, out)
+        first = [0 if option.shape[0] == count else start for option in options]
+        out, acc = last(acc, options, first, scalars[-2:], kept, blocks, start, count, out)
+        start += count
     return out.reshape(contribution.shape)
 
 

time: 283 us -> 282 us (level)
  waiting for transfers between devices: 127 us -> 123 us
    ppermute x19, waiting for transfers between devices: 84.5 us -> 80.5 us  [line(): new[odd] = lax.ppermute(what, axis, pairs)]
    pallas_call x2 -> x3, Pallas kernels: 10.1 us -> 12 us  [last(): pl.pallas_call(functools.partial(last_kernel, blocks, len(slot), first, f...]
    ppermute x5 -> x6, starting transfers between devices: 6.45 us -> 7.6 us  [the longest x3 4.05 us: line(): new[odd] = [lax.ppermute(part, axis, pairs) for part in parts]]
    unnamed x69 -> x65, local copies, waits for them, and re-layouts: 25.3 us -> 24.7 us
    ppermute x5 -> x6, waiting for transfers between devices: 20.2 us -> 20 us  [the longest x3 18.1 us: local(): lax.ppermute(groups[i], 'kk', pairs(m))]
  transfers between devices with their start and end apart: 33 -> 34, of which waited for: 13 -> 12; matrix products, arithmetic and copies ran while one was open for 3% -> 4% of each run, Pallas kernels for 28% -> 29%
where the time goes in v2:
time: 282 us; the launch traced here: 281 us
  waiting for transfers between devices  123 us (44%)
  Pallas kernels  85.1 us (30%)
  starting transfers between devices  37.6 us (13%)
  local copies, waits for them, and re-layouts  34.4 us (12%)
    ppermute x19, waiting for transfers between devices, line(): new[odd] = lax.ppermute(what, axis, pairs)  80.5 us
    pallas_call x4, Pallas kernels, add(): pl.pallas_call(functools.partial(add_kernel, [len(slot) for slot in slots...  64.5 us
    ppermute x19, starting transfers between devices, line(): new[odd] = lax.ppermute(what, axis, pairs)  25.8 us
    unnamed x65, local copies, waits for them, and re-layouts  24.7 us
    ppermute x1, waiting for transfers between devices, local(): first = lax.ppermute(whole(parts[m ^ bits[0]])[:half], 'kk', pairs(bits[0]))  21.6 us
    ppermute x3, waiting for transfers between devices, local(): lax.ppermute(groups[i], 'kk', pairs(m))  18.1 us
    pallas_call x3, Pallas kernels, last(): pl.pallas_call(functools.partial(last_kernel, blocks, len(slot), first, f...  12 us
    pallas_call x1, Pallas kernels, one(): pl.pallas_call(functools.partial(one_kernel, len(slot)), out_shape=jax.Sh...  5.75 us
  transfers between devices with their start and end apart: 34, of which 12 were waited for; matrix products, arithmetic and copies ran while one was open for 4% of the time, Pallas kernels for 29%

profile of v2, /device:TPU:0, one launch (start us, length us, event | category | flops | bytes accessed | tf_op | source)
XLA Modules:
  0.0 281.3 jit_solution(12059875083844827406)
XLA Ops:
  0.0 2.4 dynamic-slice_bitcast_fusion.2
  2.4 3.1 %collective-permute-start.1 = (f32[8,192,128]{2,1,0:T(8,128)S(1)}, f32[8,192,128]{2,1,0:T(8,128)S(1)}, u32[]{:S(2)}, u32[]{:S(2)}) collective-permute-start(f32[8,192,128]{2,1,0:T(8,128)S(1)} %get-tuple-element.16.refs_2_), channel_id=1, source_target_pairs={{4,0},{0,4},{12,8},{8,12},{5,1},{1,5},{13,9},{9,13},{6,2},{2,6},{1... | collective-permute-start | bytes 2359304 | tf_op jit(solution)/shard_map/ppermute | solution.py:279
  5.5 1.6 collective-permute-start.2
  7.0 1.5 collective-permute-start.8
  8.5 1.6 dynamic-slice_bitcast_fusion
  10.1 1.6 collective-permute-start.19
  12.2 10.8 %collective-permute-done.1.refs_3_ = f32[8,192,128]{2,1,0:T(8,128)S(1)} collective-permute-done((f32[8,192,128]{2,1,0:T(8,128)S(1)}, f32[8,192,128]{2,1,0:T(8,128)S(1)}, u32[]{:S(2)}, u32[]{:S(2)}) %collective-permute-start.1) | collective-permute-done | bytes 786464 | tf_op jit(solution)/shard_map/ppermute | solution.py:279
  23.7 1.3 collective-permute-start.3
  25.0 3.1 %copy.16 = f32[48,8,16,128]{3,1,2,0:T(8,128)} copy(f32[48,8,16,128]{3,2,1,0:T(8,128)S(1)} %bitcast.28) | data formatting | bytes 6291456
  28.2 1.7 collective-permute-start.6
  29.8 15.7 %collective-permute-done.19.refs_4_ = f32[8,192,128]{2,1,0:T(8,128)S(1)} collective-permute-done((f32[8,192,128]{2,1,0:T(8,128)S(1)}, f32[8,192,128]{2,1,0:T(8,128)S(1)}, u32[]{:S(2)}, u32[]{:S(2)}) %collective-permute-start.19) | collective-permute-done | bytes 786464 | tf_op jit(solution)/shard_map/ppermute | solution.py:301
  46.0 2.4 collective-permute-done.22.refs_2_
  48.4 3.3 %collective-permute-start.9 = (f32[8,192,128]{2,1,0:T(8,128)S(1)}, f32[8,192,128]{2,1,0:T(8,128)S(1)}, u32[]{:S(2)}, u32[]{:S(2)}) collective-permute-start(f32[8,192,128]{2,1,0:T(8,128)S(1)} %collective-permute-done.8.refs_2_), channel_id=1, source_target_pairs={{4,0},{0,4},{12,8},{8,12},{5,1},{1,5},{13,9},{9,13},{6,2},{2,6},{1... | collective-permute-start | bytes 2359304 | tf_op jit(solution)/shard_map/ppermute | solution.py:279
  51.7 0.7 collective-permute-start.10
  52.5 0.9 copy-done.5
  53.4 0.9 copy-done.17
  54.3 1.5 collective-permute-start.20
  55.8 14.3 %collective-permute-done.9.refs_3_ = f32[8,192,128]{2,1,0:T(8,128)S(1)} collective-permute-done((f32[8,192,128]{2,1,0:T(8,128)S(1)}, f32[8,192,128]{2,1,0:T(8,128)S(1)}, u32[]{:S(2)}, u32[]{:S(2)}) %collective-permute-start.9) | collective-permute-done | bytes 786464 | tf_op jit(solution)/shard_map/ppermute | solution.py:279
  70.1 2.0 collective-permute-start.23
  72.2 0.7 collective-permute-start.24
  72.9 14.1 %collective-permute-done.20.refs_5_ = f32[8,192,128]{2,1,0:T(8,128)S(1)} collective-permute-done((f32[8,192,128]{2,1,0:T(8,128)S(1)}, f32[8,192,128]{2,1,0:T(8,128)S(1)}, u32[]{:S(2)}, u32[]{:S(2)}) %collective-permute-start.20) | collective-permute-done | bytes 786464 | tf_op jit(solution)/shard_map/ppermute | solution.py:279
  87.7 10.8 %collective-permute-done.23.refs_3_ = f32[8,192,128]{2,1,0:T(8,128)S(1)} collective-permute-done((f32[8,192,128]{2,1,0:T(8,128)S(1)}, f32[8,192,128]{2,1,0:T(8,128)S(1)}, u32[]{:S(2)}, u32[]{:S(2)}) %collective-permute-start.23) | collective-permute-done | bytes 786464 | tf_op jit(solution)/shard_map/ppermute | solution.py:279
  98.5 1.3 collective-permute-start.5
  99.8 0.9 copy-done.15
  100.7 0.7 collective-permute-start.12
  101.4 0.9 copy-done.19
  102.3 18.0 %collective-permute-done.5.refs_6_ = f32[8,192,128]{2,1,0:T(8,128)S(1)} collective-permute-done((f32[8,192,128]{2,1,0:T(8,128)S(1)}, f32[8,192,128]{2,1,0:T(8,128)S(1)}, u32[]{:S(2)}, u32[]{:S(2)}) %collective-permute-start.5) | collective-permute-done | bytes 786464 | tf_op jit(solution)/shard_map/ppermute | solution.py:279
  120.4 0.9 copy-done.29
  121.2 1.3 collective-permute-start.11
  122.5 0.9 copy-done.21
  123.4 0.7 collective-permute-start.26
  124.3 0.7 collective-permute-start.30
  125.0 2.7 slice.27
  127.7 2.8 slice.26
  130.6 11.6 %collective-permute-done.11.refs_4_ = f32[8,192,128]{2,1,0:T(8,128)S(1)} collective-permute-done((f32[8,192,128]{2,1,0:T(8,128)S(1)}, f32[8,192,128]{2,1,0:T(8,128)S(1)}, u32[]{:S(2)}, u32[]{:S(2)}) %collective-permute-start.11) | collective-permute-done | bytes 786464 | tf_op jit(solution)/shard_map/ppermute | solution.py:279
  142.2 0.9 copy-done.27
  143.1 1.5 collective-permute-start.15
  145.5 3.4 %copy-done.2 = f32[8,128,16,128]{3,2,1,0:T(8,128)S(1)} copy-done((f32[8,128,16,128]{3,2,1,0:T(8,128)S(1)}, f32[8,128,16,128]{3,2,1,0:T(8,128)}, u32[]{:S(2)}) %copy-start.2) | copy-done | bytes 8388632
  148.9 2.8 fold.1.acc_ref
  151.7 3.4 %copy-done = f32[1024,2048]{1,0:T(8,128)} copy-done((f32[1024,2048]{1,0:T(8,128)}, f32[1024,2048]{1,0:T(8,128)S(1)}, u32[]{:S(2)}) %copy-start) | copy-done | bytes 8388632
  155.5 1.4 collective-permute-start.13
  156.9 21.6 %collective-permute-done.15.refs_0_ = f32[192,2048]{1,0:T(8,128)} collective-permute-done((f32[192,2048]{1,0:T(8,128)}, f32[192,2048]{1,0:T(8,128)}, u32[]{:S(2)}, u32[]{:S(2)}) %collective-permute-start.15) | collective-permute-done | bytes 1572896 | tf_op jit(solution)/shard_map/ppermute | solution.py:341
  178.5 1.2 collective-permute-done.16.refs_1_
  179.7 3.4 %copy-done.1 = f32[1024,2048]{1,0:T(8,128)S(1)} copy-done((f32[1024,2048]{1,0:T(8,128)S(1)}, f32[1024,2048]{1,0:T(8,128)}, u32[]{:S(2)}) %copy-start.1) | copy-done | bytes 8388632
  183.1 1.1 copy-done.8
  184.3 1.1 copy-done.16
  185.4 1.1 copy-done.18
  186.5 1.1 copy-done.30
  187.7 16.4 %add.77.acc_ref = f32[1024,2048]{1,0:T(8,128)S(1)} custom-call(s32[8]{0:T(128)S(1)} %stack.49.scalars, f32[1024,2048]{1,0:T(8,128)S(1)} %copy-done.1, f32[384,2048]{1,0:T(8,128)} %bitcast.24.refs_0_, f32[384,2048]{1,0:T(8,128)} %collective-permute-done.refs_1_, f32[8,192,128]{2,1,0:T(8,128)S(1)} %get-tuple-element.16.refs_2_, ...), custom_call_target="tpu_custom_call", output_to_operand_aliasing={{}: (1, {})} | custom-call | flops 9663676416 | bytes 6291456 | tf_op jit(solution)/shard_map/add/pallas_call | solution.py:101
  204.1 1.4 collective-permute-start.25
  205.5 1.3 collective-permute-start.27
  206.9 16.1 %add.78.acc_ref = f32[1024,2048]{1,0:T(8,128)S(1)} custom-call(s32[8]{0:T(128)S(1)} %stack.49.scalars, f32[1024,2048]{1,0:T(8,128)S(1)} %add.77.acc_ref, f32[384,2048]{1,0:T(8,128)} %collective-permute-done.6.refs_0_, f32[384,2048]{1,0:T(8,128)} %collective-permute-done.7.refs_1_, f32[8,192,128]{2,1,0:T(8,128)S(1)} %copy-done.6, ...), custom_call_target="tpu_custom_call", output_to_operand_aliasing={{}: (1, {})} | custom-call | flops 9663676416 | bytes 6291456 | tf_op jit(solution)/shard_map/add/pallas_call | solution.py:101
  223.0 1.4 collective-permute-start.29
  224.4 1.3 collective-permute-start.31
  225.8 16.0 %add.79 = (f32[1024,2048]{1,0:T(8,128)S(1)}, bf16[768,2048]{1,0:T(8,128)(2,1)S(1)}, bf16[768,2048]{1,0:T(8,128)(2,1)S(1)}) custom-call(s32[8]{0:T(128)S(1)} %stack.49.scalars, f32[1024,2048]{1,0:T(8,128)S(1)} %add.78.acc_ref, f32[192,2048]{1,0:T(8,128)} %collective-permute-done.15.refs_0_, ...), custom_call_target="tpu_custom_call", output_to_operand_aliasing={{0}: (1, {})} | custom-call | flops 4831838208 | bytes 6291456 | tf_op jit(solution)/shard_map/add/pallas_call | solution.py:101
  241.8 1.3 collective-permute-start.32
  243.1 0.7 collective-permute-done.27.refs_6_
  243.8 1.5 collective-permute-start.33
  245.3 16.1 %add.80.acc_ref = f32[1024,2048]{1,0:T(8,128)S(1)} custom-call(s32[8]{0:T(128)S(1)} %stack.49.scalars, f32[1024,2048]{1,0:T(8,128)S(1)} %get-tuple-element.19.acc_ref, f32[384,2048]{1,0:T(8,128)} %collective-permute-done.14.refs_0_, f32[384,2048]{1,0:T(8,128)} %collective-permute-done.21.refs_1_, ...), custom_call_target="tpu_custom_call", output_to_operand_aliasing={{}: (1, {})} | custom-call | flops 9663676416 | bytes 6291456 | tf_op jit(solution)/shard_map/add/pallas_call | solution.py:101
  261.4 5.8 %one.1.acc_ref = f32[1024,2048]{1,0:T(8,128)S(1)} custom-call(s32[2]{0:T(128)S(1)} %pad_add_fusion.1.scalars, f32[1024,2048]{1,0:T(8,128)S(1)} %add.80.acc_ref, bf16[768,2048]{1,0:T(8,128)(2,1)S(1)} %get-tuple-element.20.high_ref, bf16[768,2048]{1,0:T(8,128)(2,1)S(1)} %get-tuple-element.21.low_ref, ...), custom_call_target="tpu_custom_call", output_to_operand_aliasing={{}: (1, {})} | custom-call | flops 2415919104 | bytes 786432 | tf_op jit(solution)/shard_map/one/pallas_call | solution.py:178
  267.1 1.9 collective-permute-done.31.refs_0_
  269.1 5.1 %last.3 = (f32[16384,128]{1,0:T(8,128)}, f32[1024,2048]{1,0:T(8,128)S(1)}) custom-call(s32[2]{0:T(128)S(1)} %pad_add_fusion.scalars, f32[1024,2048]{1,0:T(8,128)S(1)} %one.1.acc_ref, bf16[768,2048]{1,0:T(8,128)(2,1)S(1)} %get-tuple-element.20.high_ref, bf16[768,2048]{1,0:T(8,128)(2,1)S(1)} %get-tuple-element.21.low_ref, ...), custom_call_target="tpu_custom_call", output_to_operand_aliasing={{1}: (1, {})} | custom-call | flops 1207959552 | bytes 4194304 | tf_op jit(solution)/shard_map/last/pallas_call | solution.py:232
  274.2 3.5 %last.4 = (f32[16384,128]{1,0:T(8,128)}, f32[1024,2048]{1,0:T(8,128)S(1)}) custom-call(s32[2]{0:T(128)S(1)} %pad_add_fusion.scalars, f32[1024,2048]{1,0:T(8,128)S(1)} %get-tuple-element.22.acc_ref, bf16[768,2048]{1,0:T(8,128)(2,1)S(1)} %get-tuple-element.20.high_ref, ...), custom_call_target="tpu_custom_call", output_to_operand_aliasing={{1}: (1, {}), {0}: (6, {})} | custom-call | flops 603979776 | bytes 2097152 | tf_op jit(solution)/shard_map/last/pallas_call | solution.py:232
  277.7 3.5 %last.5 = (f32[16384,128]{1,0:T(8,128)}, f32[1024,2048]{1,0:T(8,128)S(1)}) custom-call(s32[2]{0:T(128)S(1)} %pad_add_fusion.scalars, f32[1024,2048]{1,0:T(8,128)S(1)} %get-tuple-element.24.acc_ref, bf16[768,2048]{1,0:T(8,128)(2,1)S(1)} %get-tuple-element.20.high_ref, ...), custom_call_target="tpu_custom_call", output_to_operand_aliasing={{1}: (1, {}), {0}: (6, {})} | custom-call | flops 603979776 | bytes 2097152 | tf_op jit(solution)/shard_map/last/pallas_call | solution.py:232
  (87 shorter events, 3.9 us)
Async XLA Ops:
  2.4 20.6 %collective-permute-start.1 = (f32[8,192,128]{2,1,0:T(8,128)S(1)}, f32[8,192,128]{2,1,0:T(8,128)S(1)}, u32[]{:S(2)}, u32[]{:S(2)}) collective-permute-start(f32[8,192,128]{2,1,0:T(8,128)S(1)} %get-tuple-element.16.refs_2_), channel_id=1, source_target_pairs={{4,0},{0,4},{12,8},{8,12},{5,1},{1,5},{13,9},{9,13},{6,2},{2,6},{1... | collective-permute-start | bytes 2359304 | tf_op jit(solution)/shard_map/ppermute | solution.py:279
  5.5 18.2 %collective-permute-start.2 = (f32[8,192,128]{2,1,0:T(8,128)S(1)}, f32[8,192,128]{2,1,0:T(8,128)}, u32[]{:S(2)}, u32[]{:S(2)}) collective-permute-start(f32[8,192,128]{2,1,0:T(8,128)S(1)} %get-tuple-element.16.refs_2_), channel_id=1, source_target_pairs={{8,4},{4,8},{9,5},{5,9},{10,6},{6,10},{11,7},{7,11},{24,20},{20,24... | collective-permute-start | bytes 2359304 | tf_op jit(solution)/shard_map/ppermute | solution.py:279
  7.0 21.1 %collective-permute-start.8 = (f32[8,192,128]{2,1,0:T(8,128)}, f32[8,192,128]{2,1,0:T(8,128)S(1)}, u32[]{:S(2)}, u32[]{:S(2)}) collective-permute-start(f32[8,192,128]{2,1,0:T(8,128)} %get-tuple-element.17), channel_id=1, source_target_pairs={{0,1},{1,0},{2,3},{3,2},{4,5},{5,4},{6,7},{7,6},{8,9},{9,8},{10,11... | collective-permute-start | bytes 2359304 | tf_op jit(solution)/shard_map/ppermute | solution.py:301
  8.5 16.5 %copy-start.31 = (f32[1,384,16,128]{3,2,1,0:T(8,128)S(1)}, f32[1,384,16,128]{3,2,1,0:T(8,128)}, u32[]{:S(2)}) copy-start(f32[1,384,16,128]{3,2,1,0:T(8,128)} %param.5) | copy-start | bytes 9437188
  10.1 35.3 %collective-permute-start.19 = (f32[8,192,128]{2,1,0:T(8,128)S(1)}, f32[8,192,128]{2,1,0:T(8,128)S(1)}, u32[]{:S(2)}, u32[]{:S(2)}) collective-permute-start(f32[8,192,128]{2,1,0:T(8,128)S(1)} %get-tuple-element.28), channel_id=1, source_target_pairs={{0,3},{1,2},{2,1},{3,0},{4,7},{5,6},{6,5},{7,4},{8,11},{9,10},{10,... | collective-permute-start | bytes 2359304 | tf_op jit(solution)/shard_map/ppermute | solution.py:301
  11.7 36.7 %collective-permute-start.22 = (f32[8,192,128]{2,1,0:T(8,128)S(1)}, f32[8,192,128]{2,1,0:T(8,128)S(1)}, u32[]{:S(2)}, u32[]{:S(2)}) collective-permute-start(f32[8,192,128]{2,1,0:T(8,128)S(1)} %get-tuple-element.27), channel_id=1, source_target_pairs={{0,2},{1,3},{2,0},{3,1},{4,6},{5,7},{6,4},{7,5},{8,10},{9,11},{10,... | collective-permute-start | bytes 2359304 | tf_op jit(solution)/shard_map/ppermute | solution.py:301
  23.0 5.2 %copy-start.7 = (f32[8,192,128]{2,1,0:T(8,128)}, f32[8,192,128]{2,1,0:T(8,128)S(1)}, u32[]{:S(2)}) copy-start(f32[8,192,128]{2,1,0:T(8,128)S(1)} %collective-permute-done.1.refs_3_) | copy-start | bytes 2359300
  23.0 28.8 %collective-permute-start.4 = (f32[8,192,128]{2,1,0:T(8,128)S(1)}, f32[8,192,128]{2,1,0:T(8,128)S(1)}, u32[]{:S(2)}, u32[]{:S(2)}) collective-permute-start(f32[8,192,128]{2,1,0:T(8,128)S(1)} %collective-permute-done.1.refs_3_), channel_id=1, source_target_pairs={{8,4},{4,8},{9,5},{5,9},{10,6},{6,10},{11,7},{7,11},{24,20},{20,24... | collective-permute-start | bytes 2359304 | tf_op jit(solution)/shard_map/ppermute | solution.py:279
  23.7 29.7 %collective-permute-start.3 = (f32[8,192,128]{2,1,0:T(8,128)}, f32[8,192,128]{2,1,0:T(8,128)S(1)}, u32[]{:S(2)}, u32[]{:S(2)}) collective-permute-start(f32[8,192,128]{2,1,0:T(8,128)} %collective-permute-done.2.refs_5_), channel_id=1, source_target_pairs={{4,0},{8,12},{5,1},{9,13},{6,2},{10,14},{7,3},{11,15},{20,16},{24,... | collective-permute-start | bytes 2359304 | tf_op jit(solution)/shard_map/ppermute | solution.py:279
  28.2 96.0 %collective-permute-start.6 = (f32[384,2048]{1,0:T(8,128)}, f32[384,2048]{1,0:T(8,128)}, u32[]{:S(2)}, u32[]{:S(2)}) collective-permute-start(f32[384,2048]{1,0:T(8,128)} %bitcast.24.refs_0_), channel_id=1, source_target_pairs={{0,1},{1,0},{2,3},{3,2},{4,5},{5,4},{6,7},{7,6},{8,9},{9,8},{10,11... | collective-permute-start | bytes 9437192 | tf_op jit(solution)/shard_map/ppermute | solution.py:337
  45.5 85.1 %copy-start.3 = (f32[8,192,128]{2,1,0:T(8,128)}, f32[8,192,128]{2,1,0:T(8,128)S(1)}, u32[]{:S(2)}) copy-start(f32[8,192,128]{2,1,0:T(8,128)S(1)} %collective-permute-done.19.refs_4_) | copy-start | bytes 2359300
  45.5 78.8 %collective-permute-start.14 = (f32[384,2048]{1,0:T(8,128)}, f32[384,2048]{1,0:T(8,128)}, u32[]{:S(2)}, u32[]{:S(2)}) collective-permute-start(f32[384,2048]{1,0:T(8,128)} %bitcast.24.refs_0_), channel_id=1, source_target_pairs={{0,2},{1,3},{2,0},{3,1},{4,6},{5,7},{6,4},{7,5},{8,10},{9,11},{10,... | collective-permute-start | bytes 9437192 | tf_op jit(solution)/shard_map/ppermute | solution.py:337
  48.4 21.7 %collective-permute-start.9 = (f32[8,192,128]{2,1,0:T(8,128)S(1)}, f32[8,192,128]{2,1,0:T(8,128)S(1)}, u32[]{:S(2)}, u32[]{:S(2)}) collective-permute-start(f32[8,192,128]{2,1,0:T(8,128)S(1)} %collective-permute-done.8.refs_2_), channel_id=1, source_target_pairs={{4,0},{0,4},{12,8},{8,12},{5,1},{1,5},{13,9},{9,13},{6,2},{2,6},{1... | collective-permute-start | bytes 2359304 | tf_op jit(solution)/shard_map/ppermute | solution.py:279
  51.7 20.4 %collective-permute-start.10 = (f32[8,192,128]{2,1,0:T(8,128)S(1)}, f32[8,192,128]{2,1,0:T(8,128)S(1)}, u32[]{:S(2)}, u32[]{:S(2)}) collective-permute-start(f32[8,192,128]{2,1,0:T(8,128)S(1)} %collective-permute-done.8.refs_2_), channel_id=1, source_target_pairs={{8,4},{4,8},{9,5},{5,9},{10,6},{6,10},{11,7},{7,11},{24,20},{20,24... | collective-permute-start | bytes 2359304 | tf_op jit(solution)/shard_map/ppermute | solution.py:279
  52.5 0.9 copy-start.5
  53.4 0.9 copy-start.17
  54.3 32.7 %collective-permute-start.20 = (f32[8,192,128]{2,1,0:T(8,128)S(1)}, f32[8,192,128]{2,1,0:T(8,128)S(1)}, u32[]{:S(2)}, u32[]{:S(2)}) collective-permute-start(f32[8,192,128]{2,1,0:T(8,128)S(1)} %collective-permute-done.19.refs_4_), channel_id=1, source_target_pairs={{4,0},{0,4},{12,8},{8,12},{5,1},{1,5},{13,9},{9,13},{6,2},{2,6},{1... | collective-permute-start | bytes 2359304 | tf_op jit(solution)/shard_map/ppermute | solution.py:279
  70.1 28.4 %collective-permute-start.23 = (f32[8,192,128]{2,1,0:T(8,128)S(1)}, f32[8,192,128]{2,1,0:T(8,128)S(1)}, u32[]{:S(2)}, u32[]{:S(2)}) collective-permute-start(f32[8,192,128]{2,1,0:T(8,128)S(1)} %collective-permute-done.22.refs_2_), channel_id=1, source_target_pairs={{4,0},{0,4},{12,8},{8,12},{5,1},{1,5},{13,9},{9,13},{6,2},{2,6},{1... | collective-permute-start | bytes 2359304 | tf_op jit(solution)/shard_map/ppermute | solution.py:279
  72.2 26.4 %collective-permute-start.24 = (f32[8,192,128]{2,1,0:T(8,128)S(1)}, f32[8,192,128]{2,1,0:T(8,128)S(1)}, u32[]{:S(2)}, u32[]{:S(2)}) collective-permute-start(f32[8,192,128]{2,1,0:T(8,128)S(1)} %collective-permute-done.22.refs_2_), channel_id=1, source_target_pairs={{8,4},{4,8},{9,5},{5,9},{10,6},{6,10},{11,7},{7,11},{24,20},{20,24... | collective-permute-start | bytes 2359304 | tf_op jit(solution)/shard_map/ppermute | solution.py:279
  87.0 43.6 %copy-start.13 = (f32[8,192,128]{2,1,0:T(8,128)}, f32[8,192,128]{2,1,0:T(8,128)S(1)}, u32[]{:S(2)}) copy-start(f32[8,192,128]{2,1,0:T(8,128)S(1)} %collective-permute-done.20.refs_5_) | copy-start | bytes 2359300
  87.0 13.7 %collective-permute-start.28 = (f32[8,192,128]{2,1,0:T(8,128)S(1)}, f32[8,192,128]{2,1,0:T(8,128)S(1)}, u32[]{:S(2)}, u32[]{:S(2)}) collective-permute-start(f32[8,192,128]{2,1,0:T(8,128)S(1)} %collective-permute-done.19.refs_4_), channel_id=1, source_target_pairs={{8,4},{4,8},{9,5},{5,9},{10,6},{6,10},{11,7},{7,11},{24,20},{20,24... | collective-permute-start | bytes 2359304 | tf_op jit(solution)/shard_map/ppermute | solution.py:279
  98.5 32.0 %copy-start.9 = (f32[8,192,128]{2,1,0:T(8,128)}, f32[8,192,128]{2,1,0:T(8,128)S(1)}, u32[]{:S(2)}) copy-start(f32[8,192,128]{2,1,0:T(8,128)S(1)} %collective-permute-done.23.refs_3_) | copy-start | bytes 2359300
  98.5 56.9 %collective-permute-start = (f32[384,2048]{1,0:T(8,128)}, f32[384,2048]{1,0:T(8,128)}, u32[]{:S(2)}, u32[]{:S(2)}) collective-permute-start(f32[384,2048]{1,0:T(8,128)} %bitcast.24.refs_0_), channel_id=1, source_target_pairs={{0,16},{16,0},{1,17},{17,1},{2,18},{18,2},{3,19},{19,3},{4,20},{20... | collective-permute-start | bytes 9437192 | tf_op jit(solution)/shard_map/ppermute | solution.py:350
  98.5 32.0 %copy-start.11 = (f32[8,192,128]{2,1,0:T(8,128)}, f32[8,192,128]{2,1,0:T(8,128)S(1)}, u32[]{:S(2)}) copy-start(f32[8,192,128]{2,1,0:T(8,128)S(1)} %collective-permute-done.24.refs_5_) | copy-start | bytes 2359300
  98.5 21.8 %collective-permute-start.5 = (f32[8,192,128]{2,1,0:T(8,128)S(1)}, f32[8,192,128]{2,1,0:T(8,128)S(1)}, u32[]{:S(2)}, u32[]{:S(2)}) collective-permute-start(f32[8,192,128]{2,1,0:T(8,128)S(1)} %collective-permute-done.4.refs_7_), channel_id=1, source_target_pairs={{4,0},{8,12},{5,1},{9,13},{6,2},{10,14},{7,3},{11,15},{20,16},{24,... | collective-permute-start | bytes 2359304 | tf_op jit(solution)/shard_map/ppermute | solution.py:279
  100.7 22.7 %collective-permute-start.12 = (f32[8,192,128]{2,1,0:T(8,128)S(1)}, f32[8,192,128]{2,1,0:T(8,128)S(1)}, u32[]{:S(2)}, u32[]{:S(2)}) collective-permute-start(f32[8,192,128]{2,1,0:T(8,128)S(1)} %collective-permute-done.9.refs_3_), channel_id=1, source_target_pairs={{8,4},{4,8},{9,5},{5,9},{10,6},{6,10},{11,7},{7,11},{24,20},{20,24... | collective-permute-start | bytes 2359304 | tf_op jit(solution)/shard_map/ppermute | solution.py:279
  101.4 0.9 copy-start.19
  121.2 21.0 %collective-permute-start.11 = (f32[8,192,128]{2,1,0:T(8,128)S(1)}, f32[8,192,128]{2,1,0:T(8,128)S(1)}, u32[]{:S(2)}, u32[]{:S(2)}) collective-permute-start(f32[8,192,128]{2,1,0:T(8,128)S(1)} %collective-permute-done.10.refs_5_), channel_id=1, source_target_pairs={{4,0},{8,12},{5,1},{9,13},{6,2},{10,14},{7,3},{11,15},{20,16},{24,... | collective-permute-start | bytes 2359304 | tf_op jit(solution)/shard_map/ppermute | solution.py:279
  122.5 0.9 copy-start.21
  123.4 0.9 copy-start.25
  123.4 21.2 %collective-permute-start.26 = (f32[8,192,128]{2,1,0:T(8,128)S(1)}, f32[8,192,128]{2,1,0:T(8,128)S(1)}, u32[]{:S(2)}, u32[]{:S(2)}) collective-permute-start(f32[8,192,128]{2,1,0:T(8,128)S(1)} %collective-permute-done.23.refs_3_), channel_id=1, source_target_pairs={{8,4},{4,8},{9,5},{5,9},{10,6},{6,10},{11,7},{7,11},{24,20},{20,24... | collective-permute-start | bytes 2359304 | tf_op jit(solution)/shard_map/ppermute | solution.py:279
  124.2 81.4 %collective-permute-start.7 = (f32[384,2048]{1,0:T(8,128)}, f32[384,2048]{1,0:T(8,128)}, u32[]{:S(2)}, u32[]{:S(2)}) collective-permute-start(f32[384,2048]{1,0:T(8,128)} %collective-permute-done.6.refs_0_), channel_id=1, source_target_pairs={{0,16},{16,0},{1,17},{17,1},{2,18},{18,2},{3,19},{19,3},{4,20},{20... | collective-permute-start | bytes 9437192 | tf_op jit(solution)/shard_map/ppermute | solution.py:350
  124.3 20.8 %collective-permute-start.30 = (f32[8,192,128]{2,1,0:T(8,128)S(1)}, f32[8,192,128]{2,1,0:T(8,128)S(1)}, u32[]{:S(2)}, u32[]{:S(2)}) collective-permute-start(f32[8,192,128]{2,1,0:T(8,128)S(1)} %collective-permute-done.20.refs_5_), channel_id=1, source_target_pairs={{8,4},{4,8},{9,5},{5,9},{10,6},{6,10},{11,7},{7,11},{24,20},{20,24... | collective-permute-start | bytes 2359304 | tf_op jit(solution)/shard_map/ppermute | solution.py:279
  142.2 0.9 copy-start.27
  143.1 35.4 %collective-permute-start.15 = (f32[192,2048]{1,0:T(8,128)}, f32[192,2048]{1,0:T(8,128)}, u32[]{:S(2)}, u32[]{:S(2)}) collective-permute-start(f32[192,2048]{1,0:T(8,128)} %slice.26), channel_id=1, source_target_pairs={{0,1},{1,0},{2,3},{3,2},{4,5},{5,4},{6,7},{7,6},{8,9},{9,8},{10,11... | collective-permute-start | bytes 4718600 | tf_op jit(solution)/shard_map/ppermute | solution.py:341
  144.6 0.9 copy-start.23
  144.6 35.1 %collective-permute-start.16 = (f32[192,2048]{1,0:T(8,128)}, f32[192,2048]{1,0:T(8,128)}, u32[]{:S(2)}, u32[]{:S(2)}) collective-permute-start(f32[192,2048]{1,0:T(8,128)} %slice.27), channel_id=1, source_target_pairs={{0,2},{1,3},{2,0},{3,1},{4,6},{5,7},{6,4},{7,5},{8,10},{9,11},{10,... | collective-permute-start | bytes 4718600 | tf_op jit(solution)/shard_map/ppermute | solution.py:342
  145.5 99.7 %collective-permute-start.21 = (f32[384,2048]{1,0:T(8,128)}, f32[384,2048]{1,0:T(8,128)}, u32[]{:S(2)}, u32[]{:S(2)}) collective-permute-start(f32[384,2048]{1,0:T(8,128)} %collective-permute-done.14.refs_0_), channel_id=1, source_target_pairs={{0,16},{16,0},{1,17},{17,1},{2,18},{18,2},{3,19},{19,3},{4,20},{20... | collective-permute-start | bytes 9437192 | tf_op jit(solution)/shard_map/ppermute | solution.py:350
  145.5 3.4 %copy-start.2 = (f32[8,128,16,128]{3,2,1,0:T(8,128)S(1)}, f32[8,128,16,128]{3,2,1,0:T(8,128)}, u32[]{:S(2)}) copy-start(f32[8,128,16,128]{3,2,1,0:T(8,128)} %param.3) | copy-start | bytes 25165828
  151.7 3.4 %copy-start = (f32[1024,2048]{1,0:T(8,128)}, f32[1024,2048]{1,0:T(8,128)S(1)}, u32[]{:S(2)}) copy-start(f32[1024,2048]{1,0:T(8,128)S(1)} %fold.1.acc_ref) | copy-start | bytes 25165828
  155.4 48.7 %copy-start.12 = (f32[8,192,128]{2,1,0:T(8,128)S(1)}, f32[8,192,128]{2,1,0:T(8,128)}, u32[]{:S(2)}) copy-start(f32[8,192,128]{2,1,0:T(8,128)} %copy-done.11) | copy-start | bytes 2359300
  155.4 51.4 %copy-start.6 = (f32[8,192,128]{2,1,0:T(8,128)S(1)}, f32[8,192,128]{2,1,0:T(8,128)}, u32[]{:S(2)}) copy-start(f32[8,192,128]{2,1,0:T(8,128)} %copy-done.5) | copy-start | bytes 2359300
  155.5 48.6 %collective-permute-start.13 = (f32[8,192,128]{2,1,0:T(8,128)}, f32[8,192,128]{2,1,0:T(8,128)S(1)}, u32[]{:S(2)}, u32[]{:S(2)}) collective-permute-start(f32[8,192,128]{2,1,0:T(8,128)} %copy-done.25), channel_id=1, source_target_pairs={{4,0},{8,12},{5,1},{9,13},{6,2},{10,14},{7,3},{11,15},{20,16},{24,... | collective-permute-start | bytes 2359304 | tf_op jit(solution)/shard_map/ppermute | solution.py:279
  178.5 44.5 %collective-permute-start.17 = (f32[192,2048]{1,0:T(8,128)}, f32[192,2048]{1,0:T(8,128)S(1)}, u32[]{:S(2)}, u32[]{:S(2)}) collective-permute-start(f32[192,2048]{1,0:T(8,128)} %collective-permute-done.15.refs_0_), channel_id=1, source_target_pairs={{0,16},{16,0},{1,17},{17,1},{2,18},{18,2},{3,19},{19,3},{4,20},{20... | collective-permute-start | bytes 4718600 | tf_op jit(solution)/shard_map/ppermute | solution.py:350
  179.7 44.7 %collective-permute-start.18 = (f32[192,2048]{1,0:T(8,128)}, f32[192,2048]{1,0:T(8,128)S(1)}, u32[]{:S(2)}, u32[]{:S(2)}) collective-permute-start(f32[192,2048]{1,0:T(8,128)} %collective-permute-done.16.refs_1_), channel_id=1, source_target_pairs={{0,16},{16,0},{1,17},{17,1},{2,18},{18,2},{3,19},{19,3},{4,20},{20... | collective-permute-start | bytes 4718600 | tf_op jit(solution)/shard_map/ppermute | solution.py:350
  179.7 3.4 %copy-start.1 = (f32[1024,2048]{1,0:T(8,128)S(1)}, f32[1024,2048]{1,0:T(8,128)}, u32[]{:S(2)}) copy-start(f32[1024,2048]{1,0:T(8,128)} %copy-done) | copy-start | bytes 25165828
  183.1 1.1 copy-start.8
  184.3 1.1 copy-start.16
  185.4 1.1 copy-start.18
  186.5 1.1 copy-start.30
  187.7 17.9 %copy-start.24 = (f32[8,192,128]{2,1,0:T(8,128)S(1)}, f32[8,192,128]{2,1,0:T(8,128)}, u32[]{:S(2)}) copy-start(f32[8,192,128]{2,1,0:T(8,128)} %copy-done.23) | copy-start | bytes 2359300
  187.7 19.2 %copy-start.20 = (f32[8,192,128]{2,1,0:T(8,128)S(1)}, f32[8,192,128]{2,1,0:T(8,128)}, u32[]{:S(2)}) copy-start(f32[8,192,128]{2,1,0:T(8,128)} %copy-done.19) | copy-start | bytes 2359300
  187.7 19.2 %copy-start.22 = (f32[8,192,128]{2,1,0:T(8,128)S(1)}, f32[8,192,128]{2,1,0:T(8,128)}, u32[]{:S(2)}) copy-start(f32[8,192,128]{2,1,0:T(8,128)} %copy-done.21) | copy-start | bytes 2359300
  187.7 19.2 %copy-start.26 = (f32[8,192,128]{2,1,0:T(8,128)S(1)}, f32[8,192,128]{2,1,0:T(8,128)}, u32[]{:S(2)}) copy-start(f32[8,192,128]{2,1,0:T(8,128)} %copy-done.25) | copy-start | bytes 2359300
  187.7 19.2 %copy-start.28 = (f32[8,192,128]{2,1,0:T(8,128)S(1)}, f32[8,192,128]{2,1,0:T(8,128)}, u32[]{:S(2)}) copy-start(f32[8,192,128]{2,1,0:T(8,128)} %copy-done.27) | copy-start | bytes 2359300
  204.0 21.7 %copy-start.4 = (f32[8,192,128]{2,1,0:T(8,128)S(1)}, f32[8,192,128]{2,1,0:T(8,128)}, u32[]{:S(2)}) copy-start(f32[8,192,128]{2,1,0:T(8,128)} %copy-done.3) | copy-start | bytes 2359300
  204.1 21.7 %copy-start.14 = (f32[8,192,128]{2,1,0:T(8,128)S(1)}, f32[8,192,128]{2,1,0:T(8,128)}, u32[]{:S(2)}) copy-start(f32[8,192,128]{2,1,0:T(8,128)} %copy-done.13) | copy-start | bytes 2359300
  204.1 37.7 %collective-permute-start.25 = (f32[8,192,128]{2,1,0:T(8,128)S(1)}, f32[8,192,128]{2,1,0:T(8,128)S(1)}, u32[]{:S(2)}, u32[]{:S(2)}) collective-permute-start(f32[8,192,128]{2,1,0:T(8,128)S(1)} %copy-done.12), channel_id=1, source_target_pairs={{4,0},{8,12},{5,1},{9,13},{6,2},{10,14},{7,3},{11,15},{20,16},{24,... | collective-permute-start | bytes 2359304 | tf_op jit(solution)/shard_map/ppermute | solution.py:279
  205.5 38.3 %collective-permute-start.27 = (f32[8,192,128]{2,1,0:T(8,128)S(1)}, f32[8,192,128]{2,1,0:T(8,128)S(1)}, u32[]{:S(2)}, u32[]{:S(2)}) collective-permute-start(f32[8,192,128]{2,1,0:T(8,128)S(1)} %copy-done.24), channel_id=1, source_target_pairs={{4,0},{8,12},{5,1},{9,13},{6,2},{10,14},{7,3},{11,15},{20,16},{24,... | collective-permute-start | bytes 2359304 | tf_op jit(solution)/shard_map/ppermute | solution.py:279
  223.0 22.3 %copy-start.10 = (f32[8,192,128]{2,1,0:T(8,128)S(1)}, f32[8,192,128]{2,1,0:T(8,128)}, u32[]{:S(2)}) copy-start(f32[8,192,128]{2,1,0:T(8,128)} %copy-done.9) | copy-start | bytes 2359300
  223.0 38.4 %collective-permute-start.29 = (f32[8,192,128]{2,1,0:T(8,128)S(1)}, f32[8,192,128]{2,1,0:T(8,128)S(1)}, u32[]{:S(2)}, u32[]{:S(2)}) collective-permute-start(f32[8,192,128]{2,1,0:T(8,128)S(1)} %collective-permute-done.28.refs_1_), channel_id=1, source_target_pairs={{4,0},{8,12},{5,1},{9,13},{6,2},{10,14},{7,3},{11,15},{20,16},{24,... | collective-permute-start | bytes 2359304 | tf_op jit(solution)/shard_map/ppermute | solution.py:279
  224.4 44.6 %collective-permute-start.31 = (f32[4,192,128]{2,1,0:T(8,128)S(1)}, f32[4,192,128]{2,1,0:T(8,128)S(1)}, u32[]{:S(2)}, u32[]{:S(2)}) collective-permute-start(f32[4,192,128]{2,1,0:T(8,128)S(1)} %slice.28), channel_id=1, source_target_pairs={{4,0},{8,12},{5,1},{9,13},{6,2},{10,14},{7,3},{11,15},{20,16},{24,... | collective-permute-start | bytes 1179656 | tf_op jit(solution)/shard_map/ppermute | solution.py:277
  241.8 32.4 %collective-permute-start.32 = (f32[2,192,128]{2,1,0:T(8,128)S(1)}, f32[2,192,128]{2,1,0:T(8,128)S(1)}, u32[]{:S(2)}, u32[]{:S(2)}) collective-permute-start(f32[2,192,128]{2,1,0:T(8,128)S(1)} %get-tuple-element.32), channel_id=1, source_target_pairs={{4,0},{8,12},{5,1},{9,13},{6,2},{10,14},{7,3},{11,15},{20,16},{24,... | collective-permute-start | bytes 589832 | tf_op jit(solution)/shard_map/ppermute | solution.py:277
  243.8 33.9 %collective-permute-start.33 = (f32[2,192,128]{2,1,0:T(8,128)S(1)}, f32[2,192,128]{2,1,0:T(8,128)S(1)}, u32[]{:S(2)}, u32[]{:S(2)}) collective-permute-start(f32[2,192,128]{2,1,0:T(8,128)S(1)} %get-tuple-element.31), channel_id=1, source_target_pairs={{4,0},{8,12},{5,1},{9,13},{6,2},{10,14},{7,3},{11,15},{20,16},{24,... | collective-permute-start | bytes 589832 | tf_op jit(solution)/shard_map/ppermute | solution.py:277
  (2 other events, 1.8 us)

commit v3 on v2

--- a/solution.py
+++ b/solution.py
@@ -212,12 +212,15 @@
     parts = [split(buffer[step * row_blocks + block].T) for block in range(row_blocks)]
     left_high = jnp.concatenate([part[0] for part in parts], axis=0)
     left_low = jnp.concatenate([part[1] for part in parts], axis=0)
+    left_both = jnp.concatenate([left_high, left_low], axis=0)
     pivots = pl.ds(pl.multiple_of(scalars[0] * width, width), width)
     mine = pl.ds(pl.multiple_of(base + step * rows, rows), rows)
     pair = min(blocks, 2)
     for block in range(0, blocks, pair):
         lanes = pl.ds(block * LANES, pair * LANES)
-        value = acc_ref[mine, lanes] - product(left_high, left_low, high_ref[pivots, lanes], low_ref[pivots, lanes])
+        both = jnp.dot(left_both, high_ref[pivots, lanes], preferred_element_type=jnp.float32)
+        rest = jnp.dot(left_high, low_ref[pivots, lanes], preferred_element_type=jnp.float32)
+        value = acc_ref[mine, lanes] - (both[:rows] + (both[rows:] + rest))
         for one in range(pair):
             out_ref[pl.ds(block + one, rows, stride=blocks), :] = value[:, one * LANES : (one + 1) * LANES]
 
@@ -300,7 +303,7 @@
     groups += [group(target(kk, m)) for m in order[2:]]
     pieces = [groups[0] if m == 0 else lax.ppermute(groups[i], "kk", pairs(m)) for i, m in enumerate(order)]
 
-    tails = [row_blocks // n for n in (2, 4, 4)] if row_blocks % 4 == 0 and n_col > 2 else [row_blocks]
+    tails = [(row_blocks + 2 - n) // 3 for n in range(3)] if row_blocks > 2 and n_col > 2 else [row_blocks]
     streams = [line(piece, "col", n_col, tails if i == n_kk - 1 else ()) for i, piece in enumerate(pieces)]
     even = col % 2 == 0
     length = jnp.where(even, n_col - 1 - col, col)

time: 282 us -> 282 us (level)
  transfers between devices with their start and end apart: 34 -> 34, of which waited for: 12 -> 13; matrix products, arithmetic and copies ran while one was open for 4% -> 4% of each run, Pallas kernels for 29% -> 29%
where the time goes in v3:
time: 282 us; the launch traced here: 281 us
  waiting for transfers between devices  124 us (44%)
  Pallas kernels  84.1 us (30%)
  starting transfers between devices  37.6 us (13%)
  local copies, waits for them, and re-layouts  34.4 us (12%)
    ppermute x19, waiting for transfers between devices, line(): new[odd] = lax.ppermute(what, axis, pairs)  80.5 us
    pallas_call x4, Pallas kernels, add(): pl.pallas_call(functools.partial(add_kernel, [len(slot) for slot in slots...  64.5 us
    ppermute x19, starting transfers between devices, line(): new[odd] = lax.ppermute(what, axis, pairs)  25.6 us
    unnamed x65, local copies, waits for them, and re-layouts  24.7 us
    ppermute x1, waiting for transfers between devices, local(): first = lax.ppermute(whole(parts[m ^ bits[0]])[:half], 'kk', pairs(bits[0]))  21.6 us
    ppermute x3, waiting for transfers between devices, local(): lax.ppermute(groups[i], 'kk', pairs(m))  18.1 us
    pallas_call x3, Pallas kernels, last(): pl.pallas_call(functools.partial(last_kernel, blocks, len(slot), first, f...  11.1 us
    pallas_call x1, Pallas kernels, one(): pl.pallas_call(functools.partial(one_kernel, len(slot)), out_shape=jax.Sh...  5.75 us
  transfers between devices with their start and end apart: 34, of which 13 were waited for; matrix products, arithmetic and copies ran while one was open for 4% of the time, Pallas kernels for 29%

profile of v3, /device:TPU:0, one launch (start us, length us, event | category | flops | bytes accessed | tf_op | source)
XLA Modules:
  0.0 280.7 jit_solution(6651692263966966711)
XLA Ops:
  0.0 2.4 dynamic-slice_bitcast_fusion.2
  2.4 3.1 %collective-permute-start.1 = (f32[8,192,128]{2,1,0:T(8,128)S(1)}, f32[8,192,128]{2,1,0:T(8,128)S(1)}, u32[]{:S(2)}, u32[]{:S(2)}) collective-permute-start(f32[8,192,128]{2,1,0:T(8,128)S(1)} %get-tuple-element.16.refs_2_), channel_id=1, source_target_pairs={{4,0},{0,4},{12,8},{8,12},{5,1},{1,5},{13,9},{9,13},{6,2},{2,6},{1... | collective-permute-start | bytes 2359304 | tf_op jit(solution)/shard_map/ppermute | solution.py:282
  5.5 1.6 collective-permute-start.2
  7.0 1.5 collective-permute-start.8
  8.5 1.6 dynamic-slice_bitcast_fusion
  10.1 1.6 collective-permute-start.19
  12.2 10.8 %collective-permute-done.1.refs_3_ = f32[8,192,128]{2,1,0:T(8,128)S(1)} collective-permute-done((f32[8,192,128]{2,1,0:T(8,128)S(1)}, f32[8,192,128]{2,1,0:T(8,128)S(1)}, u32[]{:S(2)}, u32[]{:S(2)}) %collective-permute-start.1) | collective-permute-done | bytes 786464 | tf_op jit(solution)/shard_map/ppermute | solution.py:282
  23.7 1.3 collective-permute-start.3
  25.0 3.1 %copy.16 = f32[48,8,16,128]{3,1,2,0:T(8,128)} copy(f32[48,8,16,128]{3,2,1,0:T(8,128)S(1)} %bitcast.28) | data formatting | bytes 6291456
  28.2 1.7 collective-permute-start.6
  29.8 15.7 %collective-permute-done.19.refs_4_ = f32[8,192,128]{2,1,0:T(8,128)S(1)} collective-permute-done((f32[8,192,128]{2,1,0:T(8,128)S(1)}, f32[8,192,128]{2,1,0:T(8,128)S(1)}, u32[]{:S(2)}, u32[]{:S(2)}) %collective-permute-start.19) | collective-permute-done | bytes 786464 | tf_op jit(solution)/shard_map/ppermute | solution.py:304
  46.0 2.4 collective-permute-done.22.refs_2_
  48.4 3.3 %collective-permute-start.9 = (f32[8,192,128]{2,1,0:T(8,128)S(1)}, f32[8,192,128]{2,1,0:T(8,128)S(1)}, u32[]{:S(2)}, u32[]{:S(2)}) collective-permute-start(f32[8,192,128]{2,1,0:T(8,128)S(1)} %collective-permute-done.8.refs_2_), channel_id=1, source_target_pairs={{4,0},{0,4},{12,8},{8,12},{5,1},{1,5},{13,9},{9,13},{6,2},{2,6},{1... | collective-permute-start | bytes 2359304 | tf_op jit(solution)/shard_map/ppermute | solution.py:282
  51.7 0.7 collective-permute-start.10
  52.5 0.9 copy-done.5
  53.4 0.9 copy-done.17
  54.3 1.5 collective-permute-start.20
  55.8 14.3 %collective-permute-done.9.refs_3_ = f32[8,192,128]{2,1,0:T(8,128)S(1)} collective-permute-done((f32[8,192,128]{2,1,0:T(8,128)S(1)}, f32[8,192,128]{2,1,0:T(8,128)S(1)}, u32[]{:S(2)}, u32[]{:S(2)}) %collective-permute-start.9) | collective-permute-done | bytes 786464 | tf_op jit(solution)/shard_map/ppermute | solution.py:282
  70.1 2.0 collective-permute-start.23
  72.2 0.7 collective-permute-start.24
  72.9 14.1 %collective-permute-done.20.refs_5_ = f32[8,192,128]{2,1,0:T(8,128)S(1)} collective-permute-done((f32[8,192,128]{2,1,0:T(8,128)S(1)}, f32[8,192,128]{2,1,0:T(8,128)S(1)}, u32[]{:S(2)}, u32[]{:S(2)}) %collective-permute-start.20) | collective-permute-done | bytes 786464 | tf_op jit(solution)/shard_map/ppermute | solution.py:282
  87.7 10.8 %collective-permute-done.23.refs_3_ = f32[8,192,128]{2,1,0:T(8,128)S(1)} collective-permute-done((f32[8,192,128]{2,1,0:T(8,128)S(1)}, f32[8,192,128]{2,1,0:T(8,128)S(1)}, u32[]{:S(2)}, u32[]{:S(2)}) %collective-permute-start.23) | collective-permute-done | bytes 786464 | tf_op jit(solution)/shard_map/ppermute | solution.py:282
  98.5 1.3 collective-permute-start.5
  99.8 0.9 copy-done.15
  100.7 0.7 collective-permute-start.12
  101.4 0.9 copy-done.19
  102.3 18.0 %collective-permute-done.5.refs_6_ = f32[8,192,128]{2,1,0:T(8,128)S(1)} collective-permute-done((f32[8,192,128]{2,1,0:T(8,128)S(1)}, f32[8,192,128]{2,1,0:T(8,128)S(1)}, u32[]{:S(2)}, u32[]{:S(2)}) %collective-permute-start.5) | collective-permute-done | bytes 786464 | tf_op jit(solution)/shard_map/ppermute | solution.py:282
  120.4 0.9 copy-done.29
  121.2 1.3 collective-permute-start.11
  122.5 0.9 copy-done.21
  123.4 0.7 collective-permute-start.26
  124.3 0.7 collective-permute-start.30
  125.0 2.7 slice.27
  127.7 2.8 slice.26
  130.6 11.6 %collective-permute-done.11.refs_4_ = f32[8,192,128]{2,1,0:T(8,128)S(1)} collective-permute-done((f32[8,192,128]{2,1,0:T(8,128)S(1)}, f32[8,192,128]{2,1,0:T(8,128)S(1)}, u32[]{:S(2)}, u32[]{:S(2)}) %collective-permute-start.11) | collective-permute-done | bytes 786464 | tf_op jit(solution)/shard_map/ppermute | solution.py:282
  142.2 0.9 copy-done.27
  143.1 1.5 collective-permute-start.15
  145.5 3.4 %copy-done.2 = f32[8,128,16,128]{3,2,1,0:T(8,128)S(1)} copy-done((f32[8,128,16,128]{3,2,1,0:T(8,128)S(1)}, f32[8,128,16,128]{3,2,1,0:T(8,128)}, u32[]{:S(2)}) %copy-start.2) | copy-done | bytes 8388632
  148.9 2.8 %fold.1.acc_ref = f32[1024,2048]{1,0:T(8,128)S(1)} custom-call(f32[16384,128]{1,0:T(8,128)S(1)} %bitcast.25), custom_call_target="tpu_custom_call" | custom-call | bytes 8388608 | tf_op jit(solution)/shard_map/fold/pallas_call | solution.py:139
  151.7 3.4 %copy-done = f32[1024,2048]{1,0:T(8,128)} copy-done((f32[1024,2048]{1,0:T(8,128)}, f32[1024,2048]{1,0:T(8,128)S(1)}, u32[]{:S(2)}) %copy-start) | copy-done | bytes 8388632
  155.5 1.4 collective-permute-start.13
  156.9 21.6 %collective-permute-done.15.refs_0_ = f32[192,2048]{1,0:T(8,128)} collective-permute-done((f32[192,2048]{1,0:T(8,128)}, f32[192,2048]{1,0:T(8,128)}, u32[]{:S(2)}, u32[]{:S(2)}) %collective-permute-start.15) | collective-permute-done | bytes 1572896 | tf_op jit(solution)/shard_map/ppermute | solution.py:344
  178.5 1.2 collective-permute-done.16.refs_1_
  179.7 3.4 %copy-done.1 = f32[1024,2048]{1,0:T(8,128)S(1)} copy-done((f32[1024,2048]{1,0:T(8,128)S(1)}, f32[1024,2048]{1,0:T(8,128)}, u32[]{:S(2)}) %copy-start.1) | copy-done | bytes 8388632
  183.1 1.1 copy-done.8
  184.3 1.1 copy-done.16
  185.4 1.1 copy-done.18
  186.5 1.1 copy-done.30
  187.7 16.4 %add.77.acc_ref = f32[1024,2048]{1,0:T(8,128)S(1)} custom-call(s32[8]{0:T(128)S(1)} %stack.49.scalars, f32[1024,2048]{1,0:T(8,128)S(1)} %copy-done.1, f32[384,2048]{1,0:T(8,128)} %bitcast.24.refs_0_, f32[384,2048]{1,0:T(8,128)} %collective-permute-done.refs_1_, f32[8,192,128]{2,1,0:T(8,128)S(1)} %get-tuple-element.16.refs_2_, ...), custom_call_target="tpu_custom_call", output_to_operand_aliasing={{}: (1, {})} | custom-call | flops 9663676416 | bytes 6291456 | tf_op jit(solution)/shard_map/add/pallas_call | solution.py:101
  204.1 1.4 collective-permute-start.25
  205.5 1.3 collective-permute-start.27
  206.9 16.1 %add.78.acc_ref = f32[1024,2048]{1,0:T(8,128)S(1)} custom-call(s32[8]{0:T(128)S(1)} %stack.49.scalars, f32[1024,2048]{1,0:T(8,128)S(1)} %add.77.acc_ref, f32[384,2048]{1,0:T(8,128)} %collective-permute-done.6.refs_0_, f32[384,2048]{1,0:T(8,128)} %collective-permute-done.7.refs_1_, f32[8,192,128]{2,1,0:T(8,128)S(1)} %copy-done.6, ...), custom_call_target="tpu_custom_call", output_to_operand_aliasing={{}: (1, {})} | custom-call | flops 9663676416 | bytes 6291456 | tf_op jit(solution)/shard_map/add/pallas_call | solution.py:101
  223.0 1.3 collective-permute-start.29
  224.3 1.4 collective-permute-start.31
  225.8 16.0 %add.79 = (f32[1024,2048]{1,0:T(8,128)S(1)}, bf16[768,2048]{1,0:T(8,128)(2,1)S(1)}, bf16[768,2048]{1,0:T(8,128)(2,1)S(1)}) custom-call(s32[8]{0:T(128)S(1)} %stack.49.scalars, f32[1024,2048]{1,0:T(8,128)S(1)} %add.78.acc_ref, f32[192,2048]{1,0:T(8,128)} %collective-permute-done.15.refs_0_, ...), custom_call_target="tpu_custom_call", output_to_operand_aliasing={{0}: (1, {})} | custom-call | flops 4831838208 | bytes 6291456 | tf_op jit(solution)/shard_map/add/pallas_call | solution.py:101
  241.8 1.3 collective-permute-start.32
  243.1 0.7 collective-permute-done.27.refs_6_
  243.8 1.5 collective-permute-start.33
  245.3 16.1 %add.80.acc_ref = f32[1024,2048]{1,0:T(8,128)S(1)} custom-call(s32[8]{0:T(128)S(1)} %stack.49.scalars, f32[1024,2048]{1,0:T(8,128)S(1)} %get-tuple-element.19.acc_ref, f32[384,2048]{1,0:T(8,128)} %collective-permute-done.14.refs_0_, f32[384,2048]{1,0:T(8,128)} %collective-permute-done.21.refs_1_, ...), custom_call_target="tpu_custom_call", output_to_operand_aliasing={{}: (1, {})} | custom-call | flops 9663676416 | bytes 6291456 | tf_op jit(solution)/shard_map/add/pallas_call | solution.py:101
  261.4 5.8 %one.1.acc_ref = f32[1024,2048]{1,0:T(8,128)S(1)} custom-call(s32[2]{0:T(128)S(1)} %pad_add_fusion.1.scalars, f32[1024,2048]{1,0:T(8,128)S(1)} %add.80.acc_ref, bf16[768,2048]{1,0:T(8,128)(2,1)S(1)} %get-tuple-element.20.high_ref, bf16[768,2048]{1,0:T(8,128)(2,1)S(1)} %get-tuple-element.21.low_ref, ...), custom_call_target="tpu_custom_call", output_to_operand_aliasing={{}: (1, {})} | custom-call | flops 2415919104 | bytes 786432 | tf_op jit(solution)/shard_map/one/pallas_call | solution.py:178
  267.2 3.9 %last.3 = (f32[16384,128]{1,0:T(8,128)}, f32[1024,2048]{1,0:T(8,128)S(1)}) custom-call(s32[2]{0:T(128)S(1)} %pad_add_fusion.scalars, f32[1024,2048]{1,0:T(8,128)S(1)} %one.1.acc_ref, bf16[768,2048]{1,0:T(8,128)(2,1)S(1)} %get-tuple-element.20.high_ref, bf16[768,2048]{1,0:T(8,128)(2,1)S(1)} %get-tuple-element.21.low_ref, ...), custom_call_target="tpu_custom_call", output_to_operand_aliasing={{1}: (1, {})} | custom-call | flops 905969664 | bytes 3145728 | tf_op jit(solution)/shard_map/last/pallas_call | solution.py:235
  271.1 2.2 collective-permute-done.32.refs_0_
  273.3 3.9 %last.4 = (f32[16384,128]{1,0:T(8,128)}, f32[1024,2048]{1,0:T(8,128)S(1)}) custom-call(s32[2]{0:T(128)S(1)} %pad_add_fusion.scalars, f32[1024,2048]{1,0:T(8,128)S(1)} %get-tuple-element.22.acc_ref, bf16[768,2048]{1,0:T(8,128)(2,1)S(1)} %get-tuple-element.20.high_ref, ...), custom_call_target="tpu_custom_call", output_to_operand_aliasing={{1}: (1, {}), {0}: (6, {})} | custom-call | flops 905969664 | bytes 3145728 | tf_op jit(solution)/shard_map/last/pallas_call | solution.py:235
  277.3 3.2 %last.5 = (f32[16384,128]{1,0:T(8,128)}, f32[1024,2048]{1,0:T(8,128)S(1)}) custom-call(s32[2]{0:T(128)S(1)} %pad_add_fusion.scalars, f32[1024,2048]{1,0:T(8,128)S(1)} %get-tuple-element.24.acc_ref, bf16[768,2048]{1,0:T(8,128)(2,1)S(1)} %get-tuple-element.20.high_ref, ...), custom_call_target="tpu_custom_call", output_to_operand_aliasing={{1}: (1, {}), {0}: (6, {})} | custom-call | flops 603979776 | bytes 2097152 | tf_op jit(solution)/shard_map/last/pallas_call | solution.py:235
  (87 shorter events, 4.0 us)
Async XLA Ops:
  2.4 20.6 %collective-permute-start.1 = (f32[8,192,128]{2,1,0:T(8,128)S(1)}, f32[8,192,128]{2,1,0:T(8,128)S(1)}, u32[]{:S(2)}, u32[]{:S(2)}) collective-permute-start(f32[8,192,128]{2,1,0:T(8,128)S(1)} %get-tuple-element.16.refs_2_), channel_id=1, source_target_pairs={{4,0},{0,4},{12,8},{8,12},{5,1},{1,5},{13,9},{9,13},{6,2},{2,6},{1... | collective-permute-start | bytes 2359304 | tf_op jit(solution)/shard_map/ppermute | solution.py:282
  5.5 18.2 %collective-permute-start.2 = (f32[8,192,128]{2,1,0:T(8,128)S(1)}, f32[8,192,128]{2,1,0:T(8,128)}, u32[]{:S(2)}, u32[]{:S(2)}) collective-permute-start(f32[8,192,128]{2,1,0:T(8,128)S(1)} %get-tuple-element.16.refs_2_), channel_id=1, source_target_pairs={{8,4},{4,8},{9,5},{5,9},{10,6},{6,10},{11,7},{7,11},{24,20},{20,24... | collective-permute-start | bytes 2359304 | tf_op jit(solution)/shard_map/ppermute | solution.py:282
  7.0 21.1 %collective-permute-start.8 = (f32[8,192,128]{2,1,0:T(8,128)}, f32[8,192,128]{2,1,0:T(8,128)S(1)}, u32[]{:S(2)}, u32[]{:S(2)}) collective-permute-start(f32[8,192,128]{2,1,0:T(8,128)} %get-tuple-element.17), channel_id=1, source_target_pairs={{0,1},{1,0},{2,3},{3,2},{4,5},{5,4},{6,7},{7,6},{8,9},{9,8},{10,11... | collective-permute-start | bytes 2359304 | tf_op jit(solution)/shard_map/ppermute | solution.py:304
  8.5 16.5 %copy-start.31 = (f32[1,384,16,128]{3,2,1,0:T(8,128)S(1)}, f32[1,384,16,128]{3,2,1,0:T(8,128)}, u32[]{:S(2)}) copy-start(f32[1,384,16,128]{3,2,1,0:T(8,128)} %param.5) | copy-start | bytes 9437188
  10.1 35.3 %collective-permute-start.19 = (f32[8,192,128]{2,1,0:T(8,128)S(1)}, f32[8,192,128]{2,1,0:T(8,128)S(1)}, u32[]{:S(2)}, u32[]{:S(2)}) collective-permute-start(f32[8,192,128]{2,1,0:T(8,128)S(1)} %get-tuple-element.28), channel_id=1, source_target_pairs={{0,3},{1,2},{2,1},{3,0},{4,7},{5,6},{6,5},{7,4},{8,11},{9,10},{10,... | collective-permute-start | bytes 2359304 | tf_op jit(solution)/shard_map/ppermute | solution.py:304
  11.7 36.7 %collective-permute-start.22 = (f32[8,192,128]{2,1,0:T(8,128)S(1)}, f32[8,192,128]{2,1,0:T(8,128)S(1)}, u32[]{:S(2)}, u32[]{:S(2)}) collective-permute-start(f32[8,192,128]{2,1,0:T(8,128)S(1)} %get-tuple-element.27), channel_id=1, source_target_pairs={{0,2},{1,3},{2,0},{3,1},{4,6},{5,7},{6,4},{7,5},{8,10},{9,11},{10,... | collective-permute-start | bytes 2359304 | tf_op jit(solution)/shard_map/ppermute | solution.py:304
  23.0 5.2 %copy-start.7 = (f32[8,192,128]{2,1,0:T(8,128)}, f32[8,192,128]{2,1,0:T(8,128)S(1)}, u32[]{:S(2)}) copy-start(f32[8,192,128]{2,1,0:T(8,128)S(1)} %collective-permute-done.1.refs_3_) | copy-start | bytes 2359300
  23.0 28.8 %collective-permute-start.4 = (f32[8,192,128]{2,1,0:T(8,128)S(1)}, f32[8,192,128]{2,1,0:T(8,128)S(1)}, u32[]{:S(2)}, u32[]{:S(2)}) collective-permute-start(f32[8,192,128]{2,1,0:T(8,128)S(1)} %collective-permute-done.1.refs_3_), channel_id=1, source_target_pairs={{8,4},{4,8},{9,5},{5,9},{10,6},{6,10},{11,7},{7,11},{24,20},{20,24... | collective-permute-start | bytes 2359304 | tf_op jit(solution)/shard_map/ppermute | solution.py:282
  23.7 29.7 %collective-permute-start.3 = (f32[8,192,128]{2,1,0:T(8,128)}, f32[8,192,128]{2,1,0:T(8,128)S(1)}, u32[]{:S(2)}, u32[]{:S(2)}) collective-permute-start(f32[8,192,128]{2,1,0:T(8,128)} %collective-permute-done.2.refs_5_), channel_id=1, source_target_pairs={{4,0},{8,12},{5,1},{9,13},{6,2},{10,14},{7,3},{11,15},{20,16},{24,... | collective-permute-start | bytes 2359304 | tf_op jit(solution)/shard_map/ppermute | solution.py:282
  28.2 96.0 %collective-permute-start.6 = (f32[384,2048]{1,0:T(8,128)}, f32[384,2048]{1,0:T(8,128)}, u32[]{:S(2)}, u32[]{:S(2)}) collective-permute-start(f32[384,2048]{1,0:T(8,128)} %bitcast.24.refs_0_), channel_id=1, source_target_pairs={{0,1},{1,0},{2,3},{3,2},{4,5},{5,4},{6,7},{7,6},{8,9},{9,8},{10,11... | collective-permute-start | bytes 9437192 | tf_op jit(solution)/shard_map/ppermute | solution.py:340
  45.5 85.1 %copy-start.3 = (f32[8,192,128]{2,1,0:T(8,128)}, f32[8,192,128]{2,1,0:T(8,128)S(1)}, u32[]{:S(2)}) copy-start(f32[8,192,128]{2,1,0:T(8,128)S(1)} %collective-permute-done.19.refs_4_) | copy-start | bytes 2359300
  45.5 78.8 %collective-permute-start.14 = (f32[384,2048]{1,0:T(8,128)}, f32[384,2048]{1,0:T(8,128)}, u32[]{:S(2)}, u32[]{:S(2)}) collective-permute-start(f32[384,2048]{1,0:T(8,128)} %bitcast.24.refs_0_), channel_id=1, source_target_pairs={{0,2},{1,3},{2,0},{3,1},{4,6},{5,7},{6,4},{7,5},{8,10},{9,11},{10,... | collective-permute-start | bytes 9437192 | tf_op jit(solution)/shard_map/ppermute | solution.py:340
  48.4 21.7 %collective-permute-start.9 = (f32[8,192,128]{2,1,0:T(8,128)S(1)}, f32[8,192,128]{2,1,0:T(8,128)S(1)}, u32[]{:S(2)}, u32[]{:S(2)}) collective-permute-start(f32[8,192,128]{2,1,0:T(8,128)S(1)} %collective-permute-done.8.refs_2_), channel_id=1, source_target_pairs={{4,0},{0,4},{12,8},{8,12},{5,1},{1,5},{13,9},{9,13},{6,2},{2,6},{1... | collective-permute-start | bytes 2359304 | tf_op jit(solution)/shard_map/ppermute | solution.py:282
  51.7 20.4 %collective-permute-start.10 = (f32[8,192,128]{2,1,0:T(8,128)S(1)}, f32[8,192,128]{2,1,0:T(8,128)S(1)}, u32[]{:S(2)}, u32[]{:S(2)}) collective-permute-start(f32[8,192,128]{2,1,0:T(8,128)S(1)} %collective-permute-done.8.refs_2_), channel_id=1, source_target_pairs={{8,4},{4,8},{9,5},{5,9},{10,6},{6,10},{11,7},{7,11},{24,20},{20,24... | collective-permute-start | bytes 2359304 | tf_op jit(solution)/shard_map/ppermute | solution.py:282
  52.5 0.9 copy-start.5
  53.4 0.9 copy-start.17
  54.3 32.7 %collective-permute-start.20 = (f32[8,192,128]{2,1,0:T(8,128)S(1)}, f32[8,192,128]{2,1,0:T(8,128)S(1)}, u32[]{:S(2)}, u32[]{:S(2)}) collective-permute-start(f32[8,192,128]{2,1,0:T(8,128)S(1)} %collective-permute-done.19.refs_4_), channel_id=1, source_target_pairs={{4,0},{0,4},{12,8},{8,12},{5,1},{1,5},{13,9},{9,13},{6,2},{2,6},{1... | collective-permute-start | bytes 2359304 | tf_op jit(solution)/shard_map/ppermute | solution.py:282
  70.1 28.4 %collective-permute-start.23 = (f32[8,192,128]{2,1,0:T(8,128)S(1)}, f32[8,192,128]{2,1,0:T(8,128)S(1)}, u32[]{:S(2)}, u32[]{:S(2)}) collective-permute-start(f32[8,192,128]{2,1,0:T(8,128)S(1)} %collective-permute-done.22.refs_2_), channel_id=1, source_target_pairs={{4,0},{0,4},{12,8},{8,12},{5,1},{1,5},{13,9},{9,13},{6,2},{2,6},{1... | collective-permute-start | bytes 2359304 | tf_op jit(solution)/shard_map/ppermute | solution.py:282
  72.2 26.4 %collective-permute-start.24 = (f32[8,192,128]{2,1,0:T(8,128)S(1)}, f32[8,192,128]{2,1,0:T(8,128)S(1)}, u32[]{:S(2)}, u32[]{:S(2)}) collective-permute-start(f32[8,192,128]{2,1,0:T(8,128)S(1)} %collective-permute-done.22.refs_2_), channel_id=1, source_target_pairs={{8,4},{4,8},{9,5},{5,9},{10,6},{6,10},{11,7},{7,11},{24,20},{20,24... | collective-permute-start | bytes 2359304 | tf_op jit(solution)/shard_map/ppermute | solution.py:282
  87.0 43.6 %copy-start.13 = (f32[8,192,128]{2,1,0:T(8,128)}, f32[8,192,128]{2,1,0:T(8,128)S(1)}, u32[]{:S(2)}) copy-start(f32[8,192,128]{2,1,0:T(8,128)S(1)} %collective-permute-done.20.refs_5_) | copy-start | bytes 2359300
  87.0 13.7 %collective-permute-start.28 = (f32[8,192,128]{2,1,0:T(8,128)S(1)}, f32[8,192,128]{2,1,0:T(8,128)S(1)}, u32[]{:S(2)}, u32[]{:S(2)}) collective-permute-start(f32[8,192,128]{2,1,0:T(8,128)S(1)} %collective-permute-done.19.refs_4_), channel_id=1, source_target_pairs={{8,4},{4,8},{9,5},{5,9},{10,6},{6,10},{11,7},{7,11},{24,20},{20,24... | collective-permute-start | bytes 2359304 | tf_op jit(solution)/shard_map/ppermute | solution.py:282
  98.5 32.0 %copy-start.9 = (f32[8,192,128]{2,1,0:T(8,128)}, f32[8,192,128]{2,1,0:T(8,128)S(1)}, u32[]{:S(2)}) copy-start(f32[8,192,128]{2,1,0:T(8,128)S(1)} %collective-permute-done.23.refs_3_) | copy-start | bytes 2359300
  98.5 56.9 %collective-permute-start = (f32[384,2048]{1,0:T(8,128)}, f32[384,2048]{1,0:T(8,128)}, u32[]{:S(2)}, u32[]{:S(2)}) collective-permute-start(f32[384,2048]{1,0:T(8,128)} %bitcast.24.refs_0_), channel_id=1, source_target_pairs={{0,16},{16,0},{1,17},{17,1},{2,18},{18,2},{3,19},{19,3},{4,20},{20... | collective-permute-start | bytes 9437192 | tf_op jit(solution)/shard_map/ppermute | solution.py:353
  98.5 32.0 %copy-start.11 = (f32[8,192,128]{2,1,0:T(8,128)}, f32[8,192,128]{2,1,0:T(8,128)S(1)}, u32[]{:S(2)}) copy-start(f32[8,192,128]{2,1,0:T(8,128)S(1)} %collective-permute-done.24.refs_5_) | copy-start | bytes 2359300
  98.5 21.8 %collective-permute-start.5 = (f32[8,192,128]{2,1,0:T(8,128)S(1)}, f32[8,192,128]{2,1,0:T(8,128)S(1)}, u32[]{:S(2)}, u32[]{:S(2)}) collective-permute-start(f32[8,192,128]{2,1,0:T(8,128)S(1)} %collective-permute-done.4.refs_7_), channel_id=1, source_target_pairs={{4,0},{8,12},{5,1},{9,13},{6,2},{10,14},{7,3},{11,15},{20,16},{24,... | collective-permute-start | bytes 2359304 | tf_op jit(solution)/shard_map/ppermute | solution.py:282
  100.7 22.7 %collective-permute-start.12 = (f32[8,192,128]{2,1,0:T(8,128)S(1)}, f32[8,192,128]{2,1,0:T(8,128)S(1)}, u32[]{:S(2)}, u32[]{:S(2)}) collective-permute-start(f32[8,192,128]{2,1,0:T(8,128)S(1)} %collective-permute-done.9.refs_3_), channel_id=1, source_target_pairs={{8,4},{4,8},{9,5},{5,9},{10,6},{6,10},{11,7},{7,11},{24,20},{20,24... | collective-permute-start | bytes 2359304 | tf_op jit(solution)/shard_map/ppermute | solution.py:282
  101.4 0.9 copy-start.19
  121.2 21.0 %collective-permute-start.11 = (f32[8,192,128]{2,1,0:T(8,128)S(1)}, f32[8,192,128]{2,1,0:T(8,128)S(1)}, u32[]{:S(2)}, u32[]{:S(2)}) collective-permute-start(f32[8,192,128]{2,1,0:T(8,128)S(1)} %collective-permute-done.10.refs_5_), channel_id=1, source_target_pairs={{4,0},{8,12},{5,1},{9,13},{6,2},{10,14},{7,3},{11,15},{20,16},{24,... | collective-permute-start | bytes 2359304 | tf_op jit(solution)/shard_map/ppermute | solution.py:282
  122.5 0.9 copy-start.21
  123.4 0.9 copy-start.25
  123.4 21.2 %collective-permute-start.26 = (f32[8,192,128]{2,1,0:T(8,128)S(1)}, f32[8,192,128]{2,1,0:T(8,128)S(1)}, u32[]{:S(2)}, u32[]{:S(2)}) collective-permute-start(f32[8,192,128]{2,1,0:T(8,128)S(1)} %collective-permute-done.23.refs_3_), channel_id=1, source_target_pairs={{8,4},{4,8},{9,5},{5,9},{10,6},{6,10},{11,7},{7,11},{24,20},{20,24... | collective-permute-start | bytes 2359304 | tf_op jit(solution)/shard_map/ppermute | solution.py:282
  124.2 81.4 %collective-permute-start.7 = (f32[384,2048]{1,0:T(8,128)}, f32[384,2048]{1,0:T(8,128)}, u32[]{:S(2)}, u32[]{:S(2)}) collective-permute-start(f32[384,2048]{1,0:T(8,128)} %collective-permute-done.6.refs_0_), channel_id=1, source_target_pairs={{0,16},{16,0},{1,17},{17,1},{2,18},{18,2},{3,19},{19,3},{4,20},{20... | collective-permute-start | bytes 9437192 | tf_op jit(solution)/shard_map/ppermute | solution.py:353
  124.3 20.8 %collective-permute-start.30 = (f32[8,192,128]{2,1,0:T(8,128)S(1)}, f32[8,192,128]{2,1,0:T(8,128)S(1)}, u32[]{:S(2)}, u32[]{:S(2)}) collective-permute-start(f32[8,192,128]{2,1,0:T(8,128)S(1)} %collective-permute-done.20.refs_5_), channel_id=1, source_target_pairs={{8,4},{4,8},{9,5},{5,9},{10,6},{6,10},{11,7},{7,11},{24,20},{20,24... | collective-permute-start | bytes 2359304 | tf_op jit(solution)/shard_map/ppermute | solution.py:282
  142.2 0.9 copy-start.27
  143.1 35.4 %collective-permute-start.15 = (f32[192,2048]{1,0:T(8,128)}, f32[192,2048]{1,0:T(8,128)}, u32[]{:S(2)}, u32[]{:S(2)}) collective-permute-start(f32[192,2048]{1,0:T(8,128)} %slice.26), channel_id=1, source_target_pairs={{0,1},{1,0},{2,3},{3,2},{4,5},{5,4},{6,7},{7,6},{8,9},{9,8},{10,11... | collective-permute-start | bytes 4718600 | tf_op jit(solution)/shard_map/ppermute | solution.py:344
  144.6 0.9 copy-start.23
  144.6 35.1 %collective-permute-start.16 = (f32[192,2048]{1,0:T(8,128)}, f32[192,2048]{1,0:T(8,128)}, u32[]{:S(2)}, u32[]{:S(2)}) collective-permute-start(f32[192,2048]{1,0:T(8,128)} %slice.27), channel_id=1, source_target_pairs={{0,2},{1,3},{2,0},{3,1},{4,6},{5,7},{6,4},{7,5},{8,10},{9,11},{10,... | collective-permute-start | bytes 4718600 | tf_op jit(solution)/shard_map/ppermute | solution.py:345
  145.5 99.7 %collective-permute-start.21 = (f32[384,2048]{1,0:T(8,128)}, f32[384,2048]{1,0:T(8,128)}, u32[]{:S(2)}, u32[]{:S(2)}) collective-permute-start(f32[384,2048]{1,0:T(8,128)} %collective-permute-done.14.refs_0_), channel_id=1, source_target_pairs={{0,16},{16,0},{1,17},{17,1},{2,18},{18,2},{3,19},{19,3},{4,20},{20... | collective-permute-start | bytes 9437192 | tf_op jit(solution)/shard_map/ppermute | solution.py:353
  145.5 3.4 %copy-start.2 = (f32[8,128,16,128]{3,2,1,0:T(8,128)S(1)}, f32[8,128,16,128]{3,2,1,0:T(8,128)}, u32[]{:S(2)}) copy-start(f32[8,128,16,128]{3,2,1,0:T(8,128)} %param.3) | copy-start | bytes 25165828
  151.7 3.4 %copy-start = (f32[1024,2048]{1,0:T(8,128)}, f32[1024,2048]{1,0:T(8,128)S(1)}, u32[]{:S(2)}) copy-start(f32[1024,2048]{1,0:T(8,128)S(1)} %fold.1.acc_ref) | copy-start | bytes 25165828
  155.4 48.7 %copy-start.12 = (f32[8,192,128]{2,1,0:T(8,128)S(1)}, f32[8,192,128]{2,1,0:T(8,128)}, u32[]{:S(2)}) copy-start(f32[8,192,128]{2,1,0:T(8,128)} %copy-done.11) | copy-start | bytes 2359300
  155.4 51.4 %copy-start.6 = (f32[8,192,128]{2,1,0:T(8,128)S(1)}, f32[8,192,128]{2,1,0:T(8,128)}, u32[]{:S(2)}) copy-start(f32[8,192,128]{2,1,0:T(8,128)} %copy-done.5) | copy-start | bytes 2359300
  155.5 48.6 %collective-permute-start.13 = (f32[8,192,128]{2,1,0:T(8,128)}, f32[8,192,128]{2,1,0:T(8,128)S(1)}, u32[]{:S(2)}, u32[]{:S(2)}) collective-permute-start(f32[8,192,128]{2,1,0:T(8,128)} %copy-done.25), channel_id=1, source_target_pairs={{4,0},{8,12},{5,1},{9,13},{6,2},{10,14},{7,3},{11,15},{20,16},{24,... | collective-permute-start | bytes 2359304 | tf_op jit(solution)/shard_map/ppermute | solution.py:282
  178.5 44.5 %collective-permute-start.17 = (f32[192,2048]{1,0:T(8,128)}, f32[192,2048]{1,0:T(8,128)S(1)}, u32[]{:S(2)}, u32[]{:S(2)}) collective-permute-start(f32[192,2048]{1,0:T(8,128)} %collective-permute-done.15.refs_0_), channel_id=1, source_target_pairs={{0,16},{16,0},{1,17},{17,1},{2,18},{18,2},{3,19},{19,3},{4,20},{20... | collective-permute-start | bytes 4718600 | tf_op jit(solution)/shard_map/ppermute | solution.py:353
  179.7 44.5 %collective-permute-start.18 = (f32[192,2048]{1,0:T(8,128)}, f32[192,2048]{1,0:T(8,128)S(1)}, u32[]{:S(2)}, u32[]{:S(2)}) collective-permute-start(f32[192,2048]{1,0:T(8,128)} %collective-permute-done.16.refs_1_), channel_id=1, source_target_pairs={{0,16},{16,0},{1,17},{17,1},{2,18},{18,2},{3,19},{19,3},{4,20},{20... | collective-permute-start | bytes 4718600 | tf_op jit(solution)/shard_map/ppermute | solution.py:353
  179.7 3.4 %copy-start.1 = (f32[1024,2048]{1,0:T(8,128)S(1)}, f32[1024,2048]{1,0:T(8,128)}, u32[]{:S(2)}) copy-start(f32[1024,2048]{1,0:T(8,128)} %copy-done) | copy-start | bytes 25165828
  183.1 1.1 copy-start.8
  184.3 1.1 copy-start.16
  185.4 1.1 copy-start.18
  186.5 1.1 copy-start.30
  187.7 17.9 %copy-start.24 = (f32[8,192,128]{2,1,0:T(8,128)S(1)}, f32[8,192,128]{2,1,0:T(8,128)}, u32[]{:S(2)}) copy-start(f32[8,192,128]{2,1,0:T(8,128)} %copy-done.23) | copy-start | bytes 2359300
  187.7 19.2 %copy-start.20 = (f32[8,192,128]{2,1,0:T(8,128)S(1)}, f32[8,192,128]{2,1,0:T(8,128)}, u32[]{:S(2)}) copy-start(f32[8,192,128]{2,1,0:T(8,128)} %copy-done.19) | copy-start | bytes 2359300
  187.7 19.2 %copy-start.22 = (f32[8,192,128]{2,1,0:T(8,128)S(1)}, f32[8,192,128]{2,1,0:T(8,128)}, u32[]{:S(2)}) copy-start(f32[8,192,128]{2,1,0:T(8,128)} %copy-done.21) | copy-start | bytes 2359300
  187.7 19.2 %copy-start.26 = (f32[8,192,128]{2,1,0:T(8,128)S(1)}, f32[8,192,128]{2,1,0:T(8,128)}, u32[]{:S(2)}) copy-start(f32[8,192,128]{2,1,0:T(8,128)} %copy-done.25) | copy-start | bytes 2359300
  187.7 19.2 %copy-start.28 = (f32[8,192,128]{2,1,0:T(8,128)S(1)}, f32[8,192,128]{2,1,0:T(8,128)}, u32[]{:S(2)}) copy-start(f32[8,192,128]{2,1,0:T(8,128)} %copy-done.27) | copy-start | bytes 2359300
  204.0 21.7 %copy-start.4 = (f32[8,192,128]{2,1,0:T(8,128)S(1)}, f32[8,192,128]{2,1,0:T(8,128)}, u32[]{:S(2)}) copy-start(f32[8,192,128]{2,1,0:T(8,128)} %copy-done.3) | copy-start | bytes 2359300
  204.1 21.7 %copy-start.14 = (f32[8,192,128]{2,1,0:T(8,128)S(1)}, f32[8,192,128]{2,1,0:T(8,128)}, u32[]{:S(2)}) copy-start(f32[8,192,128]{2,1,0:T(8,128)} %copy-done.13) | copy-start | bytes 2359300
  204.1 37.7 %collective-permute-start.25 = (f32[8,192,128]{2,1,0:T(8,128)S(1)}, f32[8,192,128]{2,1,0:T(8,128)S(1)}, u32[]{:S(2)}, u32[]{:S(2)}) collective-permute-start(f32[8,192,128]{2,1,0:T(8,128)S(1)} %copy-done.12), channel_id=1, source_target_pairs={{4,0},{8,12},{5,1},{9,13},{6,2},{10,14},{7,3},{11,15},{20,16},{24,... | collective-permute-start | bytes 2359304 | tf_op jit(solution)/shard_map/ppermute | solution.py:282
  205.5 38.3 %collective-permute-start.27 = (f32[8,192,128]{2,1,0:T(8,128)S(1)}, f32[8,192,128]{2,1,0:T(8,128)S(1)}, u32[]{:S(2)}, u32[]{:S(2)}) collective-permute-start(f32[8,192,128]{2,1,0:T(8,128)S(1)} %copy-done.24), channel_id=1, source_target_pairs={{4,0},{8,12},{5,1},{9,13},{6,2},{10,14},{7,3},{11,15},{20,16},{24,... | collective-permute-start | bytes 2359304 | tf_op jit(solution)/shard_map/ppermute | solution.py:282
  223.0 38.4 %collective-permute-start.29 = (f32[8,192,128]{2,1,0:T(8,128)S(1)}, f32[8,192,128]{2,1,0:T(8,128)S(1)}, u32[]{:S(2)}, u32[]{:S(2)}) collective-permute-start(f32[8,192,128]{2,1,0:T(8,128)S(1)} %collective-permute-done.28.refs_1_), channel_id=1, source_target_pairs={{4,0},{8,12},{5,1},{9,13},{6,2},{10,14},{7,3},{11,15},{20,16},{24,... | collective-permute-start | bytes 2359304 | tf_op jit(solution)/shard_map/ppermute | solution.py:282
  224.3 21.0 %copy-start.10 = (f32[8,192,128]{2,1,0:T(8,128)S(1)}, f32[8,192,128]{2,1,0:T(8,128)}, u32[]{:S(2)}) copy-start(f32[8,192,128]{2,1,0:T(8,128)} %copy-done.9) | copy-start | bytes 2359300
  224.3 42.8 %collective-permute-start.31 = (f32[3,192,128]{2,1,0:T(8,128)S(1)}, f32[3,192,128]{2,1,0:T(8,128)S(1)}, u32[]{:S(2)}, u32[]{:S(2)}) collective-permute-start(f32[3,192,128]{2,1,0:T(8,128)S(1)} %get-tuple-element.32), channel_id=1, source_target_pairs={{4,0},{8,12},{5,1},{9,13},{6,2},{10,14},{7,3},{11,15},{20,16},{24,... | collective-permute-start | bytes 884744 | tf_op jit(solution)/shard_map/ppermute | solution.py:280
  241.8 31.5 %collective-permute-start.32 = (f32[3,192,128]{2,1,0:T(8,128)S(1)}, f32[3,192,128]{2,1,0:T(8,128)S(1)}, u32[]{:S(2)}, u32[]{:S(2)}) collective-permute-start(f32[3,192,128]{2,1,0:T(8,128)S(1)} %get-tuple-element.31), channel_id=1, source_target_pairs={{4,0},{8,12},{5,1},{9,13},{6,2},{10,14},{7,3},{11,15},{20,16},{24,... | collective-permute-start | bytes 884744 | tf_op jit(solution)/shard_map/ppermute | solution.py:280
  243.8 33.5 %collective-permute-start.33 = (f32[2,192,128]{2,1,0:T(8,128)S(1)}, f32[2,192,128]{2,1,0:T(8,128)S(1)}, u32[]{:S(2)}, u32[]{:S(2)}) collective-permute-start(f32[2,192,128]{2,1,0:T(8,128)S(1)} %slice.30), channel_id=1, source_target_pairs={{4,0},{8,12},{5,1},{9,13},{6,2},{10,14},{7,3},{11,15},{20,16},{24,... | collective-permute-start | bytes 589832 | tf_op jit(solution)/shard_map/ppermute | solution.py:280
  (2 other events, 1.8 us)

commit v4 on v3

--- a/solution.py
+++ b/solution.py
@@ -298,10 +298,7 @@
     power, pairs, _, target = moves(n_kk)
     left = left_panel.transpose(0, 2, 3, 1).reshape(n_kk, row_blocks, width, height)
     group = lambda index: lax.dynamic_index_in_dim(left, index, 0, keepdims=False)
-    groups = [group(kk)] + [group(target(kk, m)) for m in order[1:2]]
-    *groups, left = lax.optimization_barrier((*groups, left))
-    groups += [group(target(kk, m)) for m in order[2:]]
-    pieces = [groups[0] if m == 0 else lax.ppermute(groups[i], "kk", pairs(m)) for i, m in enumerate(order)]
+    pieces = [group(kk) if m == 0 else lax.ppermute(group(target(kk, m)), "kk", pairs(m)) for m in order]
 
     tails = [(row_blocks + 2 - n) // 3 for n in range(3)] if row_blocks > 2 and n_col > 2 else [row_blocks]
     streams = [line(piece, "col", n_col, tails if i == n_kk - 1 else ()) for i, piece in enumerate(pieces)]

time: 282 us -> 281 us (level)
    ppermute x19, waiting for transfers between devices: 80.5 us -> 84 us  [line(): new[odd] = lax.ppermute(what, axis, pairs)]
    ppermute x3, waiting for transfers between devices: 18.1 us -> 14.6 us  [local(): lax.ppermute(group(target(kk, m)), 'kk', pairs(m))]
    unnamed x65 -> x69, local copies, waits for them, and re-layouts: 24.7 us -> 25.3 us
  transfers between devices with their start and end apart: 34 -> 34, of which waited for: 13 -> 11; matrix products, arithmetic and copies ran while one was open for 4% -> 3% of each run, Pallas kernels for 29% -> 29%
where the time goes in v4:
time: 281 us; the launch traced here: 280 us
  waiting for transfers between devices  123 us (44%)
  Pallas kernels  84.1 us (30%)
  starting transfers between devices  38.7 us (14%)
  local copies, waits for them, and re-layouts  33.2 us (12%)
    ppermute x19, waiting for transfers between devices, line(): new[odd] = lax.ppermute(what, axis, pairs)  84 us
    pallas_call x4, Pallas kernels, add(): pl.pallas_call(functools.partial(add_kernel, [len(slot) for slot in slots...  64.5 us
    ppermute x19, starting transfers between devices, line(): new[odd] = lax.ppermute(what, axis, pairs)  25.6 us
    unnamed x69, local copies, waits for them, and re-layouts  25.3 us
    ppermute x1, waiting for transfers between devices, local(): first = lax.ppermute(whole(parts[m ^ bits[0]])[:half], 'kk', pairs(bits[0]))  20.9 us
    ppermute x3, waiting for transfers between devices, local(): lax.ppermute(group(target(kk, m)), 'kk', pairs(m))  14.6 us
    pallas_call x3, Pallas kernels, last(): pl.pallas_call(functools.partial(last_kernel, blocks, len(slot), first, f...  11.1 us
    pallas_call x1, Pallas kernels, one(): pl.pallas_call(functools.partial(one_kernel, len(slot)), out_shape=jax.Sh...  5.75 us
  transfers between devices with their start and end apart: 34, of which 11 were waited for; matrix products, arithmetic and copies ran while one was open for 3% of the time, Pallas kernels for 29%

profile of v4, /device:TPU:0, one launch (start us, length us, event | category | flops | bytes accessed | tf_op | source)
XLA Modules:
  0.0 279.9 jit_solution(8450581402733360752)
XLA Ops:
  0.0 2.2 dynamic-slice_bitcast_fusion
  2.2 3.1 %collective-permute-start.1 = (f32[8,192,128]{2,1,0:T(8,128)S(1)}, f32[8,192,128]{2,1,0:T(8,128)S(1)}, u32[]{:S(2)}, u32[]{:S(2)}) collective-permute-start(f32[8,192,128]{2,1,0:T(8,128)S(1)} %get-tuple-element.24.refs_2_), channel_id=1, source_target_pairs={{4,0},{0,4},{12,8},{8,12},{5,1},{1,5},{13,9},{9,13},{6,2},{2,6},{1... | collective-permute-start | bytes 2359304 | tf_op jit(solution)/shard_map/ppermute | solution.py:282
  6.1 1.6 collective-permute-start.8
  7.6 1.5 collective-permute-start.19
  9.6 13.3 %collective-permute-done.1.refs_3_ = f32[8,192,128]{2,1,0:T(8,128)S(1)} collective-permute-done((f32[8,192,128]{2,1,0:T(8,128)S(1)}, f32[8,192,128]{2,1,0:T(8,128)S(1)}, u32[]{:S(2)}, u32[]{:S(2)}) %collective-permute-start.1) | collective-permute-done | bytes 786464 | tf_op jit(solution)/shard_map/ppermute | solution.py:282
  22.9 0.7 collective-permute-start.4
  23.6 1.3 collective-permute-start.3
  24.9 3.1 %copy.16 = f32[48,8,16,128]{3,1,2,0:T(8,128)} copy(f32[48,8,16,128]{3,2,1,0:T(8,128)S(1)} %bitcast.27) | data formatting | bytes 6291456
  28.1 1.7 collective-permute-start.6
  29.8 14.6 %collective-permute-done.19.refs_4_ = f32[8,192,128]{2,1,0:T(8,128)S(1)} collective-permute-done((f32[8,192,128]{2,1,0:T(8,128)S(1)}, f32[8,192,128]{2,1,0:T(8,128)S(1)}, u32[]{:S(2)}, u32[]{:S(2)}) %collective-permute-start.19) | collective-permute-done | bytes 786464 | tf_op jit(solution)/shard_map/ppermute | solution.py:301
  44.9 4.4 %collective-permute-start.9 = (f32[8,192,128]{2,1,0:T(8,128)S(1)}, f32[8,192,128]{2,1,0:T(8,128)S(1)}, u32[]{:S(2)}, u32[]{:S(2)}) collective-permute-start(f32[8,192,128]{2,1,0:T(8,128)S(1)} %collective-permute-done.8.refs_2_), channel_id=1, source_target_pairs={{4,0},{0,4},{12,8},{8,12},{5,1},{1,5},{13,9},{9,13},{6,2},{2,6},{1... | collective-permute-start | bytes 2359304 | tf_op jit(solution)/shard_map/ppermute | solution.py:282
  49.3 0.7 collective-permute-start.10
  50.0 0.9 copy-done.5
  50.9 0.9 copy-done.19
  51.8 1.2 collective-permute-start.20
  53.0 14.6 %collective-permute-done.9.refs_3_ = f32[8,192,128]{2,1,0:T(8,128)S(1)} collective-permute-done((f32[8,192,128]{2,1,0:T(8,128)S(1)}, f32[8,192,128]{2,1,0:T(8,128)S(1)}, u32[]{:S(2)}, u32[]{:S(2)}) %collective-permute-start.9) | collective-permute-done | bytes 786464 | tf_op jit(solution)/shard_map/ppermute | solution.py:282
  67.6 2.0 collective-permute-start.23
  69.7 0.7 collective-permute-start.24
  70.4 14.1 %collective-permute-done.20.refs_5_ = f32[8,192,128]{2,1,0:T(8,128)S(1)} collective-permute-done((f32[8,192,128]{2,1,0:T(8,128)S(1)}, f32[8,192,128]{2,1,0:T(8,128)S(1)}, u32[]{:S(2)}, u32[]{:S(2)}) %collective-permute-start.20) | collective-permute-done | bytes 786464 | tf_op jit(solution)/shard_map/ppermute | solution.py:282
  84.5 0.7 collective-permute-start.28
  85.2 11.9 %collective-permute-done.23.refs_3_ = f32[8,192,128]{2,1,0:T(8,128)S(1)} collective-permute-done((f32[8,192,128]{2,1,0:T(8,128)S(1)}, f32[8,192,128]{2,1,0:T(8,128)S(1)}, u32[]{:S(2)}, u32[]{:S(2)}) %collective-permute-start.23) | collective-permute-done | bytes 786464 | tf_op jit(solution)/shard_map/ppermute | solution.py:282
  97.1 1.3 collective-permute-start.5
  98.4 0.9 copy-done.17
  99.3 0.7 collective-permute-start.12
  100.0 0.9 copy-done.21
  100.9 18.0 %collective-permute-done.5.refs_6_ = f32[8,192,128]{2,1,0:T(8,128)S(1)} collective-permute-done((f32[8,192,128]{2,1,0:T(8,128)S(1)}, f32[8,192,128]{2,1,0:T(8,128)S(1)}, u32[]{:S(2)}, u32[]{:S(2)}) %collective-permute-start.5) | collective-permute-done | bytes 786464 | tf_op jit(solution)/shard_map/ppermute | solution.py:282
  119.0 0.9 copy-done.31
  119.8 1.3 collective-permute-start.11
  121.1 0.9 copy-done.23
  122.0 0.7 collective-permute-start.26
  122.8 0.7 collective-permute-start.30
  123.6 2.7 slice.27
  126.3 2.8 slice.26
  129.1 11.7 %collective-permute-done.11.refs_4_ = f32[8,192,128]{2,1,0:T(8,128)S(1)} collective-permute-done((f32[8,192,128]{2,1,0:T(8,128)S(1)}, f32[8,192,128]{2,1,0:T(8,128)S(1)}, u32[]{:S(2)}, u32[]{:S(2)}) %collective-permute-start.11) | collective-permute-done | bytes 786464 | tf_op jit(solution)/shard_map/ppermute | solution.py:282
  140.8 0.9 copy-done.29
  141.7 1.5 collective-permute-start.15
  143.2 1.5 collective-permute-start.16
  144.9 3.4 %copy-done.2 = f32[8,128,16,128]{3,2,1,0:T(8,128)S(1)} copy-done((f32[8,128,16,128]{3,2,1,0:T(8,128)S(1)}, f32[8,128,16,128]{3,2,1,0:T(8,128)}, u32[]{:S(2)}) %copy-start.2) | copy-done | bytes 8388632
  148.3 2.8 %fold.1.acc_ref = f32[1024,2048]{1,0:T(8,128)S(1)} custom-call(f32[16384,128]{1,0:T(8,128)S(1)} %bitcast.25), custom_call_target="tpu_custom_call" | custom-call | bytes 8388608 | tf_op jit(solution)/shard_map/fold/pallas_call | solution.py:139
  151.1 3.4 %copy-done = f32[1024,2048]{1,0:T(8,128)} copy-done((f32[1024,2048]{1,0:T(8,128)}, f32[1024,2048]{1,0:T(8,128)S(1)}, u32[]{:S(2)}) %copy-start) | copy-done | bytes 8388632
  154.8 1.4 collective-permute-start.13
  156.2 20.9 %collective-permute-done.15.refs_0_ = f32[192,2048]{1,0:T(8,128)} collective-permute-done((f32[192,2048]{1,0:T(8,128)}, f32[192,2048]{1,0:T(8,128)}, u32[]{:S(2)}, u32[]{:S(2)}) %collective-permute-start.15) | collective-permute-done | bytes 1572896 | tf_op jit(solution)/shard_map/ppermute | solution.py:341
  177.1 1.2 collective-permute-done.16.refs_1_
  178.3 3.4 %copy-done.1 = f32[1024,2048]{1,0:T(8,128)S(1)} copy-done((f32[1024,2048]{1,0:T(8,128)S(1)}, f32[1024,2048]{1,0:T(8,128)}, u32[]{:S(2)}) %copy-start.1) | copy-done | bytes 8388632
  181.7 1.1 copy-done.10
  182.8 1.1 copy-done.12
  184.0 1.1 copy-done.18
  185.1 1.1 copy-done.20
  186.2 1.1 copy-done.32
  187.4 16.4 %add.77.acc_ref = f32[1024,2048]{1,0:T(8,128)S(1)} custom-call(s32[8]{0:T(128)S(1)} %stack.49.scalars, f32[1024,2048]{1,0:T(8,128)S(1)} %copy-done.1, f32[384,2048]{1,0:T(8,128)} %bitcast.24.refs_0_, f32[384,2048]{1,0:T(8,128)} %collective-permute-done.refs_1_, f32[8,192,128]{2,1,0:T(8,128)S(1)} %get-tuple-element.24.refs_2_, ...), custom_call_target="tpu_custom_call", output_to_operand_aliasing={{}: (1, {})} | custom-call | flops 9663676416 | bytes 6291456 | tf_op jit(solution)/shard_map/add/pallas_call | solution.py:101
  203.8 1.4 collective-permute-start.25
  205.3 1.3 collective-permute-start.27
  206.6 16.1 %add.78.acc_ref = f32[1024,2048]{1,0:T(8,128)S(1)} custom-call(s32[8]{0:T(128)S(1)} %stack.49.scalars, f32[1024,2048]{1,0:T(8,128)S(1)} %add.77.acc_ref, f32[384,2048]{1,0:T(8,128)} %collective-permute-done.6.refs_0_, f32[384,2048]{1,0:T(8,128)} %collective-permute-done.7.refs_1_, f32[8,192,128]{2,1,0:T(8,128)S(1)} %copy-done.6, ...), custom_call_target="tpu_custom_call", output_to_operand_aliasing={{}: (1, {})} | custom-call | flops 9663676416 | bytes 6291456 | tf_op jit(solution)/shard_map/add/pallas_call | solution.py:101
  222.7 1.3 collective-permute-start.29
  224.0 1.4 collective-permute-start.31
  225.5 16.0 %add.79 = (f32[1024,2048]{1,0:T(8,128)S(1)}, bf16[768,2048]{1,0:T(8,128)(2,1)S(1)}, bf16[768,2048]{1,0:T(8,128)(2,1)S(1)}) custom-call(s32[8]{0:T(128)S(1)} %stack.49.scalars, f32[1024,2048]{1,0:T(8,128)S(1)} %add.78.acc_ref, f32[192,2048]{1,0:T(8,128)} %collective-permute-done.15.refs_0_, ...), custom_call_target="tpu_custom_call", output_to_operand_aliasing={{0}: (1, {})} | custom-call | flops 4831838208 | bytes 6291456 | tf_op jit(solution)/shard_map/add/pallas_call | solution.py:101
  241.5 1.3 collective-permute-start.32
  243.1 1.5 collective-permute-start.33
  244.6 16.1 %add.80.acc_ref = f32[1024,2048]{1,0:T(8,128)S(1)} custom-call(s32[8]{0:T(128)S(1)} %stack.49.scalars, f32[1024,2048]{1,0:T(8,128)S(1)} %get-tuple-element.13.acc_ref, f32[384,2048]{1,0:T(8,128)} %collective-permute-done.14.refs_0_, f32[384,2048]{1,0:T(8,128)} %collective-permute-done.21.refs_1_, ...), custom_call_target="tpu_custom_call", output_to_operand_aliasing={{}: (1, {})} | custom-call | flops 9663676416 | bytes 6291456 | tf_op jit(solution)/shard_map/add/pallas_call | solution.py:101
  260.7 5.8 %one.1.acc_ref = f32[1024,2048]{1,0:T(8,128)S(1)} custom-call(s32[2]{0:T(128)S(1)} %pad_add_fusion.1.scalars, f32[1024,2048]{1,0:T(8,128)S(1)} %add.80.acc_ref, bf16[768,2048]{1,0:T(8,128)(2,1)S(1)} %get-tuple-element.14.high_ref, bf16[768,2048]{1,0:T(8,128)(2,1)S(1)} %get-tuple-element.15.low_ref, ...), custom_call_target="tpu_custom_call", output_to_operand_aliasing={{}: (1, {})} | custom-call | flops 2415919104 | bytes 786432 | tf_op jit(solution)/shard_map/one/pallas_call | solution.py:178
  266.5 3.9 %last.3 = (f32[16384,128]{1,0:T(8,128)}, f32[1024,2048]{1,0:T(8,128)S(1)}) custom-call(s32[2]{0:T(128)S(1)} %pad_add_fusion.scalars, f32[1024,2048]{1,0:T(8,128)S(1)} %one.1.acc_ref, bf16[768,2048]{1,0:T(8,128)(2,1)S(1)} %get-tuple-element.14.high_ref, bf16[768,2048]{1,0:T(8,128)(2,1)S(1)} %get-tuple-element.15.low_ref, ...), custom_call_target="tpu_custom_call", output_to_operand_aliasing={{1}: (1, {})} | custom-call | flops 905969664 | bytes 3145728 | tf_op jit(solution)/shard_map/last/pallas_call | solution.py:235
  270.4 2.2 collective-permute-done.32.refs_0_
  272.6 3.9 %last.4 = (f32[16384,128]{1,0:T(8,128)}, f32[1024,2048]{1,0:T(8,128)S(1)}) custom-call(s32[2]{0:T(128)S(1)} %pad_add_fusion.scalars, f32[1024,2048]{1,0:T(8,128)S(1)} %get-tuple-element.16.acc_ref, bf16[768,2048]{1,0:T(8,128)(2,1)S(1)} %get-tuple-element.14.high_ref, ...), custom_call_target="tpu_custom_call", output_to_operand_aliasing={{1}: (1, {}), {0}: (6, {})} | custom-call | flops 905969664 | bytes 3145728 | tf_op jit(solution)/shard_map/last/pallas_call | solution.py:235
  276.6 3.2 %last.5 = (f32[16384,128]{1,0:T(8,128)}, f32[1024,2048]{1,0:T(8,128)S(1)}) custom-call(s32[2]{0:T(128)S(1)} %pad_add_fusion.scalars, f32[1024,2048]{1,0:T(8,128)S(1)} %get-tuple-element.18.acc_ref, bf16[768,2048]{1,0:T(8,128)(2,1)S(1)} %get-tuple-element.14.high_ref, ...), custom_call_target="tpu_custom_call", output_to_operand_aliasing={{1}: (1, {}), {0}: (6, {})} | custom-call | flops 603979776 | bytes 2097152 | tf_op jit(solution)/shard_map/last/pallas_call | solution.py:235
  (90 shorter events, 2.6 us)
Async XLA Ops:
  0.0 24.9 %copy-start.33 = (f32[1,384,16,128]{3,2,1,0:T(8,128)S(1)}, f32[1,384,16,128]{3,2,1,0:T(8,128)}, u32[]{:S(2)}) copy-start(f32[1,384,16,128]{3,2,1,0:T(8,128)} %param.5) | copy-start | bytes 9437188
  2.2 20.7 %collective-permute-start.1 = (f32[8,192,128]{2,1,0:T(8,128)S(1)}, f32[8,192,128]{2,1,0:T(8,128)S(1)}, u32[]{:S(2)}, u32[]{:S(2)}) collective-permute-start(f32[8,192,128]{2,1,0:T(8,128)S(1)} %get-tuple-element.24.refs_2_), channel_id=1, source_target_pairs={{4,0},{0,4},{12,8},{8,12},{5,1},{1,5},{13,9},{9,13},{6,2},{2,6},{1... | collective-permute-start | bytes 2359304 | tf_op jit(solution)/shard_map/ppermute | solution.py:282
  5.3 18.3 %collective-permute-start.2 = (f32[8,192,128]{2,1,0:T(8,128)S(1)}, f32[8,192,128]{2,1,0:T(8,128)S(1)}, u32[]{:S(2)}, u32[]{:S(2)}) collective-permute-start(f32[8,192,128]{2,1,0:T(8,128)S(1)} %get-tuple-element.24.refs_2_), channel_id=1, source_target_pairs={{8,4},{4,8},{9,5},{5,9},{10,6},{6,10},{11,7},{7,11},{24,20},{20,24... | collective-permute-start | bytes 2359304 | tf_op jit(solution)/shard_map/ppermute | solution.py:282
  6.1 22.0 %collective-permute-start.8 = (f32[8,192,128]{2,1,0:T(8,128)S(1)}, f32[8,192,128]{2,1,0:T(8,128)S(1)}, u32[]{:S(2)}, u32[]{:S(2)}) collective-permute-start(f32[8,192,128]{2,1,0:T(8,128)S(1)} %get-tuple-element.23), channel_id=1, source_target_pairs={{0,1},{1,0},{2,3},{3,2},{4,5},{5,4},{6,7},{7,6},{8,9},{9,8},{10,11... | collective-permute-start | bytes 2359304 | tf_op jit(solution)/shard_map/ppermute | solution.py:301
  7.6 36.8 %collective-permute-start.19 = (f32[8,192,128]{2,1,0:T(8,128)S(1)}, f32[8,192,128]{2,1,0:T(8,128)S(1)}, u32[]{:S(2)}, u32[]{:S(2)}) collective-permute-start(f32[8,192,128]{2,1,0:T(8,128)S(1)} %get-tuple-element.22), channel_id=1, source_target_pairs={{0,3},{1,2},{2,1},{3,0},{4,7},{5,6},{6,5},{7,4},{8,11},{9,10},{10,... | collective-permute-start | bytes 2359304 | tf_op jit(solution)/shard_map/ppermute | solution.py:301
  9.1 35.8 %collective-permute-start.22 = (f32[8,192,128]{2,1,0:T(8,128)S(1)}, f32[8,192,128]{2,1,0:T(8,128)S(1)}, u32[]{:S(2)}, u32[]{:S(2)}) collective-permute-start(f32[8,192,128]{2,1,0:T(8,128)S(1)} %get-tuple-element.21), channel_id=1, source_target_pairs={{0,2},{1,3},{2,0},{3,1},{4,6},{5,7},{6,4},{7,5},{8,10},{9,11},{10,... | collective-permute-start | bytes 2359304 | tf_op jit(solution)/shard_map/ppermute | solution.py:301
  22.9 5.2 %copy-start.9 = (f32[8,192,128]{2,1,0:T(8,128)}, f32[8,192,128]{2,1,0:T(8,128)S(1)}, u32[]{:S(2)}) copy-start(f32[8,192,128]{2,1,0:T(8,128)S(1)} %collective-permute-done.1.refs_3_) | copy-start | bytes 2359300
  22.9 26.4 %collective-permute-start.4 = (f32[8,192,128]{2,1,0:T(8,128)S(1)}, f32[8,192,128]{2,1,0:T(8,128)S(1)}, u32[]{:S(2)}, u32[]{:S(2)}) collective-permute-start(f32[8,192,128]{2,1,0:T(8,128)S(1)} %collective-permute-done.1.refs_3_), channel_id=1, source_target_pairs={{8,4},{4,8},{9,5},{5,9},{10,6},{6,10},{11,7},{7,11},{24,20},{20,24... | collective-permute-start | bytes 2359304 | tf_op jit(solution)/shard_map/ppermute | solution.py:282
  23.6 4.5 %copy-start.11 = (f32[8,192,128]{2,1,0:T(8,128)}, f32[8,192,128]{2,1,0:T(8,128)S(1)}, u32[]{:S(2)}) copy-start(f32[8,192,128]{2,1,0:T(8,128)S(1)} %collective-permute-done.2.refs_5_) | copy-start | bytes 2359300
  23.6 27.3 %collective-permute-start.3 = (f32[8,192,128]{2,1,0:T(8,128)S(1)}, f32[8,192,128]{2,1,0:T(8,128)S(1)}, u32[]{:S(2)}, u32[]{:S(2)}) collective-permute-start(f32[8,192,128]{2,1,0:T(8,128)S(1)} %collective-permute-done.2.refs_5_), channel_id=1, source_target_pairs={{4,0},{8,12},{5,1},{9,13},{6,2},{10,14},{7,3},{11,15},{20,16},{24,... | collective-permute-start | bytes 2359304 | tf_op jit(solution)/shard_map/ppermute | solution.py:282
  28.1 94.7 %collective-permute-start.6 = (f32[384,2048]{1,0:T(8,128)}, f32[384,2048]{1,0:T(8,128)}, u32[]{:S(2)}, u32[]{:S(2)}) collective-permute-start(f32[384,2048]{1,0:T(8,128)} %bitcast.24.refs_0_), channel_id=1, source_target_pairs={{0,1},{1,0},{2,3},{3,2},{4,5},{5,4},{6,7},{7,6},{8,9},{9,8},{10,11... | collective-permute-start | bytes 9437192 | tf_op jit(solution)/shard_map/ppermute | solution.py:337
  44.4 84.7 %copy-start.3 = (f32[8,192,128]{2,1,0:T(8,128)}, f32[8,192,128]{2,1,0:T(8,128)S(1)}, u32[]{:S(2)}) copy-start(f32[8,192,128]{2,1,0:T(8,128)S(1)} %collective-permute-done.19.refs_4_) | copy-start | bytes 2359300
  44.4 78.5 %collective-permute-start.14 = (f32[384,2048]{1,0:T(8,128)}, f32[384,2048]{1,0:T(8,128)}, u32[]{:S(2)}, u32[]{:S(2)}) collective-permute-start(f32[384,2048]{1,0:T(8,128)} %bitcast.24.refs_0_), channel_id=1, source_target_pairs={{0,2},{1,3},{2,0},{3,1},{4,6},{5,7},{6,4},{7,5},{8,10},{9,11},{10,... | collective-permute-start | bytes 9437192 | tf_op jit(solution)/shard_map/ppermute | solution.py:337
  44.9 22.7 %collective-permute-start.9 = (f32[8,192,128]{2,1,0:T(8,128)S(1)}, f32[8,192,128]{2,1,0:T(8,128)S(1)}, u32[]{:S(2)}, u32[]{:S(2)}) collective-permute-start(f32[8,192,128]{2,1,0:T(8,128)S(1)} %collective-permute-done.8.refs_2_), channel_id=1, source_target_pairs={{4,0},{0,4},{12,8},{8,12},{5,1},{1,5},{13,9},{9,13},{6,2},{2,6},{1... | collective-permute-start | bytes 2359304 | tf_op jit(solution)/shard_map/ppermute | solution.py:282
  49.3 20.4 %collective-permute-start.10 = (f32[8,192,128]{2,1,0:T(8,128)S(1)}, f32[8,192,128]{2,1,0:T(8,128)S(1)}, u32[]{:S(2)}, u32[]{:S(2)}) collective-permute-start(f32[8,192,128]{2,1,0:T(8,128)S(1)} %collective-permute-done.8.refs_2_), channel_id=1, source_target_pairs={{8,4},{4,8},{9,5},{5,9},{10,6},{6,10},{11,7},{7,11},{24,20},{20,24... | collective-permute-start | bytes 2359304 | tf_op jit(solution)/shard_map/ppermute | solution.py:282
  50.0 0.9 copy-start.5
  51.8 32.7 %collective-permute-start.20 = (f32[8,192,128]{2,1,0:T(8,128)S(1)}, f32[8,192,128]{2,1,0:T(8,128)S(1)}, u32[]{:S(2)}, u32[]{:S(2)}) collective-permute-start(f32[8,192,128]{2,1,0:T(8,128)S(1)} %collective-permute-done.19.refs_4_), channel_id=1, source_target_pairs={{4,0},{0,4},{12,8},{8,12},{5,1},{1,5},{13,9},{9,13},{6,2},{2,6},{1... | collective-permute-start | bytes 2359304 | tf_op jit(solution)/shard_map/ppermute | solution.py:282
  67.6 29.5 %collective-permute-start.23 = (f32[8,192,128]{2,1,0:T(8,128)S(1)}, f32[8,192,128]{2,1,0:T(8,128)S(1)}, u32[]{:S(2)}, u32[]{:S(2)}) collective-permute-start(f32[8,192,128]{2,1,0:T(8,128)S(1)} %collective-permute-done.22.refs_2_), channel_id=1, source_target_pairs={{4,0},{0,4},{12,8},{8,12},{5,1},{1,5},{13,9},{9,13},{6,2},{2,6},{1... | collective-permute-start | bytes 2359304 | tf_op jit(solution)/shard_map/ppermute | solution.py:282
  69.7 27.4 %collective-permute-start.24 = (f32[8,192,128]{2,1,0:T(8,128)S(1)}, f32[8,192,128]{2,1,0:T(8,128)S(1)}, u32[]{:S(2)}, u32[]{:S(2)}) collective-permute-start(f32[8,192,128]{2,1,0:T(8,128)S(1)} %collective-permute-done.22.refs_2_), channel_id=1, source_target_pairs={{8,4},{4,8},{9,5},{5,9},{10,6},{6,10},{11,7},{7,11},{24,20},{20,24... | collective-permute-start | bytes 2359304 | tf_op jit(solution)/shard_map/ppermute | solution.py:282
  84.5 44.6 %copy-start.15 = (f32[8,192,128]{2,1,0:T(8,128)}, f32[8,192,128]{2,1,0:T(8,128)S(1)}, u32[]{:S(2)}) copy-start(f32[8,192,128]{2,1,0:T(8,128)S(1)} %collective-permute-done.20.refs_5_) | copy-start | bytes 2359300
  84.5 14.8 %collective-permute-start.28 = (f32[8,192,128]{2,1,0:T(8,128)S(1)}, f32[8,192,128]{2,1,0:T(8,128)S(1)}, u32[]{:S(2)}, u32[]{:S(2)}) collective-permute-start(f32[8,192,128]{2,1,0:T(8,128)S(1)} %collective-permute-done.19.refs_4_), channel_id=1, source_target_pairs={{8,4},{4,8},{9,5},{5,9},{10,6},{6,10},{11,7},{7,11},{24,20},{20,24... | collective-permute-start | bytes 2359304 | tf_op jit(solution)/shard_map/ppermute | solution.py:282
  97.1 32.0 %copy-start.7 = (f32[8,192,128]{2,1,0:T(8,128)}, f32[8,192,128]{2,1,0:T(8,128)S(1)}, u32[]{:S(2)}) copy-start(f32[8,192,128]{2,1,0:T(8,128)S(1)} %collective-permute-done.23.refs_3_) | copy-start | bytes 2359300
  97.1 57.7 %collective-permute-start = (f32[384,2048]{1,0:T(8,128)}, f32[384,2048]{1,0:T(8,128)}, u32[]{:S(2)}, u32[]{:S(2)}) collective-permute-start(f32[384,2048]{1,0:T(8,128)} %bitcast.24.refs_0_), channel_id=1, source_target_pairs={{0,16},{16,0},{1,17},{17,1},{2,18},{18,2},{3,19},{19,3},{4,20},{20... | collective-permute-start | bytes 9437192 | tf_op jit(solution)/shard_map/ppermute | solution.py:350
  97.1 32.0 %copy-start.13 = (f32[8,192,128]{2,1,0:T(8,128)}, f32[8,192,128]{2,1,0:T(8,128)S(1)}, u32[]{:S(2)}) copy-start(f32[8,192,128]{2,1,0:T(8,128)S(1)} %collective-permute-done.24.refs_5_) | copy-start | bytes 2359300
  97.1 21.8 %collective-permute-start.5 = (f32[8,192,128]{2,1,0:T(8,128)S(1)}, f32[8,192,128]{2,1,0:T(8,128)S(1)}, u32[]{:S(2)}, u32[]{:S(2)}) collective-permute-start(f32[8,192,128]{2,1,0:T(8,128)S(1)} %collective-permute-done.4.refs_7_), channel_id=1, source_target_pairs={{4,0},{8,12},{5,1},{9,13},{6,2},{10,14},{7,3},{11,15},{20,16},{24,... | collective-permute-start | bytes 2359304 | tf_op jit(solution)/shard_map/ppermute | solution.py:282
  99.3 22.7 %collective-permute-start.12 = (f32[8,192,128]{2,1,0:T(8,128)S(1)}, f32[8,192,128]{2,1,0:T(8,128)S(1)}, u32[]{:S(2)}, u32[]{:S(2)}) collective-permute-start(f32[8,192,128]{2,1,0:T(8,128)S(1)} %collective-permute-done.9.refs_3_), channel_id=1, source_target_pairs={{8,4},{4,8},{9,5},{5,9},{10,6},{6,10},{11,7},{7,11},{24,20},{20,24... | collective-permute-start | bytes 2359304 | tf_op jit(solution)/shard_map/ppermute | solution.py:282
  119.8 21.0 %collective-permute-start.11 = (f32[8,192,128]{2,1,0:T(8,128)S(1)}, f32[8,192,128]{2,1,0:T(8,128)S(1)}, u32[]{:S(2)}, u32[]{:S(2)}) collective-permute-start(f32[8,192,128]{2,1,0:T(8,128)S(1)} %collective-permute-done.10.refs_5_), channel_id=1, source_target_pairs={{4,0},{8,12},{5,1},{9,13},{6,2},{10,14},{7,3},{11,15},{20,16},{24,... | collective-permute-start | bytes 2359304 | tf_op jit(solution)/shard_map/ppermute | solution.py:282
  121.1 0.9 copy-start.23
  122.0 7.1 %copy-start.27 = (f32[8,192,128]{2,1,0:T(8,128)}, f32[8,192,128]{2,1,0:T(8,128)S(1)}, u32[]{:S(2)}) copy-start(f32[8,192,128]{2,1,0:T(8,128)S(1)} %collective-permute-done.12.refs_7_) | copy-start | bytes 2359300
  122.0 21.2 %collective-permute-start.26 = (f32[8,192,128]{2,1,0:T(8,128)S(1)}, f32[8,192,128]{2,1,0:T(8,128)S(1)}, u32[]{:S(2)}, u32[]{:S(2)}) collective-permute-start(f32[8,192,128]{2,1,0:T(8,128)S(1)} %collective-permute-done.23.refs_3_), channel_id=1, source_target_pairs={{8,4},{4,8},{9,5},{5,9},{10,6},{6,10},{11,7},{7,11},{24,20},{20,24... | collective-permute-start | bytes 2359304 | tf_op jit(solution)/shard_map/ppermute | solution.py:282
  122.8 82.5 %collective-permute-start.7 = (f32[384,2048]{1,0:T(8,128)}, f32[384,2048]{1,0:T(8,128)}, u32[]{:S(2)}, u32[]{:S(2)}) collective-permute-start(f32[384,2048]{1,0:T(8,128)} %collective-permute-done.6.refs_0_), channel_id=1, source_target_pairs={{0,16},{16,0},{1,17},{17,1},{2,18},{18,2},{3,19},{19,3},{4,20},{20... | collective-permute-start | bytes 9437192 | tf_op jit(solution)/shard_map/ppermute | solution.py:350
  122.8 21.9 %collective-permute-start.30 = (f32[8,192,128]{2,1,0:T(8,128)S(1)}, f32[8,192,128]{2,1,0:T(8,128)S(1)}, u32[]{:S(2)}, u32[]{:S(2)}) collective-permute-start(f32[8,192,128]{2,1,0:T(8,128)S(1)} %collective-permute-done.20.refs_5_), channel_id=1, source_target_pairs={{8,4},{4,8},{9,5},{5,9},{10,6},{6,10},{11,7},{7,11},{24,20},{20,24... | collective-permute-start | bytes 2359304 | tf_op jit(solution)/shard_map/ppermute | solution.py:282
  140.8 0.9 copy-start.29
  141.7 35.4 %collective-permute-start.15 = (f32[192,2048]{1,0:T(8,128)}, f32[192,2048]{1,0:T(8,128)}, u32[]{:S(2)}, u32[]{:S(2)}) collective-permute-start(f32[192,2048]{1,0:T(8,128)} %slice.26), channel_id=1, source_target_pairs={{0,1},{1,0},{2,3},{3,2},{4,5},{5,4},{6,7},{7,6},{8,9},{9,8},{10,11... | collective-permute-start | bytes 4718600 | tf_op jit(solution)/shard_map/ppermute | solution.py:341
  143.2 1.5 copy-start.25
  143.2 35.1 %collective-permute-start.16 = (f32[192,2048]{1,0:T(8,128)}, f32[192,2048]{1,0:T(8,128)}, u32[]{:S(2)}, u32[]{:S(2)}) collective-permute-start(f32[192,2048]{1,0:T(8,128)} %slice.27), channel_id=1, source_target_pairs={{0,2},{1,3},{2,0},{3,1},{4,6},{5,7},{6,4},{7,5},{8,10},{9,11},{10,... | collective-permute-start | bytes 4718600 | tf_op jit(solution)/shard_map/ppermute | solution.py:342
  144.7 99.8 %collective-permute-start.21 = (f32[384,2048]{1,0:T(8,128)}, f32[384,2048]{1,0:T(8,128)}, u32[]{:S(2)}, u32[]{:S(2)}) collective-permute-start(f32[384,2048]{1,0:T(8,128)} %collective-permute-done.14.refs_0_), channel_id=1, source_target_pairs={{0,16},{16,0},{1,17},{17,1},{2,18},{18,2},{3,19},{19,3},{4,20},{20... | collective-permute-start | bytes 9437192 | tf_op jit(solution)/shard_map/ppermute | solution.py:350
  144.9 3.4 %copy-start.2 = (f32[8,128,16,128]{3,2,1,0:T(8,128)S(1)}, f32[8,128,16,128]{3,2,1,0:T(8,128)}, u32[]{:S(2)}) copy-start(f32[8,128,16,128]{3,2,1,0:T(8,128)} %param.3) | copy-start | bytes 25165828
  151.1 3.4 %copy-start = (f32[1024,2048]{1,0:T(8,128)}, f32[1024,2048]{1,0:T(8,128)S(1)}, u32[]{:S(2)}) copy-start(f32[1024,2048]{1,0:T(8,128)S(1)} %fold.1.acc_ref) | copy-start | bytes 25165828
  154.7 49.1 %copy-start.14 = (f32[8,192,128]{2,1,0:T(8,128)S(1)}, f32[8,192,128]{2,1,0:T(8,128)}, u32[]{:S(2)}) copy-start(f32[8,192,128]{2,1,0:T(8,128)} %copy-done.13) | copy-start | bytes 2359300
  154.7 51.8 %copy-start.6 = (f32[8,192,128]{2,1,0:T(8,128)S(1)}, f32[8,192,128]{2,1,0:T(8,128)}, u32[]{:S(2)}) copy-start(f32[8,192,128]{2,1,0:T(8,128)} %copy-done.5) | copy-start | bytes 2359300
  154.8 49.0 %collective-permute-start.13 = (f32[8,192,128]{2,1,0:T(8,128)}, f32[8,192,128]{2,1,0:T(8,128)S(1)}, u32[]{:S(2)}, u32[]{:S(2)}) collective-permute-start(f32[8,192,128]{2,1,0:T(8,128)} %copy-done.27), channel_id=1, source_target_pairs={{4,0},{8,12},{5,1},{9,13},{6,2},{10,14},{7,3},{11,15},{20,16},{24,... | collective-permute-start | bytes 2359304 | tf_op jit(solution)/shard_map/ppermute | solution.py:282
  177.1 45.6 %collective-permute-start.17 = (f32[192,2048]{1,0:T(8,128)}, f32[192,2048]{1,0:T(8,128)S(1)}, u32[]{:S(2)}, u32[]{:S(2)}) collective-permute-start(f32[192,2048]{1,0:T(8,128)} %collective-permute-done.15.refs_0_), channel_id=1, source_target_pairs={{0,16},{16,0},{1,17},{17,1},{2,18},{18,2},{3,19},{19,3},{4,20},{20... | collective-permute-start | bytes 4718600 | tf_op jit(solution)/shard_map/ppermute | solution.py:350
  178.3 45.7 %collective-permute-start.18 = (f32[192,2048]{1,0:T(8,128)}, f32[192,2048]{1,0:T(8,128)S(1)}, u32[]{:S(2)}, u32[]{:S(2)}) collective-permute-start(f32[192,2048]{1,0:T(8,128)} %collective-permute-done.16.refs_1_), channel_id=1, source_target_pairs={{0,16},{16,0},{1,17},{17,1},{2,18},{18,2},{3,19},{19,3},{4,20},{20... | collective-permute-start | bytes 4718600 | tf_op jit(solution)/shard_map/ppermute | solution.py:350
  178.3 3.4 %copy-start.1 = (f32[1024,2048]{1,0:T(8,128)S(1)}, f32[1024,2048]{1,0:T(8,128)}, u32[]{:S(2)}) copy-start(f32[1024,2048]{1,0:T(8,128)} %copy-done) | copy-start | bytes 25165828
  181.7 1.1 copy-start.10
  182.8 1.1 copy-start.12
  184.0 1.1 copy-start.18
  185.1 1.1 copy-start.20
  186.2 1.1 copy-start.32
  187.4 17.9 %copy-start.26 = (f32[8,192,128]{2,1,0:T(8,128)S(1)}, f32[8,192,128]{2,1,0:T(8,128)}, u32[]{:S(2)}) copy-start(f32[8,192,128]{2,1,0:T(8,128)} %copy-done.25) | copy-start | bytes 2359300
  187.4 19.2 %copy-start.22 = (f32[8,192,128]{2,1,0:T(8,128)S(1)}, f32[8,192,128]{2,1,0:T(8,128)}, u32[]{:S(2)}) copy-start(f32[8,192,128]{2,1,0:T(8,128)} %copy-done.21) | copy-start | bytes 2359300
  187.4 19.2 %copy-start.24 = (f32[8,192,128]{2,1,0:T(8,128)S(1)}, f32[8,192,128]{2,1,0:T(8,128)}, u32[]{:S(2)}) copy-start(f32[8,192,128]{2,1,0:T(8,128)} %copy-done.23) | copy-start | bytes 2359300
  187.4 19.2 %copy-start.28 = (f32[8,192,128]{2,1,0:T(8,128)S(1)}, f32[8,192,128]{2,1,0:T(8,128)}, u32[]{:S(2)}) copy-start(f32[8,192,128]{2,1,0:T(8,128)} %copy-done.27) | copy-start | bytes 2359300
  187.4 19.2 %copy-start.30 = (f32[8,192,128]{2,1,0:T(8,128)S(1)}, f32[8,192,128]{2,1,0:T(8,128)}, u32[]{:S(2)}) copy-start(f32[8,192,128]{2,1,0:T(8,128)} %copy-done.29) | copy-start | bytes 2359300
  203.8 21.7 %copy-start.4 = (f32[8,192,128]{2,1,0:T(8,128)S(1)}, f32[8,192,128]{2,1,0:T(8,128)}, u32[]{:S(2)}) copy-start(f32[8,192,128]{2,1,0:T(8,128)} %copy-done.3) | copy-start | bytes 2359300
  203.8 21.7 %copy-start.16 = (f32[8,192,128]{2,1,0:T(8,128)S(1)}, f32[8,192,128]{2,1,0:T(8,128)}, u32[]{:S(2)}) copy-start(f32[8,192,128]{2,1,0:T(8,128)} %copy-done.15) | copy-start | bytes 2359300
  203.8 37.7 %collective-permute-start.25 = (f32[8,192,128]{2,1,0:T(8,128)S(1)}, f32[8,192,128]{2,1,0:T(8,128)S(1)}, u32[]{:S(2)}, u32[]{:S(2)}) collective-permute-start(f32[8,192,128]{2,1,0:T(8,128)S(1)} %copy-done.14), channel_id=1, source_target_pairs={{4,0},{8,12},{5,1},{9,13},{6,2},{10,14},{7,3},{11,15},{20,16},{24,... | collective-permute-start | bytes 2359304 | tf_op jit(solution)/shard_map/ppermute | solution.py:282
  205.3 37.8 %collective-permute-start.27 = (f32[8,192,128]{2,1,0:T(8,128)S(1)}, f32[8,192,128]{2,1,0:T(8,128)S(1)}, u32[]{:S(2)}, u32[]{:S(2)}) collective-permute-start(f32[8,192,128]{2,1,0:T(8,128)S(1)} %copy-done.26), channel_id=1, source_target_pairs={{4,0},{8,12},{5,1},{9,13},{6,2},{10,14},{7,3},{11,15},{20,16},{24,... | collective-permute-start | bytes 2359304 | tf_op jit(solution)/shard_map/ppermute | solution.py:282
  222.7 38.0 %collective-permute-start.29 = (f32[8,192,128]{2,1,0:T(8,128)S(1)}, f32[8,192,128]{2,1,0:T(8,128)S(1)}, u32[]{:S(2)}, u32[]{:S(2)}) collective-permute-start(f32[8,192,128]{2,1,0:T(8,128)S(1)} %collective-permute-done.28.refs_1_), channel_id=1, source_target_pairs={{4,0},{8,12},{5,1},{9,13},{6,2},{10,14},{7,3},{11,15},{20,16},{24,... | collective-permute-start | bytes 2359304 | tf_op jit(solution)/shard_map/ppermute | solution.py:282
  224.0 20.6 %copy-start.8 = (f32[8,192,128]{2,1,0:T(8,128)S(1)}, f32[8,192,128]{2,1,0:T(8,128)}, u32[]{:S(2)}) copy-start(f32[8,192,128]{2,1,0:T(8,128)} %copy-done.7) | copy-start | bytes 2359300
  224.0 42.4 %collective-permute-start.31 = (f32[3,192,128]{2,1,0:T(8,128)S(1)}, f32[3,192,128]{2,1,0:T(8,128)S(1)}, u32[]{:S(2)}, u32[]{:S(2)}) collective-permute-start(f32[3,192,128]{2,1,0:T(8,128)S(1)} %get-tuple-element.26), channel_id=1, source_target_pairs={{4,0},{8,12},{5,1},{9,13},{6,2},{10,14},{7,3},{11,15},{20,16},{24,... | collective-permute-start | bytes 884744 | tf_op jit(solution)/shard_map/ppermute | solution.py:280
  241.5 31.1 %collective-permute-start.32 = (f32[3,192,128]{2,1,0:T(8,128)S(1)}, f32[3,192,128]{2,1,0:T(8,128)S(1)}, u32[]{:S(2)}, u32[]{:S(2)}) collective-permute-start(f32[3,192,128]{2,1,0:T(8,128)S(1)} %get-tuple-element.25), channel_id=1, source_target_pairs={{4,0},{8,12},{5,1},{9,13},{6,2},{10,14},{7,3},{11,15},{20,16},{24,... | collective-permute-start | bytes 884744 | tf_op jit(solution)/shard_map/ppermute | solution.py:280
  243.1 33.4 %collective-permute-start.33 = (f32[2,192,128]{2,1,0:T(8,128)S(1)}, f32[2,192,128]{2,1,0:T(8,128)S(1)}, u32[]{:S(2)}, u32[]{:S(2)}) collective-permute-start(f32[2,192,128]{2,1,0:T(8,128)S(1)} %slice.30), channel_id=1, source_target_pairs={{4,0},{8,12},{5,1},{9,13},{6,2},{10,14},{7,3},{11,15},{20,16},{24,... | collective-permute-start | bytes 589832 | tf_op jit(solution)/shard_map/ppermute | solution.py:280
  (4 other events, 3.6 us)

commit v5 on v3

--- a/solution.py
+++ b/solution.py
@@ -150,7 +150,7 @@
 
 def one_kernel(count, scalars, acc_ref, high_ref, low_ref, *refs):
     slot = refs[:count]
-    out_ref, buffer, sem, left_high, left_low = refs[count:]
+    out_ref, buffer, sem, left = refs[count:]
     row_blocks, width, height = buffer.shape
     cut = acc_ref.shape[1] // pl.num_programs(0)
     step = pl.program_id(0)
@@ -160,14 +160,16 @@
         fetch(slot, scalars[1], (0, 0), buffer, sem).wait()
         for block in range(row_blocks):
             high, low = split(buffer[block].T)
-            left_high[block * height : (block + 1) * height, :] = high
-            left_low[block * height : (block + 1) * height, :] = low
+            left[block * height : (block + 1) * height, :] = high
+            low_row = (row_blocks + block) * height
+            left[low_row : low_row + height, :] = low
 
     pivots = pl.ds(pl.multiple_of(scalars[0] * width, width), width)
     lanes = pl.ds(pl.multiple_of(step * cut, cut), cut)
-    out_ref[:, lanes] = acc_ref[:, lanes] - product(
-        left_high[...], left_low[...], high_ref[pivots, lanes], low_ref[pivots, lanes]
-    )
+    rows = acc_ref.shape[0]
+    both = jnp.dot(left[...], high_ref[pivots, lanes], preferred_element_type=jnp.float32)
+    rest = jnp.dot(left[:rows, :], low_ref[pivots, lanes], preferred_element_type=jnp.float32)
+    out_ref[:, lanes] = acc_ref[:, lanes] - (both[:rows] + (both[rows:] + rest))
 
 
 def one(acc, slot, scalars, right):
@@ -186,8 +188,7 @@
             scratch_shapes=[
                 pltpu.VMEM(slot[0].shape, jnp.float32),
                 pltpu.SemaphoreType.DMA,
-                pltpu.VMEM((rows, width), jnp.bfloat16),
-                pltpu.VMEM((rows, width), jnp.bfloat16),
+                pltpu.VMEM((2 * rows, width), jnp.bfloat16),
             ],
         ),
         input_output_aliases={1: 0},

time: 282 us -> 282 us (level)
  no operation moved by 1% of the time
where the time goes in v5:
time: 282 us; the launch traced here: 281 us
  waiting for transfers between devices  124 us (44%)
  Pallas kernels  84.1 us (30%)
  starting transfers between devices  37.6 us (13%)
  local copies, waits for them, and re-layouts  34.4 us (12%)
    ppermute x19, waiting for transfers between devices, line(): new[odd] = lax.ppermute(what, axis, pairs)  80.5 us
    pallas_call x4, Pallas kernels, add(): pl.pallas_call(functools.partial(add_kernel, [len(slot) for slot in slots...  64.5 us
    ppermute x19, starting transfers between devices, line(): new[odd] = lax.ppermute(what, axis, pairs)  25.6 us
    unnamed x65, local copies, waits for them, and re-layouts  24.7 us
    ppermute x1, waiting for transfers between devices, local(): first = lax.ppermute(whole(parts[m ^ bits[0]])[:half], 'kk', pairs(bits[0]))  21.6 us
    ppermute x3, waiting for transfers between devices, local(): lax.ppermute(groups[i], 'kk', pairs(m))  18.1 us
    pallas_call x3, Pallas kernels, last(): pl.pallas_call(functools.partial(last_kernel, blocks, len(slot), first, f...  11.1 us
    pallas_call x1, Pallas kernels, one(): pl.pallas_call(functools.partial(one_kernel, len(slot)), out_shape=jax.Sh...  5.73 us
  transfers between devices with their start and end apart: 34, of which 13 were waited for; matrix products, arithmetic and copies ran while one was open for 4% of the time, Pallas kernels for 29%

profile of v5, /device:TPU:0, one launch (start us, length us, event | category | flops | bytes accessed | tf_op | source)
XLA Modules:
  0.0 280.7 jit_solution(13218166301687534763)
XLA Ops:
  0.0 2.4 dynamic-slice_bitcast_fusion.2
  2.4 3.1 %collective-permute-start.1 = (f32[8,192,128]{2,1,0:T(8,128)S(1)}, f32[8,192,128]{2,1,0:T(8,128)S(1)}, u32[]{:S(2)}, u32[]{:S(2)}) collective-permute-start(f32[8,192,128]{2,1,0:T(8,128)S(1)} %get-tuple-element.16.refs_2_), channel_id=1, source_target_pairs={{4,0},{0,4},{12,8},{8,12},{5,1},{1,5},{13,9},{9,13},{6,2},{2,6},{1... | collective-permute-start | bytes 2359304 | tf_op jit(solution)/shard_map/ppermute | solution.py:283
  5.5 1.6 collective-permute-start.2
  7.0 1.5 collective-permute-start.8
  8.5 1.6 dynamic-slice_bitcast_fusion
  10.1 1.6 collective-permute-start.19
  12.2 10.8 %collective-permute-done.1.refs_3_ = f32[8,192,128]{2,1,0:T(8,128)S(1)} collective-permute-done((f32[8,192,128]{2,1,0:T(8,128)S(1)}, f32[8,192,128]{2,1,0:T(8,128)S(1)}, u32[]{:S(2)}, u32[]{:S(2)}) %collective-permute-start.1) | collective-permute-done | bytes 786464 | tf_op jit(solution)/shard_map/ppermute | solution.py:283
  23.7 1.3 collective-permute-start.3
  25.0 3.1 %copy.16 = f32[48,8,16,128]{3,1,2,0:T(8,128)} copy(f32[48,8,16,128]{3,2,1,0:T(8,128)S(1)} %bitcast.28) | data formatting | bytes 6291456
  28.2 1.7 collective-permute-start.6
  29.8 15.7 %collective-permute-done.19.refs_4_ = f32[8,192,128]{2,1,0:T(8,128)S(1)} collective-permute-done((f32[8,192,128]{2,1,0:T(8,128)S(1)}, f32[8,192,128]{2,1,0:T(8,128)S(1)}, u32[]{:S(2)}, u32[]{:S(2)}) %collective-permute-start.19) | collective-permute-done | bytes 786464 | tf_op jit(solution)/shard_map/ppermute | solution.py:305
  46.0 2.4 collective-permute-done.22.refs_2_
  48.4 3.3 %collective-permute-start.9 = (f32[8,192,128]{2,1,0:T(8,128)S(1)}, f32[8,192,128]{2,1,0:T(8,128)S(1)}, u32[]{:S(2)}, u32[]{:S(2)}) collective-permute-start(f32[8,192,128]{2,1,0:T(8,128)S(1)} %collective-permute-done.8.refs_2_), channel_id=1, source_target_pairs={{4,0},{0,4},{12,8},{8,12},{5,1},{1,5},{13,9},{9,13},{6,2},{2,6},{1... | collective-permute-start | bytes 2359304 | tf_op jit(solution)/shard_map/ppermute | solution.py:283
  51.7 0.7 collective-permute-start.10
  52.5 0.9 copy-done.5
  53.4 0.9 copy-done.17
  54.3 1.5 collective-permute-start.20
  55.8 14.3 %collective-permute-done.9.refs_3_ = f32[8,192,128]{2,1,0:T(8,128)S(1)} collective-permute-done((f32[8,192,128]{2,1,0:T(8,128)S(1)}, f32[8,192,128]{2,1,0:T(8,128)S(1)}, u32[]{:S(2)}, u32[]{:S(2)}) %collective-permute-start.9) | collective-permute-done | bytes 786464 | tf_op jit(solution)/shard_map/ppermute | solution.py:283
  70.1 2.0 collective-permute-start.23
  72.2 0.7 collective-permute-start.24
  72.9 14.1 %collective-permute-done.20.refs_5_ = f32[8,192,128]{2,1,0:T(8,128)S(1)} collective-permute-done((f32[8,192,128]{2,1,0:T(8,128)S(1)}, f32[8,192,128]{2,1,0:T(8,128)S(1)}, u32[]{:S(2)}, u32[]{:S(2)}) %collective-permute-start.20) | collective-permute-done | bytes 786464 | tf_op jit(solution)/shard_map/ppermute | solution.py:283
  87.7 10.8 %collective-permute-done.23.refs_3_ = f32[8,192,128]{2,1,0:T(8,128)S(1)} collective-permute-done((f32[8,192,128]{2,1,0:T(8,128)S(1)}, f32[8,192,128]{2,1,0:T(8,128)S(1)}, u32[]{:S(2)}, u32[]{:S(2)}) %collective-permute-start.23) | collective-permute-done | bytes 786464 | tf_op jit(solution)/shard_map/ppermute | solution.py:283
  98.5 1.3 collective-permute-start.5
  99.8 0.9 copy-done.15
  100.7 0.7 collective-permute-start.12
  101.4 0.9 copy-done.19
  102.3 18.0 %collective-permute-done.5.refs_6_ = f32[8,192,128]{2,1,0:T(8,128)S(1)} collective-permute-done((f32[8,192,128]{2,1,0:T(8,128)S(1)}, f32[8,192,128]{2,1,0:T(8,128)S(1)}, u32[]{:S(2)}, u32[]{:S(2)}) %collective-permute-start.5) | collective-permute-done | bytes 786464 | tf_op jit(solution)/shard_map/ppermute | solution.py:283
  120.4 0.9 copy-done.29
  121.2 1.3 collective-permute-start.11
  122.5 0.9 copy-done.21
  123.4 0.7 collective-permute-start.26
  124.3 0.7 collective-permute-start.30
  125.0 2.7 slice.27
  127.7 2.8 slice.26
  130.6 11.6 %collective-permute-done.11.refs_4_ = f32[8,192,128]{2,1,0:T(8,128)S(1)} collective-permute-done((f32[8,192,128]{2,1,0:T(8,128)S(1)}, f32[8,192,128]{2,1,0:T(8,128)S(1)}, u32[]{:S(2)}, u32[]{:S(2)}) %collective-permute-start.11) | collective-permute-done | bytes 786464 | tf_op jit(solution)/shard_map/ppermute | solution.py:283
  142.2 0.9 copy-done.27
  143.1 1.5 collective-permute-start.15
  145.5 3.4 %copy-done.2 = f32[8,128,16,128]{3,2,1,0:T(8,128)S(1)} copy-done((f32[8,128,16,128]{3,2,1,0:T(8,128)S(1)}, f32[8,128,16,128]{3,2,1,0:T(8,128)}, u32[]{:S(2)}) %copy-start.2) | copy-done | bytes 8388632
  148.9 2.8 %fold.1.acc_ref = f32[1024,2048]{1,0:T(8,128)S(1)} custom-call(f32[16384,128]{1,0:T(8,128)S(1)} %bitcast.25), custom_call_target="tpu_custom_call" | custom-call | bytes 8388608 | tf_op jit(solution)/shard_map/fold/pallas_call | solution.py:139
  151.7 3.4 %copy-done = f32[1024,2048]{1,0:T(8,128)} copy-done((f32[1024,2048]{1,0:T(8,128)}, f32[1024,2048]{1,0:T(8,128)S(1)}, u32[]{:S(2)}) %copy-start) | copy-done | bytes 8388632
  155.5 1.4 collective-permute-start.13
  156.9 21.6 %collective-permute-done.15.refs_0_ = f32[192,2048]{1,0:T(8,128)} collective-permute-done((f32[192,2048]{1,0:T(8,128)}, f32[192,2048]{1,0:T(8,128)}, u32[]{:S(2)}, u32[]{:S(2)}) %collective-permute-start.15) | collective-permute-done | bytes 1572896 | tf_op jit(solution)/shard_map/ppermute | solution.py:345
  178.5 1.2 collective-permute-done.16.refs_1_
  179.7 3.4 %copy-done.1 = f32[1024,2048]{1,0:T(8,128)S(1)} copy-done((f32[1024,2048]{1,0:T(8,128)S(1)}, f32[1024,2048]{1,0:T(8,128)}, u32[]{:S(2)}) %copy-start.1) | copy-done | bytes 8388632
  183.1 1.1 copy-done.8
  184.3 1.1 copy-done.16
  185.4 1.1 copy-done.18
  186.5 1.1 copy-done.30
  187.7 16.4 %add.77.acc_ref = f32[1024,2048]{1,0:T(8,128)S(1)} custom-call(s32[8]{0:T(128)S(1)} %stack.49.scalars, f32[1024,2048]{1,0:T(8,128)S(1)} %copy-done.1, f32[384,2048]{1,0:T(8,128)} %bitcast.24.refs_0_, f32[384,2048]{1,0:T(8,128)} %collective-permute-done.refs_1_, f32[8,192,128]{2,1,0:T(8,128)S(1)} %get-tuple-element.16.refs_2_, ...), custom_call_target="tpu_custom_call", output_to_operand_aliasing={{}: (1, {})} | custom-call | flops 9663676416 | bytes 6291456 | tf_op jit(solution)/shard_map/add/pallas_call | solution.py:101
  204.1 1.4 collective-permute-start.25
  205.5 1.3 collective-permute-start.27
  206.9 16.1 %add.78.acc_ref = f32[1024,2048]{1,0:T(8,128)S(1)} custom-call(s32[8]{0:T(128)S(1)} %stack.49.scalars, f32[1024,2048]{1,0:T(8,128)S(1)} %add.77.acc_ref, f32[384,2048]{1,0:T(8,128)} %collective-permute-done.6.refs_0_, f32[384,2048]{1,0:T(8,128)} %collective-permute-done.7.refs_1_, f32[8,192,128]{2,1,0:T(8,128)S(1)} %copy-done.6, ...), custom_call_target="tpu_custom_call", output_to_operand_aliasing={{}: (1, {})} | custom-call | flops 9663676416 | bytes 6291456 | tf_op jit(solution)/shard_map/add/pallas_call | solution.py:101
  223.0 1.3 collective-permute-start.29
  224.3 1.4 collective-permute-start.31
  225.8 16.0 %add.79 = (f32[1024,2048]{1,0:T(8,128)S(1)}, bf16[768,2048]{1,0:T(8,128)(2,1)S(1)}, bf16[768,2048]{1,0:T(8,128)(2,1)S(1)}) custom-call(s32[8]{0:T(128)S(1)} %stack.49.scalars, f32[1024,2048]{1,0:T(8,128)S(1)} %add.78.acc_ref, f32[192,2048]{1,0:T(8,128)} %collective-permute-done.15.refs_0_, ...), custom_call_target="tpu_custom_call", output_to_operand_aliasing={{0}: (1, {})} | custom-call | flops 4831838208 | bytes 6291456 | tf_op jit(solution)/shard_map/add/pallas_call | solution.py:101
  241.8 1.3 collective-permute-start.32
  243.1 0.7 collective-permute-done.27.refs_6_
  243.8 1.5 collective-permute-start.33
  245.3 16.1 %add.80.acc_ref = f32[1024,2048]{1,0:T(8,128)S(1)} custom-call(s32[8]{0:T(128)S(1)} %stack.49.scalars, f32[1024,2048]{1,0:T(8,128)S(1)} %get-tuple-element.19.acc_ref, f32[384,2048]{1,0:T(8,128)} %collective-permute-done.14.refs_0_, f32[384,2048]{1,0:T(8,128)} %collective-permute-done.21.refs_1_, ...), custom_call_target="tpu_custom_call", output_to_operand_aliasing={{}: (1, {})} | custom-call | flops 9663676416 | bytes 6291456 | tf_op jit(solution)/shard_map/add/pallas_call | solution.py:101
  261.4 5.7 %one.1.acc_ref = f32[1024,2048]{1,0:T(8,128)S(1)} custom-call(s32[2]{0:T(128)S(1)} %pad_add_fusion.1.scalars, f32[1024,2048]{1,0:T(8,128)S(1)} %add.80.acc_ref, bf16[768,2048]{1,0:T(8,128)(2,1)S(1)} %get-tuple-element.20.high_ref, bf16[768,2048]{1,0:T(8,128)(2,1)S(1)} %get-tuple-element.21.low_ref, ...), custom_call_target="tpu_custom_call", output_to_operand_aliasing={{}: (1, {})} | custom-call | flops 2415919104 | bytes 786432 | tf_op jit(solution)/shard_map/one/pallas_call | solution.py:180
  267.1 3.9 %last.3 = (f32[16384,128]{1,0:T(8,128)}, f32[1024,2048]{1,0:T(8,128)S(1)}) custom-call(s32[2]{0:T(128)S(1)} %pad_add_fusion.scalars, f32[1024,2048]{1,0:T(8,128)S(1)} %one.1.acc_ref, bf16[768,2048]{1,0:T(8,128)(2,1)S(1)} %get-tuple-element.20.high_ref, bf16[768,2048]{1,0:T(8,128)(2,1)S(1)} %get-tuple-element.21.low_ref, ...), custom_call_target="tpu_custom_call", output_to_operand_aliasing={{1}: (1, {})} | custom-call | flops 905969664 | bytes 3145728 | tf_op jit(solution)/shard_map/last/pallas_call | solution.py:236
  271.1 2.2 collective-permute-done.32.refs_0_
  273.3 3.9 %last.4 = (f32[16384,128]{1,0:T(8,128)}, f32[1024,2048]{1,0:T(8,128)S(1)}) custom-call(s32[2]{0:T(128)S(1)} %pad_add_fusion.scalars, f32[1024,2048]{1,0:T(8,128)S(1)} %get-tuple-element.22.acc_ref, bf16[768,2048]{1,0:T(8,128)(2,1)S(1)} %get-tuple-element.20.high_ref, ...), custom_call_target="tpu_custom_call", output_to_operand_aliasing={{1}: (1, {}), {0}: (6, {})} | custom-call | flops 905969664 | bytes 3145728 | tf_op jit(solution)/shard_map/last/pallas_call | solution.py:236
  277.3 3.2 %last.5 = (f32[16384,128]{1,0:T(8,128)}, f32[1024,2048]{1,0:T(8,128)S(1)}) custom-call(s32[2]{0:T(128)S(1)} %pad_add_fusion.scalars, f32[1024,2048]{1,0:T(8,128)S(1)} %get-tuple-element.24.acc_ref, bf16[768,2048]{1,0:T(8,128)(2,1)S(1)} %get-tuple-element.20.high_ref, ...), custom_call_target="tpu_custom_call", output_to_operand_aliasing={{1}: (1, {}), {0}: (6, {})} | custom-call | flops 603979776 | bytes 2097152 | tf_op jit(solution)/shard_map/last/pallas_call | solution.py:236
  (87 shorter events, 4.0 us)
Async XLA Ops:
  2.4 20.6 %collective-permute-start.1 = (f32[8,192,128]{2,1,0:T(8,128)S(1)}, f32[8,192,128]{2,1,0:T(8,128)S(1)}, u32[]{:S(2)}, u32[]{:S(2)}) collective-permute-start(f32[8,192,128]{2,1,0:T(8,128)S(1)} %get-tuple-element.16.refs_2_), channel_id=1, source_target_pairs={{4,0},{0,4},{12,8},{8,12},{5,1},{1,5},{13,9},{9,13},{6,2},{2,6},{1... | collective-permute-start | bytes 2359304 | tf_op jit(solution)/shard_map/ppermute | solution.py:283
  5.5 18.2 %collective-permute-start.2 = (f32[8,192,128]{2,1,0:T(8,128)S(1)}, f32[8,192,128]{2,1,0:T(8,128)}, u32[]{:S(2)}, u32[]{:S(2)}) collective-permute-start(f32[8,192,128]{2,1,0:T(8,128)S(1)} %get-tuple-element.16.refs_2_), channel_id=1, source_target_pairs={{8,4},{4,8},{9,5},{5,9},{10,6},{6,10},{11,7},{7,11},{24,20},{20,24... | collective-permute-start | bytes 2359304 | tf_op jit(solution)/shard_map/ppermute | solution.py:283
  7.0 21.1 %collective-permute-start.8 = (f32[8,192,128]{2,1,0:T(8,128)}, f32[8,192,128]{2,1,0:T(8,128)S(1)}, u32[]{:S(2)}, u32[]{:S(2)}) collective-permute-start(f32[8,192,128]{2,1,0:T(8,128)} %get-tuple-element.17), channel_id=1, source_target_pairs={{0,1},{1,0},{2,3},{3,2},{4,5},{5,4},{6,7},{7,6},{8,9},{9,8},{10,11... | collective-permute-start | bytes 2359304 | tf_op jit(solution)/shard_map/ppermute | solution.py:305
  8.5 16.5 %copy-start.31 = (f32[1,384,16,128]{3,2,1,0:T(8,128)S(1)}, f32[1,384,16,128]{3,2,1,0:T(8,128)}, u32[]{:S(2)}) copy-start(f32[1,384,16,128]{3,2,1,0:T(8,128)} %param.5) | copy-start | bytes 9437188
  10.1 35.3 %collective-permute-start.19 = (f32[8,192,128]{2,1,0:T(8,128)S(1)}, f32[8,192,128]{2,1,0:T(8,128)S(1)}, u32[]{:S(2)}, u32[]{:S(2)}) collective-permute-start(f32[8,192,128]{2,1,0:T(8,128)S(1)} %get-tuple-element.28), channel_id=1, source_target_pairs={{0,3},{1,2},{2,1},{3,0},{4,7},{5,6},{6,5},{7,4},{8,11},{9,10},{10,... | collective-permute-start | bytes 2359304 | tf_op jit(solution)/shard_map/ppermute | solution.py:305
  11.7 36.7 %collective-permute-start.22 = (f32[8,192,128]{2,1,0:T(8,128)S(1)}, f32[8,192,128]{2,1,0:T(8,128)S(1)}, u32[]{:S(2)}, u32[]{:S(2)}) collective-permute-start(f32[8,192,128]{2,1,0:T(8,128)S(1)} %get-tuple-element.27), channel_id=1, source_target_pairs={{0,2},{1,3},{2,0},{3,1},{4,6},{5,7},{6,4},{7,5},{8,10},{9,11},{10,... | collective-permute-start | bytes 2359304 | tf_op jit(solution)/shard_map/ppermute | solution.py:305
  23.0 5.2 %copy-start.7 = (f32[8,192,128]{2,1,0:T(8,128)}, f32[8,192,128]{2,1,0:T(8,128)S(1)}, u32[]{:S(2)}) copy-start(f32[8,192,128]{2,1,0:T(8,128)S(1)} %collective-permute-done.1.refs_3_) | copy-start | bytes 2359300
  23.0 28.8 %collective-permute-start.4 = (f32[8,192,128]{2,1,0:T(8,128)S(1)}, f32[8,192,128]{2,1,0:T(8,128)S(1)}, u32[]{:S(2)}, u32[]{:S(2)}) collective-permute-start(f32[8,192,128]{2,1,0:T(8,128)S(1)} %collective-permute-done.1.refs_3_), channel_id=1, source_target_pairs={{8,4},{4,8},{9,5},{5,9},{10,6},{6,10},{11,7},{7,11},{24,20},{20,24... | collective-permute-start | bytes 2359304 | tf_op jit(solution)/shard_map/ppermute | solution.py:283
  23.7 29.7 %collective-permute-start.3 = (f32[8,192,128]{2,1,0:T(8,128)}, f32[8,192,128]{2,1,0:T(8,128)S(1)}, u32[]{:S(2)}, u32[]{:S(2)}) collective-permute-start(f32[8,192,128]{2,1,0:T(8,128)} %collective-permute-done.2.refs_5_), channel_id=1, source_target_pairs={{4,0},{8,12},{5,1},{9,13},{6,2},{10,14},{7,3},{11,15},{20,16},{24,... | collective-permute-start | bytes 2359304 | tf_op jit(solution)/shard_map/ppermute | solution.py:283
  28.2 96.0 %collective-permute-start.6 = (f32[384,2048]{1,0:T(8,128)}, f32[384,2048]{1,0:T(8,128)}, u32[]{:S(2)}, u32[]{:S(2)}) collective-permute-start(f32[384,2048]{1,0:T(8,128)} %bitcast.24.refs_0_), channel_id=1, source_target_pairs={{0,1},{1,0},{2,3},{3,2},{4,5},{5,4},{6,7},{7,6},{8,9},{9,8},{10,11... | collective-permute-start | bytes 9437192 | tf_op jit(solution)/shard_map/ppermute | solution.py:341
  45.5 85.1 %copy-start.3 = (f32[8,192,128]{2,1,0:T(8,128)}, f32[8,192,128]{2,1,0:T(8,128)S(1)}, u32[]{:S(2)}) copy-start(f32[8,192,128]{2,1,0:T(8,128)S(1)} %collective-permute-done.19.refs_4_) | copy-start | bytes 2359300
  45.5 78.8 %collective-permute-start.14 = (f32[384,2048]{1,0:T(8,128)}, f32[384,2048]{1,0:T(8,128)}, u32[]{:S(2)}, u32[]{:S(2)}) collective-permute-start(f32[384,2048]{1,0:T(8,128)} %bitcast.24.refs_0_), channel_id=1, source_target_pairs={{0,2},{1,3},{2,0},{3,1},{4,6},{5,7},{6,4},{7,5},{8,10},{9,11},{10,... | collective-permute-start | bytes 9437192 | tf_op jit(solution)/shard_map/ppermute | solution.py:341
  48.4 21.7 %collective-permute-start.9 = (f32[8,192,128]{2,1,0:T(8,128)S(1)}, f32[8,192,128]{2,1,0:T(8,128)S(1)}, u32[]{:S(2)}, u32[]{:S(2)}) collective-permute-start(f32[8,192,128]{2,1,0:T(8,128)S(1)} %collective-permute-done.8.refs_2_), channel_id=1, source_target_pairs={{4,0},{0,4},{12,8},{8,12},{5,1},{1,5},{13,9},{9,13},{6,2},{2,6},{1... | collective-permute-start | bytes 2359304 | tf_op jit(solution)/shard_map/ppermute | solution.py:283
  51.7 20.4 %collective-permute-start.10 = (f32[8,192,128]{2,1,0:T(8,128)S(1)}, f32[8,192,128]{2,1,0:T(8,128)S(1)}, u32[]{:S(2)}, u32[]{:S(2)}) collective-permute-start(f32[8,192,128]{2,1,0:T(8,128)S(1)} %collective-permute-done.8.refs_2_), channel_id=1, source_target_pairs={{8,4},{4,8},{9,5},{5,9},{10,6},{6,10},{11,7},{7,11},{24,20},{20,24... | collective-permute-start | bytes 2359304 | tf_op jit(solution)/shard_map/ppermute | solution.py:283
  52.5 0.9 copy-start.5
  53.4 0.9 copy-start.17
  54.3 32.7 %collective-permute-start.20 = (f32[8,192,128]{2,1,0:T(8,128)S(1)}, f32[8,192,128]{2,1,0:T(8,128)S(1)}, u32[]{:S(2)}, u32[]{:S(2)}) collective-permute-start(f32[8,192,128]{2,1,0:T(8,128)S(1)} %collective-permute-done.19.refs_4_), channel_id=1, source_target_pairs={{4,0},{0,4},{12,8},{8,12},{5,1},{1,5},{13,9},{9,13},{6,2},{2,6},{1... | collective-permute-start | bytes 2359304 | tf_op jit(solution)/shard_map/ppermute | solution.py:283
  70.1 28.4 %collective-permute-start.23 = (f32[8,192,128]{2,1,0:T(8,128)S(1)}, f32[8,192,128]{2,1,0:T(8,128)S(1)}, u32[]{:S(2)}, u32[]{:S(2)}) collective-permute-start(f32[8,192,128]{2,1,0:T(8,128)S(1)} %collective-permute-done.22.refs_2_), channel_id=1, source_target_pairs={{4,0},{0,4},{12,8},{8,12},{5,1},{1,5},{13,9},{9,13},{6,2},{2,6},{1... | collective-permute-start | bytes 2359304 | tf_op jit(solution)/shard_map/ppermute | solution.py:283
  72.2 26.4 %collective-permute-start.24 = (f32[8,192,128]{2,1,0:T(8,128)S(1)}, f32[8,192,128]{2,1,0:T(8,128)S(1)}, u32[]{:S(2)}, u32[]{:S(2)}) collective-permute-start(f32[8,192,128]{2,1,0:T(8,128)S(1)} %collective-permute-done.22.refs_2_), channel_id=1, source_target_pairs={{8,4},{4,8},{9,5},{5,9},{10,6},{6,10},{11,7},{7,11},{24,20},{20,24... | collective-permute-start | bytes 2359304 | tf_op jit(solution)/shard_map/ppermute | solution.py:283
  87.0 43.6 %copy-start.13 = (f32[8,192,128]{2,1,0:T(8,128)}, f32[8,192,128]{2,1,0:T(8,128)S(1)}, u32[]{:S(2)}) copy-start(f32[8,192,128]{2,1,0:T(8,128)S(1)} %collective-permute-done.20.refs_5_) | copy-start | bytes 2359300
  87.0 13.7 %collective-permute-start.28 = (f32[8,192,128]{2,1,0:T(8,128)S(1)}, f32[8,192,128]{2,1,0:T(8,128)S(1)}, u32[]{:S(2)}, u32[]{:S(2)}) collective-permute-start(f32[8,192,128]{2,1,0:T(8,128)S(1)} %collective-permute-done.19.refs_4_), channel_id=1, source_target_pairs={{8,4},{4,8},{9,5},{5,9},{10,6},{6,10},{11,7},{7,11},{24,20},{20,24... | collective-permute-start | bytes 2359304 | tf_op jit(solution)/shard_map/ppermute | solution.py:283
  98.5 32.0 %copy-start.9 = (f32[8,192,128]{2,1,0:T(8,128)}, f32[8,192,128]{2,1,0:T(8,128)S(1)}, u32[]{:S(2)}) copy-start(f32[8,192,128]{2,1,0:T(8,128)S(1)} %collective-permute-done.23.refs_3_) | copy-start | bytes 2359300
  98.5 56.9 %collective-permute-start = (f32[384,2048]{1,0:T(8,128)}, f32[384,2048]{1,0:T(8,128)}, u32[]{:S(2)}, u32[]{:S(2)}) collective-permute-start(f32[384,2048]{1,0:T(8,128)} %bitcast.24.refs_0_), channel_id=1, source_target_pairs={{0,16},{16,0},{1,17},{17,1},{2,18},{18,2},{3,19},{19,3},{4,20},{20... | collective-permute-start | bytes 9437192 | tf_op jit(solution)/shard_map/ppermute | solution.py:354
  98.5 32.0 %copy-start.11 = (f32[8,192,128]{2,1,0:T(8,128)}, f32[8,192,128]{2,1,0:T(8,128)S(1)}, u32[]{:S(2)}) copy-start(f32[8,192,128]{2,1,0:T(8,128)S(1)} %collective-permute-done.24.refs_5_) | copy-start | bytes 2359300
  98.5 21.8 %collective-permute-start.5 = (f32[8,192,128]{2,1,0:T(8,128)S(1)}, f32[8,192,128]{2,1,0:T(8,128)S(1)}, u32[]{:S(2)}, u32[]{:S(2)}) collective-permute-start(f32[8,192,128]{2,1,0:T(8,128)S(1)} %collective-permute-done.4.refs_7_), channel_id=1, source_target_pairs={{4,0},{8,12},{5,1},{9,13},{6,2},{10,14},{7,3},{11,15},{20,16},{24,... | collective-permute-start | bytes 2359304 | tf_op jit(solution)/shard_map/ppermute | solution.py:283
  100.7 22.7 %collective-permute-start.12 = (f32[8,192,128]{2,1,0:T(8,128)S(1)}, f32[8,192,128]{2,1,0:T(8,128)S(1)}, u32[]{:S(2)}, u32[]{:S(2)}) collective-permute-start(f32[8,192,128]{2,1,0:T(8,128)S(1)} %collective-permute-done.9.refs_3_), channel_id=1, source_target_pairs={{8,4},{4,8},{9,5},{5,9},{10,6},{6,10},{11,7},{7,11},{24,20},{20,24... | collective-permute-start | bytes 2359304 | tf_op jit(solution)/shard_map/ppermute | solution.py:283
  101.4 0.9 copy-start.19
  121.2 21.0 %collective-permute-start.11 = (f32[8,192,128]{2,1,0:T(8,128)S(1)}, f32[8,192,128]{2,1,0:T(8,128)S(1)}, u32[]{:S(2)}, u32[]{:S(2)}) collective-permute-start(f32[8,192,128]{2,1,0:T(8,128)S(1)} %collective-permute-done.10.refs_5_), channel_id=1, source_target_pairs={{4,0},{8,12},{5,1},{9,13},{6,2},{10,14},{7,3},{11,15},{20,16},{24,... | collective-permute-start | bytes 2359304 | tf_op jit(solution)/shard_map/ppermute | solution.py:283
  122.5 0.9 copy-start.21
  123.4 0.9 copy-start.25
  123.4 21.2 %collective-permute-start.26 = (f32[8,192,128]{2,1,0:T(8,128)S(1)}, f32[8,192,128]{2,1,0:T(8,128)S(1)}, u32[]{:S(2)}, u32[]{:S(2)}) collective-permute-start(f32[8,192,128]{2,1,0:T(8,128)S(1)} %collective-permute-done.23.refs_3_), channel_id=1, source_target_pairs={{8,4},{4,8},{9,5},{5,9},{10,6},{6,10},{11,7},{7,11},{24,20},{20,24... | collective-permute-start | bytes 2359304 | tf_op jit(solution)/shard_map/ppermute | solution.py:283
  124.2 81.4 %collective-permute-start.7 = (f32[384,2048]{1,0:T(8,128)}, f32[384,2048]{1,0:T(8,128)}, u32[]{:S(2)}, u32[]{:S(2)}) collective-permute-start(f32[384,2048]{1,0:T(8,128)} %collective-permute-done.6.refs_0_), channel_id=1, source_target_pairs={{0,16},{16,0},{1,17},{17,1},{2,18},{18,2},{3,19},{19,3},{4,20},{20... | collective-permute-start | bytes 9437192 | tf_op jit(solution)/shard_map/ppermute | solution.py:354
  124.3 20.8 %collective-permute-start.30 = (f32[8,192,128]{2,1,0:T(8,128)S(1)}, f32[8,192,128]{2,1,0:T(8,128)S(1)}, u32[]{:S(2)}, u32[]{:S(2)}) collective-permute-start(f32[8,192,128]{2,1,0:T(8,128)S(1)} %collective-permute-done.20.refs_5_), channel_id=1, source_target_pairs={{8,4},{4,8},{9,5},{5,9},{10,6},{6,10},{11,7},{7,11},{24,20},{20,24... | collective-permute-start | bytes 2359304 | tf_op jit(solution)/shard_map/ppermute | solution.py:283
  142.2 0.9 copy-start.27
  143.1 35.4 %collective-permute-start.15 = (f32[192,2048]{1,0:T(8,128)}, f32[192,2048]{1,0:T(8,128)}, u32[]{:S(2)}, u32[]{:S(2)}) collective-permute-start(f32[192,2048]{1,0:T(8,128)} %slice.26), channel_id=1, source_target_pairs={{0,1},{1,0},{2,3},{3,2},{4,5},{5,4},{6,7},{7,6},{8,9},{9,8},{10,11... | collective-permute-start | bytes 4718600 | tf_op jit(solution)/shard_map/ppermute | solution.py:345
  144.6 0.9 copy-start.23
  144.6 35.1 %collective-permute-start.16 = (f32[192,2048]{1,0:T(8,128)}, f32[192,2048]{1,0:T(8,128)}, u32[]{:S(2)}, u32[]{:S(2)}) collective-permute-start(f32[192,2048]{1,0:T(8,128)} %slice.27), channel_id=1, source_target_pairs={{0,2},{1,3},{2,0},{3,1},{4,6},{5,7},{6,4},{7,5},{8,10},{9,11},{10,... | collective-permute-start | bytes 4718600 | tf_op jit(solution)/shard_map/ppermute | solution.py:346
  145.5 99.7 %collective-permute-start.21 = (f32[384,2048]{1,0:T(8,128)}, f32[384,2048]{1,0:T(8,128)}, u32[]{:S(2)}, u32[]{:S(2)}) collective-permute-start(f32[384,2048]{1,0:T(8,128)} %collective-permute-done.14.refs_0_), channel_id=1, source_target_pairs={{0,16},{16,0},{1,17},{17,1},{2,18},{18,2},{3,19},{19,3},{4,20},{20... | collective-permute-start | bytes 9437192 | tf_op jit(solution)/shard_map/ppermute | solution.py:354
  145.5 3.4 %copy-start.2 = (f32[8,128,16,128]{3,2,1,0:T(8,128)S(1)}, f32[8,128,16,128]{3,2,1,0:T(8,128)}, u32[]{:S(2)}) copy-start(f32[8,128,16,128]{3,2,1,0:T(8,128)} %param.3) | copy-start | bytes 25165828
  151.7 3.4 %copy-start = (f32[1024,2048]{1,0:T(8,128)}, f32[1024,2048]{1,0:T(8,128)S(1)}, u32[]{:S(2)}) copy-start(f32[1024,2048]{1,0:T(8,128)S(1)} %fold.1.acc_ref) | copy-start | bytes 25165828
  155.4 48.7 %copy-start.12 = (f32[8,192,128]{2,1,0:T(8,128)S(1)}, f32[8,192,128]{2,1,0:T(8,128)}, u32[]{:S(2)}) copy-start(f32[8,192,128]{2,1,0:T(8,128)} %copy-done.11) | copy-start | bytes 2359300
  155.4 51.4 %copy-start.6 = (f32[8,192,128]{2,1,0:T(8,128)S(1)}, f32[8,192,128]{2,1,0:T(8,128)}, u32[]{:S(2)}) copy-start(f32[8,192,128]{2,1,0:T(8,128)} %copy-done.5) | copy-start | bytes 2359300
  155.5 48.6 %collective-permute-start.13 = (f32[8,192,128]{2,1,0:T(8,128)}, f32[8,192,128]{2,1,0:T(8,128)S(1)}, u32[]{:S(2)}, u32[]{:S(2)}) collective-permute-start(f32[8,192,128]{2,1,0:T(8,128)} %copy-done.25), channel_id=1, source_target_pairs={{4,0},{8,12},{5,1},{9,13},{6,2},{10,14},{7,3},{11,15},{20,16},{24,... | collective-permute-start | bytes 2359304 | tf_op jit(solution)/shard_map/ppermute | solution.py:283
  178.5 44.5 %collective-permute-start.17 = (f32[192,2048]{1,0:T(8,128)}, f32[192,2048]{1,0:T(8,128)S(1)}, u32[]{:S(2)}, u32[]{:S(2)}) collective-permute-start(f32[192,2048]{1,0:T(8,128)} %collective-permute-done.15.refs_0_), channel_id=1, source_target_pairs={{0,16},{16,0},{1,17},{17,1},{2,18},{18,2},{3,19},{19,3},{4,20},{20... | collective-permute-start | bytes 4718600 | tf_op jit(solution)/shard_map/ppermute | solution.py:354
  179.7 44.5 %collective-permute-start.18 = (f32[192,2048]{1,0:T(8,128)}, f32[192,2048]{1,0:T(8,128)S(1)}, u32[]{:S(2)}, u32[]{:S(2)}) collective-permute-start(f32[192,2048]{1,0:T(8,128)} %collective-permute-done.16.refs_1_), channel_id=1, source_target_pairs={{0,16},{16,0},{1,17},{17,1},{2,18},{18,2},{3,19},{19,3},{4,20},{20... | collective-permute-start | bytes 4718600 | tf_op jit(solution)/shard_map/ppermute | solution.py:354
  179.7 3.4 %copy-start.1 = (f32[1024,2048]{1,0:T(8,128)S(1)}, f32[1024,2048]{1,0:T(8,128)}, u32[]{:S(2)}) copy-start(f32[1024,2048]{1,0:T(8,128)} %copy-done) | copy-start | bytes 25165828
  183.1 1.1 copy-start.8
  184.3 1.1 copy-start.16
  185.4 1.1 copy-start.18
  186.5 1.1 copy-start.30
  187.7 17.9 %copy-start.24 = (f32[8,192,128]{2,1,0:T(8,128)S(1)}, f32[8,192,128]{2,1,0:T(8,128)}, u32[]{:S(2)}) copy-start(f32[8,192,128]{2,1,0:T(8,128)} %copy-done.23) | copy-start | bytes 2359300
  187.7 19.2 %copy-start.20 = (f32[8,192,128]{2,1,0:T(8,128)S(1)}, f32[8,192,128]{2,1,0:T(8,128)}, u32[]{:S(2)}) copy-start(f32[8,192,128]{2,1,0:T(8,128)} %copy-done.19) | copy-start | bytes 2359300
  187.7 19.2 %copy-start.22 = (f32[8,192,128]{2,1,0:T(8,128)S(1)}, f32[8,192,128]{2,1,0:T(8,128)}, u32[]{:S(2)}) copy-start(f32[8,192,128]{2,1,0:T(8,128)} %copy-done.21) | copy-start | bytes 2359300
  187.7 19.2 %copy-start.26 = (f32[8,192,128]{2,1,0:T(8,128)S(1)}, f32[8,192,128]{2,1,0:T(8,128)}, u32[]{:S(2)}) copy-start(f32[8,192,128]{2,1,0:T(8,128)} %copy-done.25) | copy-start | bytes 2359300
  187.7 19.2 %copy-start.28 = (f32[8,192,128]{2,1,0:T(8,128)S(1)}, f32[8,192,128]{2,1,0:T(8,128)}, u32[]{:S(2)}) copy-start(f32[8,192,128]{2,1,0:T(8,128)} %copy-done.27) | copy-start | bytes 2359300
  204.0 21.7 %copy-start.4 = (f32[8,192,128]{2,1,0:T(8,128)S(1)}, f32[8,192,128]{2,1,0:T(8,128)}, u32[]{:S(2)}) copy-start(f32[8,192,128]{2,1,0:T(8,128)} %copy-done.3) | copy-start | bytes 2359300
  204.1 21.7 %copy-start.14 = (f32[8,192,128]{2,1,0:T(8,128)S(1)}, f32[8,192,128]{2,1,0:T(8,128)}, u32[]{:S(2)}) copy-start(f32[8,192,128]{2,1,0:T(8,128)} %copy-done.13) | copy-start | bytes 2359300
  204.1 37.7 %collective-permute-start.25 = (f32[8,192,128]{2,1,0:T(8,128)S(1)}, f32[8,192,128]{2,1,0:T(8,128)S(1)}, u32[]{:S(2)}, u32[]{:S(2)}) collective-permute-start(f32[8,192,128]{2,1,0:T(8,128)S(1)} %copy-done.12), channel_id=1, source_target_pairs={{4,0},{8,12},{5,1},{9,13},{6,2},{10,14},{7,3},{11,15},{20,16},{24,... | collective-permute-start | bytes 2359304 | tf_op jit(solution)/shard_map/ppermute | solution.py:283
  205.5 38.3 %collective-permute-start.27 = (f32[8,192,128]{2,1,0:T(8,128)S(1)}, f32[8,192,128]{2,1,0:T(8,128)S(1)}, u32[]{:S(2)}, u32[]{:S(2)}) collective-permute-start(f32[8,192,128]{2,1,0:T(8,128)S(1)} %copy-done.24), channel_id=1, source_target_pairs={{4,0},{8,12},{5,1},{9,13},{6,2},{10,14},{7,3},{11,15},{20,16},{24,... | collective-permute-start | bytes 2359304 | tf_op jit(solution)/shard_map/ppermute | solution.py:283
  223.0 38.4 %collective-permute-start.29 = (f32[8,192,128]{2,1,0:T(8,128)S(1)}, f32[8,192,128]{2,1,0:T(8,128)S(1)}, u32[]{:S(2)}, u32[]{:S(2)}) collective-permute-start(f32[8,192,128]{2,1,0:T(8,128)S(1)} %collective-permute-done.28.refs_1_), channel_id=1, source_target_pairs={{4,0},{8,12},{5,1},{9,13},{6,2},{10,14},{7,3},{11,15},{20,16},{24,... | collective-permute-start | bytes 2359304 | tf_op jit(solution)/shard_map/ppermute | solution.py:283
  224.3 21.0 %copy-start.10 = (f32[8,192,128]{2,1,0:T(8,128)S(1)}, f32[8,192,128]{2,1,0:T(8,128)}, u32[]{:S(2)}) copy-start(f32[8,192,128]{2,1,0:T(8,128)} %copy-done.9) | copy-start | bytes 2359300
  224.3 42.8 %collective-permute-start.31 = (f32[3,192,128]{2,1,0:T(8,128)S(1)}, f32[3,192,128]{2,1,0:T(8,128)S(1)}, u32[]{:S(2)}, u32[]{:S(2)}) collective-permute-start(f32[3,192,128]{2,1,0:T(8,128)S(1)} %get-tuple-element.32), channel_id=1, source_target_pairs={{4,0},{8,12},{5,1},{9,13},{6,2},{10,14},{7,3},{11,15},{20,16},{24,... | collective-permute-start | bytes 884744 | tf_op jit(solution)/shard_map/ppermute | solution.py:281
  241.8 31.5 %collective-permute-start.32 = (f32[3,192,128]{2,1,0:T(8,128)S(1)}, f32[3,192,128]{2,1,0:T(8,128)S(1)}, u32[]{:S(2)}, u32[]{:S(2)}) collective-permute-start(f32[3,192,128]{2,1,0:T(8,128)S(1)} %get-tuple-element.31), channel_id=1, source_target_pairs={{4,0},{8,12},{5,1},{9,13},{6,2},{10,14},{7,3},{11,15},{20,16},{24,... | collective-permute-start | bytes 884744 | tf_op jit(solution)/shard_map/ppermute | solution.py:281
  243.8 33.5 %collective-permute-start.33 = (f32[2,192,128]{2,1,0:T(8,128)S(1)}, f32[2,192,128]{2,1,0:T(8,128)S(1)}, u32[]{:S(2)}, u32[]{:S(2)}) collective-permute-start(f32[2,192,128]{2,1,0:T(8,128)S(1)} %slice.30), channel_id=1, source_target_pairs={{4,0},{8,12},{5,1},{9,13},{6,2},{10,14},{7,3},{11,15},{20,16},{24,... | collective-permute-start | bytes 589832 | tf_op jit(solution)/shard_map/ppermute | solution.py:281
  (2 other events, 1.8 us)
